TPU v7x, 32 devices: a whole 2x2x4 slice. The times are simulated.
32 devices in a mesh: row: 4 (over y, x), col: 8 (over z, core).
Axes of the slice: x: 2, y: 2, z: 4, core: 2. Of those that a mesh axis runs over, the one named last changes fastest.
Arguments:
- inverse: bfloat16 [26624, 26624], P('row', 'col'), may hold values from -6 to 6
- panels: bfloat16 [2, 8192, 512], P(None, 'col'), may hold values from -0.0625 to 0.0625
- block_slot: int32 [208], replicated, may hold values from 0 to 207, as said below
- list_ids: int32 [2, 64], replicated, may hold values from 0 to 207, as said below
Outputs:
- packed_panels: float32 [2, 16384, 512], P(None, ('row', 'col'))
- diag_update: float32 [2, 512, 512], replicated
Inputs may be any that keep to these rules, and one draw needn't show every extreme that they name: block_slot is a permutation of the slots. `list_ids`: each supernode lists distinct blocks; at most 32 of a supernode's listed blocks have slots in one grid row (slot // 52 equal), and in every supernode some grid row holds exactly 32. `list_ids`: in each aligned group of 8 list positions of a supernode, at most 4 listed blocks have slots in one grid column (slot // 26 equal).
All inputs are finite; a program needn't handle non-finite values.
Results may differ from a plain program's by a relative error of at most 0.0003.
Values may be sent and summed in bfloat16 or wider, within the bound.
No kernel may reach another device: no remote copies, remote signals or barrier semaphores. Data moves between devices by JAX's collectives and lax.ppermute only.
A program may use at most 192 MiB of HBM per device.

v0:
```python
import jax
import jax.numpy as jnp
from jax import lax
from jax.sharding import PartitionSpec as P

BS = 128


def lookup_slots(block_slot, list_ids):
    block_ids = jnp.arange(block_slot.shape[0], dtype=jnp.int32)
    matches = list_ids[..., None] == block_ids
    return jnp.sum(jnp.where(matches, block_slot, 0), axis=-1)


def exact_product(left_rows, right_rows):
    return jnp.dot(left_rows.astype(jnp.float32).T, right_rows, precision=lax.Precision.HIGHEST)


def local(inverse, panels, block_slot, list_ids):
    panel_width = panels.shape[2]
    row_blocks = inverse.shape[0] // BS
    col_blocks = inverse.shape[1] // BS
    listed = list_ids.shape[1]
    grid_rows = lax.axis_size("row")
    grid_cols = lax.axis_size("col")
    max_rows = 2 * listed // grid_rows
    own_rows = max_rows * BS // grid_cols
    my_row = lax.axis_index("row")
    my_col = lax.axis_index("col")
    slots = lookup_slots(block_slot, list_ids)
    grid_row = slots // row_blocks
    local_row = slots % row_blocks
    grid_col = slots // col_blocks
    local_col = slots % col_blocks
    a_blocks = inverse.reshape(row_blocks, BS, col_blocks * BS)
    positions = jnp.arange(listed, dtype=jnp.int32)
    col_ids = jnp.arange(col_blocks, dtype=jnp.int32)
    panel_sums = []
    diag_terms = []
    for supernode in range(panels.shape[0]):
        cols_here = grid_col[supernode]
        in_row = grid_row[supernode] == my_row
        chosen_pos = jnp.argsort(jnp.where(in_row, positions, listed + positions), stable=True)[
            :max_rows
        ]
        is_valid = in_row[chosen_pos]
        picked = a_blocks[local_row[supernode][chosen_pos]]
        picked = jnp.where(is_valid[:, None, None], picked, jnp.zeros((), jnp.bfloat16)).reshape(
            max_rows * BS, col_blocks * BS
        )
        panel_rows = lax.all_gather(panels[supernode], "col", axis=0, tiled=True)
        blocks = panel_rows.reshape(listed, BS, panel_width)
        select = (
            (cols_here == my_col)[None, :] & (local_col[supernode][None, :] == col_ids[:, None])
        ).astype(jnp.bfloat16)
        chosen = jnp.einsum("kp,pbw->kbw", select, blocks, preferred_element_type=jnp.float32)
        chosen = chosen.astype(jnp.bfloat16).reshape(col_blocks * BS, panel_width)
        left_rows = jnp.where(
            is_valid[:, None, None], blocks[chosen_pos], jnp.zeros((), jnp.bfloat16)
        ).reshape(max_rows * BS, panel_width)

        def partial_rows(first_row, row_count, picked=picked, chosen=chosen):
            return jnp.dot(picked, chosen, preferred_element_type=jnp.float32)

        mine_sums = lax.psum_scatter(
            partial_rows(jnp.int32(0), own_rows * lax.axis_size("col")),
            "col",
            scatter_dimension=0,
            tiled=True,
        )
        own_left = lax.dynamic_slice_in_dim(left_rows, my_col * own_rows, own_rows, 0)
        contrib = exact_product(own_left, mine_sums)
        panel_sums.append(mine_sums)
        diag_terms.append(contrib)
    diag_total = lax.psum(jnp.stack(diag_terms), ("row", "col"))
    return (jnp.stack(panel_sums), -diag_total)


def solution(mesh):
    return jax.shard_map(
        local,
        mesh=mesh,
        in_specs=(P("row", "col"), P(None, "col", None), P(), P()),
        out_specs=(P(None, ("row", "col"), None), P()),
        check_vma=False,
    )
```

profile of v0, /device:TPU:0, one launch (start us, length us, event | category | flops | bytes accessed | tf_op | source)
XLA Modules:
  0.0 507.0 jit_solution(3406132472872825563)
XLA Ops:
  7.2 0.0 all-gather.5.cloned.1.call-start
  7.2 3.0 fusion.31
  10.2 0.0 all-gather.5.cloned.1.call-update
  10.2 0.0 all-gather.7.cloned.1.call-start
  10.3 0.7 all-gather.7.cloned.1.call-update
  11.0 0.0 reduce-scatter.3.cloned.1.call-start
  11.0 0.9 select_reduce_fusion
  12.0 2.1 sort.31
  14.1 0.7 gather_fusion.1
  14.8 0.7 gather_fusion
  15.5 2.1 sort.32
  17.6 0.7 gather_fusion.4
  18.4 21.5 %gather_fusion.2 = bf16[32,128,3328]{2,1,0:T(8,128)(2,1)} fusion(bf16[52,128,3328]{2,1,0:T(8,128)(2,1)} %bitcast.57, s32[1024]{0:T(1024)S(1)} %pad_clamp_fusion.2), kind=kCustom, calls=%fused_computation.2 | custom fusion | bytes 54526080 | tf_op jit(solution)/shard_map/gather | solution.py:47
  39.8 19.0 %broadcast_select_fusion.1 = bf16[32,128,3328]{2,1,0:T(8,128)(2,1)} fusion(bf16[32,128,3328]{2,1,0:T(8,128)(2,1)} %gather_fusion.2, pred[32]{0:T(512)(128)(4,1)S(1)} %gather_fusion), kind=kLoop, calls=%fused_computation.9 | loop fusion | flops 13631488 | bytes 54525984 | tf_op jit(solution)/shard_map/jit(_where)/select_n | solution.py:48
  58.9 36.3 %all-gather.5.cloned.1.call-done = bf16[1,8192,512]{2,1,0:T(8,128)(2,1)} async-done(((bf16[1,1024,512]{2,1,0:T(8,128)(2,1)}), bf16[1,8192,512]{2,1,0:T(8,128)(2,1)}) %all-gather.5.cloned.1.call-update) | async-done | bytes 8388624 | tf_op jit(solution)/shard_map/all_gather | solution.py:51
  95.1 13.4 %fusion.4 = bf16[26,128,512]{2,0,1:T(8,128)(2,1)S(1)} fusion(bf16[64,128,512]{2,1,0:T(8,128)(2,1)} %bitcast.61, s32[64]{0:T(128)S(1)} %get-tuple-element.14, pred[64]{0:T(512)(128)(4,1)S(1)} %get-tuple-element.12), kind=kOutput, calls=%fused_computation.14 | convolution fusion | flops 219811072 | bytes 11796800 | tf_op jit(solution)/shard_map/kp,pbw->kbw/dot_general | solution.py:56
  108.6 1.9 copy.11
  110.5 20.2 %fusion.32 = f32[4096,512]{1,0:T(8,128)} fusion(bf16[4096,3328]{1,0:T(8,128)(2,1)} %bitcast.60, bf16[3328,512]{1,0:T(8,128)(2,1)S(1)} %bitcast.69), kind=kOutput, calls=%fused_computation.73 | convolution fusion | flops 13958643712 | bytes 39059456 | tf_op jit(solution)/shard_map/dot_general | solution.py:63
  130.7 0.0 reduce-scatter.3.cloned.1.call-update
  130.7 0.0 reduce-scatter.5.cloned.1.call-start
  130.8 19.0 %gather_fusion.5 = bf16[32,128,3328]{2,1,0:T(8,128)(2,1)} fusion(bf16[52,128,3328]{2,1,0:T(8,128)(2,1)} %bitcast.58, s32[1024]{0:T(1024)S(1)} %pad_clamp_fusion), kind=kCustom, calls=%fused_computation.5 | custom fusion | bytes 54526080 | tf_op jit(solution)/shard_map/gather | solution.py:47
  149.8 0.7 gather_fusion.3
  150.5 19.0 %broadcast_select_fusion = bf16[32,128,3328]{2,1,0:T(8,128)(2,1)} fusion(bf16[32,128,3328]{2,1,0:T(8,128)(2,1)} %gather_fusion.5, pred[32]{0:T(512)(128)(4,1)S(1)} %gather_fusion.3), kind=kLoop, calls=%fused_computation.8 | loop fusion | flops 13631488 | bytes 54525984 | tf_op jit(solution)/shard_map/jit(_where)/select_n | solution.py:48
  169.5 8.4 %all-gather.7.cloned.1.call-done = bf16[1,8192,512]{2,1,0:T(8,128)(2,1)} async-done(((bf16[1,1024,512]{2,1,0:T(8,128)(2,1)}), bf16[1,8192,512]{2,1,0:T(8,128)(2,1)}) %all-gather.7.cloned.1.call-update) | async-done | bytes 8388624 | tf_op jit(solution)/shard_map/all_gather | solution.py:51
  177.9 13.4 %fusion.7 = bf16[26,128,512]{2,0,1:T(8,128)(2,1)S(1)} fusion(bf16[64,128,512]{2,1,0:T(8,128)(2,1)} %bitcast.63, s32[64]{0:T(128)S(1)} %get-tuple-element.15, pred[64]{0:T(512)(128)(4,1)S(1)} %get-tuple-element.13), kind=kOutput, calls=%fused_computation.15 | convolution fusion | flops 219811072 | bytes 11796800 | tf_op jit(solution)/shard_map/kp,pbw->kbw/dot_general | solution.py:56
  191.3 1.9 copy.13
  193.2 20.1 %fusion.33 = f32[4096,512]{1,0:T(8,128)} fusion(bf16[4096,3328]{1,0:T(8,128)(2,1)} %bitcast.59, bf16[3328,512]{1,0:T(8,128)(2,1)S(1)} %bitcast.70), kind=kOutput, calls=%fused_computation.74 | convolution fusion | flops 13958643712 | bytes 39059456 | tf_op jit(solution)/shard_map/dot_general | solution.py:63
  213.3 0.0 reduce-scatter.5.cloned.1.call-update
  213.4 0.0 all-reduce.2.cloned.1.call-start
  213.4 0.1 broadcast_bitcast_fusion.1
  213.5 0.1 dynamic-slice
  213.6 0.1 broadcast_bitcast_fusion
  213.6 0.1 dynamic-slice.1
  213.7 6.2 %gather_fusion.6 = bf16[32,128,512]{2,1,0:T(8,128)(2,1)} fusion(bf16[64,128,512]{2,1,0:T(8,128)(2,1)} %bitcast.62, s32[1024]{0:T(1024)S(1)} %pad_clamp_fusion.3), kind=kCustom, calls=%fused_computation.6 | custom fusion | bytes 8388736 | tf_op jit(solution)/shard_map/gather | solution.py:59
  219.9 6.2 %gather_fusion.7 = bf16[32,128,512]{2,1,0:T(8,128)(2,1)} fusion(bf16[64,128,512]{2,1,0:T(8,128)(2,1)} %bitcast.64, s32[1024]{0:T(1024)S(1)} %pad_clamp_fusion.1), kind=kCustom, calls=%fused_computation.7 | custom fusion | bytes 8388736 | tf_op jit(solution)/shard_map/gather | solution.py:59
  226.1 42.1 %reduce-scatter.3.cloned.1.call-done = f32[512,512]{1,0:T(8,128)} async-done(((f32[4096,512]{1,0:T(8,128)}), f32[512,512]{1,0:T(8,128)}) %reduce-scatter.3.cloned.1.call-update) | async-done | bytes 1048592 | tf_op jit(solution)/shard_map/reduce_scatter | solution.py:65
  268.2 0.0 copy-start
  268.2 2.7 convolution_bitcast_fusion.1
  270.9 87.5 %reduce-scatter.5.cloned.1.call-done = f32[512,512]{1,0:T(8,128)} async-done(((f32[4096,512]{1,0:T(8,128)}), f32[512,512]{1,0:T(8,128)}) %reduce-scatter.5.cloned.1.call-update) | async-done | bytes 1048592 | tf_op jit(solution)/shard_map/reduce_scatter | solution.py:65
  358.4 0.0 copy-start.1
  358.4 2.7 convolution_bitcast_fusion
  361.1 1.5 pad_maximum_fusion.1
  362.6 0.0 all-reduce.2.cloned.1.call-update
  362.6 0.0 copy-done
  362.6 0.0 copy-done.1
  362.6 1.5 pad_maximum_fusion
  364.1 133.1 %all-reduce.2.cloned.1.call-done = f32[2,512,512]{2,1,0:T(8,128)} async-done(((f32[2,512,512]{2,1,0:T(8,128)}), f32[2,512,512]{2,1,0:T(8,128)}) %all-reduce.2.cloned.1.call-update) | async-done | bytes 2097168 | tf_op jit(solution)/shard_map/psum | solution.py:75
  497.2 3.1 neg.3
  (14 shorter events, 0.1 us)
Async XLA Ops:
  7.2 88.0 %all-gather.5.cloned.1.call-start = ((), (), s32[]{:S(2)}) async-start(), calls=%async_computation.5 | async-start | bytes 9437184 | tf_op jit(solution)/shard_map/all_gather | solution.py:51
  10.2 167.6 %all-gather.7.cloned.1.call-start = ((), (), s32[]{:S(2)}) async-start(), calls=%async_computation.6 | async-start | bytes 9437184 | tf_op jit(solution)/shard_map/all_gather | solution.py:51
  11.0 257.2 %reduce-scatter.3.cloned.1.call-start = ((), (), s32[]{:S(2)}) async-start(), calls=%async_computation.2 | async-start | bytes 9437184 | tf_op jit(solution)/shard_map/reduce_scatter | solution.py:65
  130.7 227.7 %reduce-scatter.5.cloned.1.call-start = ((), (), s32[]{:S(2)}) async-start(), calls=%async_computation.3 | async-start | bytes 9437184 | tf_op jit(solution)/shard_map/reduce_scatter | solution.py:65
  213.4 283.8 %all-reduce.2.cloned.1.call-start = ((), (), s32[]{:S(2)}) async-start(), calls=%async_computation.4 | async-start | bytes 4194304 | tf_op jit(solution)/shard_map/psum | solution.py:75
  268.2 94.4 %copy-start = (f32[512,512]{1,0:T(8,128)S(1)}, f32[512,512]{1,0:T(8,128)}, u32[]{:S(2)}) copy-start(f32[512,512]{1,0:T(8,128)} %reduce-scatter.3.cloned.1.call-done) | copy-start | bytes 3145732
  358.4 4.2 copy-start.1
Sparse Core Ops, SparseCore 0:
  10.3 84.7 all-gather.4
  97.3 80.5 all-gather.6
  180.2 88.0 reduce-scatter.2
  270.4 87.9 reduce-scatter.4
  364.1 132.9 all-reduce.1
where the time goes:
time: 517 us; the launch traced here: 507 us
  waiting for transfers between devices  308 us (60%)
  matrix products  72.5 us (14%)
  local copies, waits for them, and re-layouts  62.8 us (12%)
  other arithmetic  49.4 us (10%)
  between operations  14.1 us (3%)
    psum x1, waiting for transfers between devices, local(): diag_total = lax.psum(jnp.stack(diag_terms), ('row', 'col'))  133 us
    reduce_scatter x2, waiting for transfers between devices, local(): lax.psum_scatter(partial_rows(jnp.int32(0), own_rows * lax.axis_size('col...  130 us
    all_gather x2, waiting for transfers between devices, local(): panel_rows = lax.all_gather(panels[supernode], 'col', axis=0, tiled=True)  44.7 us
    gather x4, local copies, waits for them, and re-layouts, local(): picked = a_blocks[local_row[supernode][chosen_pos]]  41.9 us
    dot_general x2, matrix products, partial_rows(): return jnp.dot(picked, chosen, preferred_element_type=jnp.float32)  40.4 us
    select_n x2, other arithmetic, local(): jnp.where(is_valid[:, None, None], picked, jnp.zeros((), jnp.bfloat16))  38 us
    dot_general x2, matrix products, local(): jnp.einsum('kp,pbw->kbw', select, blocks, preferred_element_type=jnp.floa...  26.8 us
    gather x2, local copies, waits for them, and re-layouts, local(): blocks[chosen_pos]  12.4 us
  transfers between devices with their start and end apart: 5, of which 5 were waited for; matrix products, arithmetic and copies ran while one was open for 34% of the time, Pallas kernels for 0%

commit v1 on v0

v1 whole, which is shorter than its diff:
```python
import functools

import jax
import jax.numpy as jnp
from jax import lax
from jax.experimental import pallas as pl
from jax.experimental.pallas import tpu as pltpu
from jax.sharding import PartitionSpec as P

BS = 128
GROUP = 4
TAIL = 16
AXES = ("row", "col")


def swap_bit(bits, parity, bit):
    return 1 << (bit if parity == 0 else bits - 1 - bit)


def row_swap(n_row, n_col, bit):
    bits = n_row.bit_length() - 1
    return [
        ((r ^ swap_bit(bits, c % 2, bit)) * n_col + c, r * n_col + c)
        for r in range(n_row)
        for c in range(n_col)
    ]


def core_swap(n_col):
    return [(c ^ 1, c) for c in range(n_col)]


def line_shift(n_col, shift):
    return [((c + 2 * shift) % n_col, c) for c in range(n_col)]


def pick_table(hit, value, capacity):
    listed = hit.shape[1]
    pos = jnp.arange(listed, dtype=jnp.int32)
    ahead = (pos[:, None] < pos[None, :]) & hit[:, :, None]
    rank = jnp.sum(ahead.astype(jnp.int32), axis=1)
    here = hit[:, None, :] & (rank[:, None, :] == jnp.arange(capacity, dtype=jnp.int32)[None, :, None])
    both = jnp.stack([jnp.broadcast_to(pos, hit.shape), value], axis=1)
    return jnp.sum(jnp.where(here[:, None], both[:, :, None, :], 0), axis=-1)


def encode(rows):
    top = jnp.max(jnp.abs(rows), axis=0, keepdims=True)
    exponent = jnp.ceil(jnp.log2(jnp.maximum(top * (1 + 2.0**-12), 2.0**-100)))
    coded = (rows * jnp.exp2(15.0 - exponent) + 32768.5).astype(jnp.int32) - 32768
    tail = jnp.broadcast_to(exponent, (TAIL, rows.shape[1]))
    return coded.astype(jnp.int16), tail.astype(jnp.int32).astype(jnp.int16)


def decode(coded, tail):
    scale = jnp.exp2(tail[0:1].astype(jnp.int32).astype(jnp.float32) - 15.0)
    return coded.astype(jnp.int32).astype(jnp.float32) * scale


def start_fetch(dims, supernode, my_row, my_col, own, pieces, listed, buf, at, sem):
    n_row, n_col, per_col, _, _, sub = dims
    bits = n_row.bit_length() - 1
    n_line = n_col // 2
    source = lax.div(listed, per_col)
    item = lax.rem(listed, per_col)
    parity = lax.rem(source, 2)
    swapped = parity != lax.rem(my_col, 2)
    shift = lax.rem(lax.div(source, 2) - lax.div(my_col, 2) + n_line, n_line)
    start = pl.multiple_of(at * BS, BS)
    for other in (0, 1):
        mine = swapped if other else jnp.logical_not(swapped)

        @pl.when(mine & (shift == 0))
        def _(other=other):
            pltpu.make_async_copy(own[other].at[supernode * per_col + item], buf.at[pl.ds(start, BS)], sem).start()

        @pl.when(mine & (shift != 0))
        def _(other=other):
            for e in range(n_row):
                masks = [sum(swap_bit(bits, p, b) for b in range(bits) if e >> b & 1) for p in (0, 1)]
                mask = jnp.where(parity == 0, masks[0], masks[1])
                place = pl.multiple_of(start + (my_row ^ mask) * sub, sub)
                pltpu.make_async_copy(
                    pieces[other][e].at[(shift - 1) * per_col + item], buf.at[pl.ds(place, sub)], sem
                ).start()


def wait_fetch(buf, at, sem):
    part = buf.at[pl.ds(pl.multiple_of(at * BS, BS), BS)]
    pltpu.make_async_copy(part, part, sem).wait()


def clear_block(buf, at):
    buf[pl.ds(pl.multiple_of(at * BS, BS), BS), :] = jnp.zeros((BS, buf.shape[1]), buf.dtype)


def slot_of(dims, my_col, parity, at):
    _, n_col, _, max_rows, _, _ = dims
    in_chunk = max_rows // n_col
    n_line = n_col // 2
    chunk = 2 * lax.rem(lax.div(my_col, 2) + lax.div(at, in_chunk), n_line) + parity
    return chunk * in_chunk + lax.rem(at, in_chunk)


def pack_kernel(tab, strip, out):
    out[...] = strip[...]


def pack_strips(tab, inverse, dims):
    _, _, _, max_rows, max_cols, _ = dims
    base = 2 * max_rows + 2 * max_cols
    count = max_rows // 2
    block = (BS, inverse.shape[1])

    def strip(at, tab):
        my_col = tab[base + 3]
        return tab[max_rows + slot_of(dims, my_col, 1 - lax.rem(my_col, 2), at)], 0

    return pl.pallas_call(
        pack_kernel,
        out_shape=jax.ShapeDtypeStruct((count * BS, inverse.shape[1]), inverse.dtype),
        grid_spec=pltpu.PrefetchScalarGridSpec(
            num_scalar_prefetch=1,
            grid=(count,),
            in_specs=[pl.BlockSpec(block, strip)],
            out_specs=pl.BlockSpec(block, lambda at, tab: (at, 0)),
        ),
        cost_estimate=pl.CostEstimate(flops=0, bytes_accessed=27 * 10**6, transcendentals=0),
        name="pack_strips",
    )(tab, inverse)


def product_kernel(dims, supernode, tab, inverse, packed, *refs):
    n_row, n_col, _, max_rows, max_cols, _ = dims
    n_line = n_col // 2
    in_chunk = max_rows // n_col
    own = refs[0:2]
    pieces = (refs[2 : 2 + n_row], refs[2 + n_row : 2 + 2 * n_row])
    first_ref, diag, *outs = refs[2 + 2 * n_row : -7]
    total, cols_buf, rows_buf, strips, cols_sem, rows_sem, strip_sem = refs[-7:]
    step = pl.program_id(0)
    chunk_rows = in_chunk * BS
    group_rows = GROUP * BS
    half_cols = inverse.shape[1]
    base = 2 * max_rows + 2 * max_cols
    n_rows, n_cols, my_row, my_col = tab[base], tab[base + 1], tab[base + 2], tab[base + 3]
    my_parity = lax.rem(my_col, 2)
    slots = strips.shape[0]

    def strip_copies(at, item, slot):
        block = tab[max_rows + slot_of(dims, my_col, my_parity, at * in_chunk + item)]
        rows = pl.ds(item * BS, BS)
        sem = strip_sem.at[slot, item]
        return (
            pltpu.make_async_copy(
                inverse.at[pl.ds(pl.multiple_of(block * BS, BS), BS)], strips.at[slot, rows, pl.ds(0, half_cols)], sem.at[0]
            ),
            pltpu.make_async_copy(
                packed.at[pl.ds(pl.multiple_of((at * in_chunk + item) * BS, BS), BS)],
                strips.at[slot, rows, pl.ds(half_cols, half_cols)],
                sem.at[1],
            ),
        )

    def left_of(at):
        return n_rows - slot_of(dims, my_col, my_parity, at * in_chunk)

    def start_strips(at, slot):
        @pl.when(left_of(at) > 0)
        def _():
            for item in range(in_chunk):
                for copy in strip_copies(at, item, slot):
                    copy.start()

    slot = lax.rem(step, slots)

    @pl.when(step == 0)
    def _():
        start_strips(0, 0)

        @pl.loop(0, n_cols)
        def _(j):
            listed = tab[2 * max_rows + j]
            start_fetch(dims, supernode, my_row, my_col, own, pieces, listed, cols_buf, j, cols_sem.at[j])

        for ahead in range(1, slots - 1):
            start_strips(ahead, ahead)

        @pl.loop(0, n_line * in_chunk)
        def _(at):
            k = slot_of(dims, my_col, my_parity, at)

            @pl.when(k < n_rows)
            def _():
                start_fetch(dims, supernode, my_row, my_col, own, pieces, tab[k], rows_buf, at, rows_sem.at[at])

            @pl.when(k >= n_rows)
            def _():
                clear_block(rows_buf, at)

        @pl.loop(n_cols, lax.div(n_cols + GROUP - 1, GROUP) * GROUP)
        def _(j):
            clear_block(cols_buf, j)

        diag[...] = jnp.zeros_like(diag)

        @pl.loop(0, n_cols)
        def _(j):
            wait_fetch(cols_buf, j, cols_sem.at[j])

    @pl.when(step + slots - 1 < n_line)
    def _():
        start_strips(step + slots - 1, lax.rem(step + slots - 1, slots))

    left = left_of(step)

    @pl.when((left <= 0) | (n_cols == 0))
    def _():
        total[...] = jnp.zeros_like(total)

    @pl.when(left > 0)
    def _():
        for item in range(in_chunk):
            for copy in strip_copies(step, item, slot):
                copy.wait()

        def term(k):
            parts = []
            for item in range(GROUP):
                col = tab[2 * max_rows + max_cols + k * GROUP + item]
                parts.append(strips[slot, :, pl.ds(pl.multiple_of(col * BS, BS), BS)])
            right = cols_buf[pl.ds(pl.multiple_of(k * group_rows, group_rows), group_rows), :]
            return jnp.dot(jnp.concatenate(parts, axis=1), right, preferred_element_type=jnp.float32)

        @pl.when(n_cols > 0)
        def _():
            total[...] = term(0)

        @pl.loop(1, lax.div(n_cols + GROUP - 1, GROUP))
        def _(k):
            total[...] += term(k)

        for item in range(in_chunk):

            @pl.when(item >= left)
            def _(item=item):
                total[pl.ds(item * BS, BS), :] = jnp.zeros((BS, total.shape[1]), total.dtype)

            @pl.when(item < left)
            def _(item=item):
                wait_fetch(rows_buf, step * in_chunk + item, rows_sem.at[step * in_chunk + item])

        sums = total[...]
        high = sums.astype(jnp.bfloat16)
        low = (sums - high.astype(jnp.float32)).astype(jnp.bfloat16)
        rows = rows_buf[pl.ds(pl.multiple_of(step * chunk_rows, chunk_rows), chunk_rows), :].T
        rows = jnp.concatenate([rows, rows], axis=1)
        both = jnp.concatenate([high, low], axis=0)
        diag[...] -= jnp.dot(rows, both, preferred_element_type=jnp.float32)

    @pl.when(step == 0)
    def _():
        first_ref[...] = total[...]

    for shift, out in enumerate(outs, 1):

        @pl.when(step == shift)
        def _(out=out):
            body, tail = encode(total[...])
            out[0:chunk_rows, :] = body
            out[chunk_rows:, :] = tail


def products(tab, inverse, packed, own, pieces, dims, supernode):
    _, n_col, _, max_rows, max_cols, _ = dims
    n_line = n_col // 2
    width = own[0].shape[-1]
    in_chunk = max_rows // n_col
    chunk_rows = in_chunk * BS
    coded_shape = (chunk_rows + TAIL, width)
    any_spec = pl.BlockSpec(memory_space=pl.ANY)
    whole = lambda shape: pl.BlockSpec(shape, lambda g, tab: (0, 0))
    operands = [inverse, packed, *own, *pieces[0], *pieces[1]]
    return pl.pallas_call(
        functools.partial(product_kernel, dims, supernode),
        out_shape=(
            jax.ShapeDtypeStruct((chunk_rows, width), jnp.float32),
            jax.ShapeDtypeStruct((width, width), jnp.float32),
        )
        + (jax.ShapeDtypeStruct(coded_shape, jnp.int16),) * (n_line - 1),
        grid_spec=pltpu.PrefetchScalarGridSpec(
            num_scalar_prefetch=1,
            grid=(n_line,),
            in_specs=[any_spec] * len(operands),
            out_specs=[whole((chunk_rows, width)), whole((width, width))] + [whole(coded_shape)] * (n_line - 1),
            scratch_shapes=[
                pltpu.VMEM((chunk_rows, width), jnp.float32),
                pltpu.VMEM((max_cols * BS, width), jnp.bfloat16),
                pltpu.VMEM((n_line * chunk_rows, width), jnp.bfloat16),
                pltpu.VMEM((3, chunk_rows, 2 * inverse.shape[1]), jnp.bfloat16),
                pltpu.SemaphoreType.DMA((max_cols,)),
                pltpu.SemaphoreType.DMA((n_line * in_chunk,)),
                pltpu.SemaphoreType.DMA((3, in_chunk, 2)),
            ],
        ),
        cost_estimate=pl.CostEstimate(flops=10**10, bytes_accessed=3 * 10**7, transcendentals=0),
        name="products",
    )(tab, *operands)


def final_kernel(count, first, *refs):
    out = refs[-1]
    total = first[...]
    for part in range(count):
        total = total + decode(refs[part][...], refs[count + part][...])
    out[0] = total


def final_sums(supernodes, supernode, first, coded, earlier):
    chunk_rows, width = first.shape
    rows = chunk_rows // 2
    tile = lambda: pl.BlockSpec((rows, width), lambda g: (g, 0))
    tail = lambda: pl.BlockSpec((TAIL, width), lambda g: (chunk_rows // TAIL, 0))
    operands = [first, *coded, *coded]
    specs = [tile()] + [tile()] * len(coded) + [tail()] * len(coded)
    aliases = {}
    if earlier is not None:
        aliases = {len(operands): 0}
        operands.append(earlier)
        specs.append(pl.BlockSpec(memory_space=pl.ANY))
    return pl.pallas_call(
        functools.partial(final_kernel, len(coded)),
        out_shape=jax.ShapeDtypeStruct((supernodes, chunk_rows, width), jnp.float32),
        grid=(2,),
        in_specs=specs,
        out_specs=pl.BlockSpec((1, rows, width), lambda g: (supernode, g, 0)),
        input_output_aliases=aliases,
        cost_estimate=pl.CostEstimate(flops=10**7, bytes_accessed=4 * 10**6, transcendentals=0),
        name="final_sums",
    )(*operands)


def half(array, index):
    rows = array.shape[0] // 2
    return lax.dynamic_slice_in_dim(array, index * rows, rows, 0)


def row_bit(bits, step, my_row, my_parity):
    place = jnp.where(my_parity == 0, step, bits - 1 - step)
    return (my_row >> place) & 1


def sum_over_all(part, n_row, n_col, my_row, my_parity):
    bits = n_row.bit_length() - 1
    n_line = n_col // 2
    part = half(part, my_parity) + lax.ppermute(half(part, 1 - my_parity), "col", core_swap(n_col))
    for step in range(bits):
        bit = row_bit(bits, step, my_row, my_parity)
        part = half(part, bit) + lax.ppermute(half(part, 1 - bit), AXES, row_swap(n_row, n_col, step))
    got = [lax.ppermute(part, "col", line_shift(n_col, shift)) for shift in range(1, n_line)]
    whole = sum(got, part)
    for step in reversed(range(bits)):
        other = lax.ppermute(whole, AXES, row_swap(n_row, n_col, step))
        bit = row_bit(bits, step, my_row, my_parity)
        whole = jnp.where(bit == 0, jnp.concatenate([whole, other]), jnp.concatenate([other, whole]))
    return whole, lax.ppermute(whole, "col", core_swap(n_col))


def local(inverse, panels, block_slot, list_ids):
    supernodes, _, width = panels.shape
    row_blocks = inverse.shape[0] // BS
    col_blocks = inverse.shape[1] // BS
    listed = list_ids.shape[1]
    n_row = lax.axis_size("row")
    n_col = lax.axis_size("col")
    n_line = n_col // 2
    per_col = listed // n_col
    max_rows = 2 * listed // n_row
    max_cols = max_rows if n_col == 2 * n_row else -(-2 * col_blocks // GROUP) * GROUP
    sub = BS // n_row
    my_row = lax.axis_index("row")
    my_col = lax.axis_index("col")

    block_ids = jnp.arange(block_slot.shape[0], dtype=jnp.int32)
    slots = jnp.sum(jnp.where(list_ids[..., None] == block_ids, block_slot, 0), axis=-1)
    in_row = slots // row_blocks == my_row
    in_col = slots // (2 * col_blocks) == my_col // 2
    place = (slots // col_blocks != my_col).astype(jnp.int32) * col_blocks + slots % col_blocks
    row_table = pick_table(in_row, slots % row_blocks, max_rows)
    col_table = pick_table(in_col, place, max_cols)
    scalars = jnp.stack(
        [
            jnp.sum(in_row.astype(jnp.int32), axis=1),
            jnp.sum(in_col.astype(jnp.int32), axis=1),
            jnp.full((supernodes,), my_row, jnp.int32),
            jnp.full((supernodes,), my_col, jnp.int32),
        ],
        axis=1,
    )
    tables = jnp.concatenate(
        [row_table.reshape(supernodes, -1), col_table.reshape(supernodes, -1), scalars], axis=1
    )

    blocks = panels.reshape(supernodes * per_col, BS, width)
    own = (blocks, lax.ppermute(blocks, "col", core_swap(n_col)))
    dims = (n_row, n_col, per_col, max_rows, max_cols, sub)
    held = []
    for s in range(supernodes):
        mine = lax.dynamic_slice(
            blocks, (s * per_col, my_row * sub, 0), (per_col, sub, width)
        )
        line = jnp.concatenate(
            [lax.ppermute(mine, "col", line_shift(n_col, shift)) for shift in range(1, n_line)], axis=0
        )
        pieces = [line]
        for e in range(1, n_row):
            bit = e.bit_length() - 1
            pieces.append(lax.ppermute(pieces[e ^ (1 << bit)], AXES, row_swap(n_row, n_col, bit)))
        other = [lax.ppermute(piece, "col", core_swap(n_col)) for piece in pieces]
        held.append((pieces, other))
    out = None
    halves = []
    for s in range(supernodes):
        packed = pack_strips(tables[s], inverse, dims)
        packed = lax.ppermute(packed, "col", core_swap(n_col))
        first, diag, *coded = products(tables[s], inverse, packed, own, held[s], dims, s)
        coded = [lax.ppermute(part, "col", line_shift(n_col, n_line - shift)) for shift, part in enumerate(coded, 1)]
        halves.append(sum_over_all(diag, n_row, n_col, my_row, my_col % 2))
        out = final_sums(supernodes, s, first, coded, out)
    even = jnp.concatenate([part for mine, other in halves for part in (mine, other)])
    odd = jnp.concatenate([part for mine, other in halves for part in (other, mine)])
    return out, jnp.where(my_col % 2 == 0, even, odd).reshape(supernodes, width, width)


def solution(mesh):
    return jax.shard_map(
        local,
        mesh=mesh,
        in_specs=(P("row", "col"), P(None, "col", None), P(), P()),
        out_specs=(P(None, ("row", "col"), None), P()),
        check_vma=False,
    )
```

time: 517 us -> 331 us (0.64)
  the two profiles are of different devices: /device:TPU:0 before, /device:TPU:25 now
where the time goes in v1:
time: 331 us; the launch traced here: 330 us
  waiting for transfers between devices  147 us (44%)
  starting transfers between devices  90.3 us (27%)
  Pallas kernels  72.8 us (22%)
  other arithmetic  9.7 us (3%)
  local copies, waits for them, and re-layouts  8.48 us (3%)
    ppermute x6, waiting for transfers between devices, local(): lax.ppermute(part, 'col', line_shift(n_col, n_line - shift))  64.8 us
    ppermute x6, starting transfers between devices, local(): lax.ppermute(part, 'col', line_shift(n_col, n_line - shift))  34.6 us
    pallas_call x2, Pallas kernels, products(): pl.pallas_call(functools.partial(product_kernel, dims, supernode), out_sh...  34.3 us
    pallas_call x2, Pallas kernels, pack_strips(): pl.pallas_call(pack_kernel, out_shape=jax.ShapeDtypeStruct((count * BS, i...  33.1 us
    ppermute x6, waiting for transfers between devices, local(): lax.ppermute(pieces[e ^ 1 << bit], AXES, row_swap(n_row, n_col, bit))  27.1 us
    ppermute x6, waiting for transfers between devices, local(): lax.ppermute(mine, 'col', line_shift(n_col, shift))  24.3 us
    ppermute x8, starting transfers between devices, local(): other = [lax.ppermute(piece, 'col', core_swap(n_col)) for piece in pieces]  21.7 us
    ppermute x6, waiting for transfers between devices, sum_over_all(): lax.ppermute(part, 'col', line_shift(n_col, shift))  17.2 us
  transfers between devices with their start and end apart: 47, of which 20 were waited for; matrix products, arithmetic and copies ran while one was open for 2% of the time, Pallas kernels for 17%

profile of v1, /device:TPU:25, one launch (start us, length us, event | category | flops | bytes accessed | tf_op | source)
XLA Modules:
  0.0 329.6 jit_solution(17087576637234273184)
XLA Ops:
  0.7 0.9 select_reduce_fusion
  2.8 0.6 fusion.4
  3.3 16.5 %pack_strips.2 = bf16[2048,3328]{1,0:T(8,128)(2,1)} custom-call(s32[132]{0:T(256)} %bitcast.25, bf16[6656,3328]{1,0:T(8,128)(2,1)} %inverse.3), custom_call_target="tpu_custom_call" | custom-call | bytes 27000000 | tf_op jit(solution)/shard_map/pack_strips/pallas_call | solution.py:119
  19.8 0.7 collective-permute-start
  20.5 16.6 %pack_strips.3 = bf16[2048,3328]{1,0:T(8,128)(2,1)} custom-call(s32[132]{0:T(256)} %bitcast.23, bf16[6656,3328]{1,0:T(8,128)(2,1)} %inverse.3), custom_call_target="tpu_custom_call" | custom-call | bytes 27000000 | tf_op jit(solution)/shard_map/pack_strips/pallas_call | solution.py:119
  37.2 0.2 collective-permute-start.2
  37.4 3.1 collective-permute-start.4
  40.5 6.0 %collective-permute-done.2 = bf16[8,32,512]{2,1,0:T(8,128)(2,1)S(1)} collective-permute-done((bf16[8,32,512]{2,1,0:T(8,128)(2,1)S(1)}, bf16[8,32,512]{2,1,0:T(8,128)(2,1)S(1)}, u32[]{:S(2)}, u32[]{:S(2)}) %collective-permute-start.2) | collective-permute-done | bytes 262176 | tf_op jit(solution)/shard_map/ppermute | solution.py:413
  46.5 10.6 %collective-permute-done.3 = bf16[8,32,512]{2,1,0:T(8,128)(2,1)S(1)} collective-permute-done((bf16[8,32,512]{2,1,0:T(8,128)(2,1)S(1)}, bf16[8,32,512]{2,1,0:T(8,128)(2,1)S(1)}, u32[]{:S(2)}, u32[]{:S(2)}) %collective-permute-start.3) | collective-permute-done | bytes 262176 | tf_op jit(solution)/shard_map/ppermute | solution.py:413
  57.2 10.5 %collective-permute-start.17 = (bf16[8,32,512]{2,1,0:T(8,128)(2,1)S(1)}, bf16[8,32,512]{2,1,0:T(8,128)(2,1)S(1)}, u32[]{:S(2)}, u32[]{:S(2)}) collective-permute-start(bf16[8,32,512]{2,1,0:T(8,128)(2,1)S(1)} %get-tuple-element.29), channel_id=1, source_target_pairs={{4,0},{5,1},{6,2},{7,3},{0,4},{1,5},{2,6},{3,7},{12,8},{13,9},{14,... | collective-permute-start | bytes 786440 | tf_op jit(solution)/shard_map/ppermute | solution.py:413
  67.8 3.1 collective-permute-start.18
  70.9 7.6 %collective-permute-done.17 = bf16[8,32,512]{2,1,0:T(8,128)(2,1)S(1)} collective-permute-done((bf16[8,32,512]{2,1,0:T(8,128)(2,1)S(1)}, bf16[8,32,512]{2,1,0:T(8,128)(2,1)S(1)}, u32[]{:S(2)}, u32[]{:S(2)}) %collective-permute-start.17) | collective-permute-done | bytes 262176 | tf_op jit(solution)/shard_map/ppermute | solution.py:413
  78.6 3.6 %collective-permute-start.8 = (bf16[24,32,512]{2,1,0:T(8,128)(2,1)S(1)}, bf16[24,32,512]{2,1,0:T(8,128)(2,1)S(1)}, u32[]{:S(2)}, u32[]{:S(2)}) collective-permute-start(bf16[24,32,512]{2,1,0:T(8,128)(2,1)S(1)} %constant_dynamic-update-slice_fusion.refs_2_), channel_id=1, source_target_pairs={{1,0},{0,1},{3,2},{2,3},{5,4},{4,5},{7,6},{6,7},{9,8},{8,9},{11,10... | collective-permute-start | bytes 2359304 | tf_op jit(solution)/shard_map/ppermute | solution.py:419
  82.3 1.8 collective-permute-start.19
  84.1 9.6 %collective-permute-done.6.refs_4_ = bf16[24,32,512]{2,1,0:T(8,128)(2,1)S(1)} collective-permute-done((bf16[24,32,512]{2,1,0:T(8,128)(2,1)S(1)}, bf16[24,32,512]{2,1,0:T(8,128)(2,1)S(1)}, u32[]{:S(2)}, u32[]{:S(2)}) %collective-permute-start.6) | collective-permute-done | bytes 786464 | tf_op jit(solution)/shard_map/ppermute | solution.py:418
  93.7 0.3 collective-permute-start.20
  94.0 1.2 collective-permute-start.7
  95.2 7.0 %collective-permute-done.19.refs_3_ = bf16[24,32,512]{2,1,0:T(8,128)(2,1)} collective-permute-done((bf16[24,32,512]{2,1,0:T(8,128)(2,1)S(1)}, bf16[24,32,512]{2,1,0:T(8,128)(2,1)}, u32[]{:S(2)}, u32[]{:S(2)}) %collective-permute-start.19) | collective-permute-done | bytes 786464 | tf_op jit(solution)/shard_map/ppermute | solution.py:418
  102.2 2.4 collective-permute-start.1
  104.6 1.8 collective-permute-done.20.refs_4_
  106.4 8.2 %collective-permute-start.9 = (bf16[24,32,512]{2,1,0:T(8,128)(2,1)S(1)}, bf16[24,32,512]{2,1,0:T(8,128)(2,1)S(1)}, u32[]{:S(2)}, u32[]{:S(2)}) collective-permute-start(bf16[24,32,512]{2,1,0:T(8,128)(2,1)S(1)} %collective-permute-done.5.refs_3_), channel_id=1, source_target_pairs={{1,0},{0,1},{3,2},{2,3},{5,4},{4,5},{7,6},{6,7},{9,8},{8,9},{11,10... | collective-permute-start | bytes 2359304 | tf_op jit(solution)/shard_map/ppermute | solution.py:419
  114.6 0.4 collective-permute-done.7.refs_5_
  115.0 8.2 %collective-permute-start.10 = (bf16[24,32,512]{2,1,0:T(8,128)(2,1)S(1)}, bf16[24,32,512]{2,1,0:T(8,128)(2,1)S(1)}, u32[]{:S(2)}, u32[]{:S(2)}) collective-permute-start(bf16[24,32,512]{2,1,0:T(8,128)(2,1)S(1)} %collective-permute-done.6.refs_4_), channel_id=1, source_target_pairs={{1,0},{0,1},{3,2},{2,3},{5,4},{4,5},{7,6},{6,7},{9,8},{8,9},{11,10... | collective-permute-start | bytes 2359304 | tf_op jit(solution)/shard_map/ppermute | solution.py:419
  123.2 1.8 collective-permute-done.10.refs_8_
  125.0 0.9 copy-done.16
  125.9 0.4 collective-permute-start.11
  126.3 8.3 %collective-permute-done.21.refs_5_ = bf16[24,32,512]{2,1,0:T(8,128)(2,1)} collective-permute-done((bf16[24,32,512]{2,1,0:T(8,128)(2,1)}, bf16[24,32,512]{2,1,0:T(8,128)(2,1)}, u32[]{:S(2)}, u32[]{:S(2)}) %collective-permute-start.21) | collective-permute-done | bytes 786464 | tf_op jit(solution)/shard_map/ppermute | solution.py:418
  134.6 0.9 collective-permute-start.22
  135.5 0.5 collective-permute-start.24
  136.1 17.1 %products.2 = (f32[512,512]{1,0:T(8,128)}, f32[512,512]{1,0:T(8,128)}, s16[528,512]{1,0:T(8,128)(2,1)}, s16[528,512]{1,0:T(8,128)(2,1)}, s16[528,512]{1,0:T(8,128)(2,1)}) custom-call(s32[132]{0:T(256)} %bitcast.26, bf16[6656,3328]{1,0:T(8,128)(2,1)} %inverse.3, bf16[2048,3328]{1,0:T(8,128)(2,1)} %collective-permute-done.packed, ...), custom_call_target="tpu_custom_call" | custom-call | flops 10000000000 | bytes 30000000 | tf_op jit(solution)/shard_map/products/pallas_call | solution.py:284
  153.2 1.9 constant_dynamic-slice_fusion.2
  155.1 0.4 collective-permute-start.38
  155.6 17.1 %products.3 = (f32[512,512]{1,0:T(8,128)}, f32[512,512]{1,0:T(8,128)}, s16[528,512]{1,0:T(8,128)(2,1)}, s16[528,512]{1,0:T(8,128)(2,1)}, s16[528,512]{1,0:T(8,128)(2,1)}) custom-call(s32[132]{0:T(256)} %bitcast.24, bf16[6656,3328]{1,0:T(8,128)(2,1)} %inverse.3, bf16[2048,3328]{1,0:T(8,128)(2,1)} %collective-permute-done.15.packed, ...), custom_call_target="tpu_custom_call" | custom-call | flops 10000000000 | bytes 30000000 | tf_op jit(solution)/shard_map/products/pallas_call | solution.py:284
  172.7 2.0 constant_dynamic-slice_fusion.5
  174.7 0.2 collective-permute-start.29
  174.9 26.7 %collective-permute-start.26 = (s16[528,512]{1,0:T(8,128)(2,1)}, s16[528,512]{1,0:T(8,128)(2,1)S(1)}, u32[]{:S(2)}, u32[]{:S(2)}) collective-permute-start(s16[528,512]{1,0:T(8,128)(2,1)} %get-tuple-element.17), channel_id=1, source_target_pairs={{6,0},{7,1},{0,2},{1,3},{2,4},{3,5},{4,6},{5,7},{14,8},{15,9},{8,1... | collective-permute-start | bytes 1622024 | tf_op jit(solution)/shard_map/ppermute | solution.py:427
  201.9 1.1 dynamic-slice_add_fusion.1
  203.0 1.5 collective-permute-start.30
  204.5 2.8 collective-permute-done.39
  207.5 2.7 collective-permute-done.30
  210.3 2.5 collective-permute-done.40
  212.9 1.4 collective-permute-start.41
  214.3 2.1 collective-permute-start.34
  216.5 2.0 collective-permute-done.43
  218.5 4.0 %collective-permute-done.42 = f32[64,512]{1,0:T(8,128)S(1)} collective-permute-done((f32[64,512]{1,0:T(8,128)S(1)}, f32[64,512]{1,0:T(8,128)S(1)}, u32[]{:S(2)}, u32[]{:S(2)}) %collective-permute-start.42) | collective-permute-done | bytes 131104 | tf_op jit(solution)/shard_map/ppermute | solution.py:360
  222.4 1.3 collective-permute-start.32
  223.8 0.8 collective-permute-done.34
  224.7 10.4 %collective-permute-done.33 = f32[64,512]{1,0:T(8,128)S(1)} collective-permute-done((f32[64,512]{1,0:T(8,128)S(1)}, f32[64,512]{1,0:T(8,128)S(1)}, u32[]{:S(2)}, u32[]{:S(2)}) %collective-permute-start.33) | collective-permute-done | bytes 131104 | tf_op jit(solution)/shard_map/ppermute | solution.py:360
  235.2 4.4 %collective-permute-start.27 = (s16[528,512]{1,0:T(8,128)(2,1)}, s16[528,512]{1,0:T(8,128)(2,1)S(1)}, u32[]{:S(2)}, u32[]{:S(2)}) collective-permute-start(s16[528,512]{1,0:T(8,128)(2,1)} %get-tuple-element.18), channel_id=1, source_target_pairs={{4,0},{5,1},{6,2},{7,3},{0,4},{1,5},{2,6},{3,7},{12,8},{13,9},{14,... | collective-permute-start | bytes 1622024 | tf_op jit(solution)/shard_map/ppermute | solution.py:427
  239.7 1.5 collective-permute-start.36
  241.2 4.0 %collective-permute-done.45 = f32[128,512]{1,0:T(8,128)S(1)} collective-permute-done((f32[128,512]{1,0:T(8,128)S(1)}, f32[128,512]{1,0:T(8,128)S(1)}, u32[]{:S(2)}, u32[]{:S(2)}) %collective-permute-start.45) | collective-permute-done | bytes 262176 | tf_op jit(solution)/shard_map/ppermute | solution.py:363
  245.2 3.3 collective-permute-start.12
  248.5 0.8 maximum_select_fusion.2
  249.3 0.7 copy-done.17
  250.1 0.2 collective-permute-start.14
  250.3 1.9 maximum_select_fusion.1
  252.2 23.9 %collective-permute-done.27.refs_1_.refs_4_ = s16[528,512]{1,0:T(8,128)(2,1)S(1)} collective-permute-done((s16[528,512]{1,0:T(8,128)(2,1)}, s16[528,512]{1,0:T(8,128)(2,1)S(1)}, u32[]{:S(2)}, u32[]{:S(2)}) %collective-permute-start.27) | collective-permute-done | bytes 540704 | tf_op jit(solution)/shard_map/ppermute | solution.py:427
  276.1 1.4 collective-permute-start.46
  277.6 0.7 copy-done.3
  278.3 2.7 final_sums.2.refs_6_
  281.0 40.9 %collective-permute-done.13.refs_1_.refs_4_ = s16[528,512]{1,0:T(8,128)(2,1)S(1)} collective-permute-done((s16[528,512]{1,0:T(8,128)(2,1)}, s16[528,512]{1,0:T(8,128)(2,1)S(1)}, u32[]{:S(2)}, u32[]{:S(2)}) %collective-permute-start.13) | collective-permute-done | bytes 540704 | tf_op jit(solution)/shard_map/ppermute | solution.py:427
  322.0 0.8 copy-done.5
  322.9 2.7 final_sums.3
  325.7 3.9 %maximum_select_fusion = f32[1024,512]{1,0:T(8,128)} fusion(f32[256,512]{1,0:T(8,128)} %collective-permute-done.46, f32[256,512]{1,0:T(8,128)} %maximum_select_fusion.2, f32[256,512]{1,0:T(8,128)} %collective-permute-done.37, f32[256,512]{1,0:T(8,128)} %maximum_select_fusion.1, pred[]{:T(512)S(6)} %eq.114), kind=kLoop, calls=%fused_computation | loop fusion | flops 3670016 | bytes 4194305 | tf_op jit(solution)/shard_map/jit(_where)/select_n | solution.py:432
  (119 shorter events, 3.1 us)
Async XLA Ops:
  19.8 116.2 %collective-permute-start = (bf16[2048,3328]{1,0:T(8,128)(2,1)}, bf16[2048,3328]{1,0:T(8,128)(2,1)}, u32[]{:S(2)}, u32[]{:S(2)}) collective-permute-start(bf16[2048,3328]{1,0:T(8,128)(2,1)} %pack_strips.2), channel_id=1, source_target_pairs={{1,0},{0,1},{3,2},{2,3},{5,4},{4,5},{7,6},{6,7},{9,8},{8,9},{11,10... | collective-permute-start | bytes 40894472 | tf_op jit(solution)/shard_map/ppermute | solution.py:425
  20.5 16.6 %copy-start = (bf16[2,1024,512]{2,1,0:T(8,128)(2,1)S(1)}, bf16[2,1024,512]{2,1,0:T(8,128)(2,1)}, u32[]{:S(2)}) copy-start(bf16[2,1024,512]{2,1,0:T(8,128)(2,1)} %param.5) | copy-start | bytes 6291460
  37.1 118.4 %collective-permute-start.15 = (bf16[2048,3328]{1,0:T(8,128)(2,1)}, bf16[2048,3328]{1,0:T(8,128)(2,1)}, u32[]{:S(2)}, u32[]{:S(2)}) collective-permute-start(bf16[2048,3328]{1,0:T(8,128)(2,1)} %pack_strips.3), channel_id=1, source_target_pairs={{1,0},{0,1},{3,2},{2,3},{5,4},{4,5},{7,6},{6,7},{9,8},{8,9},{11,10... | collective-permute-start | bytes 40894472 | tf_op jit(solution)/shard_map/ppermute | solution.py:425
  37.2 9.3 %collective-permute-start.2 = (bf16[8,32,512]{2,1,0:T(8,128)(2,1)S(1)}, bf16[8,32,512]{2,1,0:T(8,128)(2,1)S(1)}, u32[]{:S(2)}, u32[]{:S(2)}) collective-permute-start(bf16[8,32,512]{2,1,0:T(8,128)(2,1)S(1)} %get-tuple-element.30), channel_id=1, source_target_pairs={{2,0},{3,1},{4,2},{5,3},{6,4},{7,5},{0,6},{1,7},{10,8},{11,9},{12,... | collective-permute-start | bytes 786440 | tf_op jit(solution)/shard_map/ppermute | solution.py:413
  37.4 19.7 %collective-permute-start.3 = (bf16[8,32,512]{2,1,0:T(8,128)(2,1)S(1)}, bf16[8,32,512]{2,1,0:T(8,128)(2,1)S(1)}, u32[]{:S(2)}, u32[]{:S(2)}) collective-permute-start(bf16[8,32,512]{2,1,0:T(8,128)(2,1)S(1)} %get-tuple-element.30), channel_id=1, source_target_pairs={{4,0},{5,1},{6,2},{7,3},{0,4},{1,5},{2,6},{3,7},{12,8},{13,9},{14,... | collective-permute-start | bytes 786440 | tf_op jit(solution)/shard_map/ppermute | solution.py:413
  37.4 19.7 %collective-permute-start.4 = (bf16[8,32,512]{2,1,0:T(8,128)(2,1)S(1)}, bf16[8,32,512]{2,1,0:T(8,128)(2,1)S(1)}, u32[]{:S(2)}, u32[]{:S(2)}) collective-permute-start(bf16[8,32,512]{2,1,0:T(8,128)(2,1)S(1)} %get-tuple-element.30), channel_id=1, source_target_pairs={{6,0},{7,1},{0,2},{1,3},{2,4},{3,5},{4,6},{5,7},{14,8},{15,9},{8,1... | collective-permute-start | bytes 786440 | tf_op jit(solution)/shard_map/ppermute | solution.py:413
  46.5 21.3 %collective-permute-start.16 = (bf16[8,32,512]{2,1,0:T(8,128)(2,1)S(1)}, bf16[8,32,512]{2,1,0:T(8,128)(2,1)S(1)}, u32[]{:S(2)}, u32[]{:S(2)}) collective-permute-start(bf16[8,32,512]{2,1,0:T(8,128)(2,1)S(1)} %get-tuple-element.29), channel_id=1, source_target_pairs={{2,0},{3,1},{4,2},{5,3},{6,4},{7,5},{0,6},{1,7},{10,8},{11,9},{12,... | collective-permute-start | bytes 786440 | tf_op jit(solution)/shard_map/ppermute | solution.py:413
  57.1 79.0 %copy-start.7 = (bf16[24,32,512]{2,1,0:T(8,128)(2,1)}, bf16[24,32,512]{2,1,0:T(8,128)(2,1)S(1)}, u32[]{:S(2)}) copy-start(bf16[24,32,512]{2,1,0:T(8,128)(2,1)S(1)} %constant_dynamic-update-slice_fusion.refs_2_) | copy-start | bytes 2359300
  57.1 25.1 %collective-permute-start.5 = (bf16[24,32,512]{2,1,0:T(8,128)(2,1)S(1)}, bf16[24,32,512]{2,1,0:T(8,128)(2,1)S(1)}, u32[]{:S(2)}, u32[]{:S(2)}) collective-permute-start(bf16[24,32,512]{2,1,0:T(8,128)(2,1)S(1)} %constant_dynamic-update-slice_fusion.refs_2_), channel_id=1, source_target_pairs={{8,0},{17,1},{10,2},{19,3},{12,4},{21,5},{14,6},{23,7},{0,8},{25,9... | collective-permute-start | bytes 2359304 | tf_op jit(solution)/shard_map/ppermute | solution.py:418
  57.2 21.2 %collective-permute-start.17 = (bf16[8,32,512]{2,1,0:T(8,128)(2,1)S(1)}, bf16[8,32,512]{2,1,0:T(8,128)(2,1)S(1)}, u32[]{:S(2)}, u32[]{:S(2)}) collective-permute-start(bf16[8,32,512]{2,1,0:T(8,128)(2,1)S(1)} %get-tuple-element.29), channel_id=1, source_target_pairs={{4,0},{5,1},{6,2},{7,3},{0,4},{1,5},{2,6},{3,7},{12,8},{13,9},{14,... | collective-permute-start | bytes 786440 | tf_op jit(solution)/shard_map/ppermute | solution.py:413
  67.8 10.9 %collective-permute-start.18 = (bf16[8,32,512]{2,1,0:T(8,128)(2,1)S(1)}, bf16[8,32,512]{2,1,0:T(8,128)(2,1)S(1)}, u32[]{:S(2)}, u32[]{:S(2)}) collective-permute-start(bf16[8,32,512]{2,1,0:T(8,128)(2,1)S(1)} %get-tuple-element.29), channel_id=1, source_target_pairs={{6,0},{7,1},{0,2},{1,3},{2,4},{3,5},{4,6},{5,7},{14,8},{15,9},{8,1... | collective-permute-start | bytes 786440 | tf_op jit(solution)/shard_map/ppermute | solution.py:413
  78.4 15.3 %collective-permute-start.6 = (bf16[24,32,512]{2,1,0:T(8,128)(2,1)S(1)}, bf16[24,32,512]{2,1,0:T(8,128)(2,1)S(1)}, u32[]{:S(2)}, u32[]{:S(2)}) collective-permute-start(bf16[24,32,512]{2,1,0:T(8,128)(2,1)S(1)} %constant_dynamic-update-slice_fusion.refs_2_), channel_id=1, source_target_pairs={{16,0},{9,1},{18,2},{11,3},{20,4},{13,5},{22,6},{15,7},{24,8},{1,9... | collective-permute-start | bytes 2359304 | tf_op jit(solution)/shard_map/ppermute | solution.py:418
  78.6 15.4 %collective-permute-start.8 = (bf16[24,32,512]{2,1,0:T(8,128)(2,1)S(1)}, bf16[24,32,512]{2,1,0:T(8,128)(2,1)S(1)}, u32[]{:S(2)}, u32[]{:S(2)}) collective-permute-start(bf16[24,32,512]{2,1,0:T(8,128)(2,1)S(1)} %constant_dynamic-update-slice_fusion.refs_2_), channel_id=1, source_target_pairs={{1,0},{0,1},{3,2},{2,3},{5,4},{4,5},{7,6},{6,7},{9,8},{8,9},{11,10... | collective-permute-start | bytes 2359304 | tf_op jit(solution)/shard_map/ppermute | solution.py:419
  82.3 22.4 %copy-start.8 = (bf16[24,32,512]{2,1,0:T(8,128)(2,1)}, bf16[24,32,512]{2,1,0:T(8,128)(2,1)S(1)}, u32[]{:S(2)}) copy-start(bf16[24,32,512]{2,1,0:T(8,128)(2,1)S(1)} %constant_dynamic-update-slice_fusion.3.refs_2_) | copy-start | bytes 2359300
  82.3 24.1 %copy-start.11 = (bf16[24,32,512]{2,1,0:T(8,128)(2,1)}, bf16[24,32,512]{2,1,0:T(8,128)(2,1)S(1)}, u32[]{:S(2)}) copy-start(bf16[24,32,512]{2,1,0:T(8,128)(2,1)S(1)} %collective-permute-done.5.refs_3_) | copy-start | bytes 2359300
  82.3 19.9 %collective-permute-start.19 = (bf16[24,32,512]{2,1,0:T(8,128)(2,1)S(1)}, bf16[24,32,512]{2,1,0:T(8,128)(2,1)}, u32[]{:S(2)}, u32[]{:S(2)}) collective-permute-start(bf16[24,32,512]{2,1,0:T(8,128)(2,1)S(1)} %constant_dynamic-update-slice_fusion.3.refs_2_), channel_id=1, source_target_pairs={{8,0},{17,1},{10,2},{19,3},{12,4},{21,5},{14,6},{23,7},{0,8},{25,9... | collective-permute-start | bytes 2359304 | tf_op jit(solution)/shard_map/ppermute | solution.py:418
  93.7 29.5 %copy-start.13 = (bf16[24,32,512]{2,1,0:T(8,128)(2,1)}, bf16[24,32,512]{2,1,0:T(8,128)(2,1)S(1)}, u32[]{:S(2)}) copy-start(bf16[24,32,512]{2,1,0:T(8,128)(2,1)S(1)} %collective-permute-done.6.refs_4_) | copy-start | bytes 2359300
  93.7 12.7 %collective-permute-start.20 = (bf16[24,32,512]{2,1,0:T(8,128)(2,1)S(1)}, bf16[24,32,512]{2,1,0:T(8,128)(2,1)S(1)}, u32[]{:S(2)}, u32[]{:S(2)}) collective-permute-start(bf16[24,32,512]{2,1,0:T(8,128)(2,1)S(1)} %constant_dynamic-update-slice_fusion.3.refs_2_), channel_id=1, source_target_pairs={{16,0},{9,1},{18,2},{11,3},{20,4},{13,5},{22,6},{15,7},{24,8},{1,9... | collective-permute-start | bytes 2359304 | tf_op jit(solution)/shard_map/ppermute | solution.py:418
  94.0 31.0 %copy-start.14 = (bf16[24,32,512]{2,1,0:T(8,128)(2,1)}, bf16[24,32,512]{2,1,0:T(8,128)(2,1)S(1)}, u32[]{:S(2)}) copy-start(bf16[24,32,512]{2,1,0:T(8,128)(2,1)S(1)} %collective-permute-done.8.refs_6_) | copy-start | bytes 2359300
  94.0 21.0 %collective-permute-start.7 = (bf16[24,32,512]{2,1,0:T(8,128)(2,1)S(1)}, bf16[24,32,512]{2,1,0:T(8,128)(2,1)}, u32[]{:S(2)}, u32[]{:S(2)}) collective-permute-start(bf16[24,32,512]{2,1,0:T(8,128)(2,1)S(1)} %collective-permute-done.5.refs_3_), channel_id=1, source_target_pairs={{16,0},{9,1},{18,2},{11,3},{20,4},{13,5},{22,6},{15,7},{24,8},{1,9... | collective-permute-start | bytes 2359304 | tf_op jit(solution)/shard_map/ppermute | solution.py:418
  102.2 33.3 %collective-permute-start.1 = (bf16[16,128,512]{2,1,0:T(8,128)(2,1)S(1)}, bf16[16,128,512]{2,1,0:T(8,128)(2,1)}, u32[]{:S(2)}, u32[]{:S(2)}) collective-permute-start(bf16[16,128,512]{2,1,0:T(8,128)(2,1)S(1)} %bitcast.21), channel_id=1, source_target_pairs={{1,0},{0,1},{3,2},{2,3},{5,4},{4,5},{7,6},{6,7},{9,8},{8,9},{11,10... | collective-permute-start | bytes 6291464 | tf_op jit(solution)/shard_map/ppermute | solution.py:405
  106.4 16.7 %copy-start.12 = (bf16[24,32,512]{2,1,0:T(8,128)(2,1)}, bf16[24,32,512]{2,1,0:T(8,128)(2,1)S(1)}, u32[]{:S(2)}) copy-start(bf16[24,32,512]{2,1,0:T(8,128)(2,1)S(1)} %collective-permute-done.20.refs_4_) | copy-start | bytes 2359300
  106.4 16.7 %collective-permute-start.9 = (bf16[24,32,512]{2,1,0:T(8,128)(2,1)S(1)}, bf16[24,32,512]{2,1,0:T(8,128)(2,1)S(1)}, u32[]{:S(2)}, u32[]{:S(2)}) collective-permute-start(bf16[24,32,512]{2,1,0:T(8,128)(2,1)S(1)} %collective-permute-done.5.refs_3_), channel_id=1, source_target_pairs={{1,0},{0,1},{3,2},{2,3},{5,4},{4,5},{7,6},{6,7},{9,8},{8,9},{11,10... | collective-permute-start | bytes 2359304 | tf_op jit(solution)/shard_map/ppermute | solution.py:419
  115.0 10.1 %collective-permute-start.10 = (bf16[24,32,512]{2,1,0:T(8,128)(2,1)S(1)}, bf16[24,32,512]{2,1,0:T(8,128)(2,1)S(1)}, u32[]{:S(2)}, u32[]{:S(2)}) collective-permute-start(bf16[24,32,512]{2,1,0:T(8,128)(2,1)S(1)} %collective-permute-done.6.refs_4_), channel_id=1, source_target_pairs={{1,0},{0,1},{3,2},{2,3},{5,4},{4,5},{7,6},{6,7},{9,8},{8,9},{11,10... | collective-permute-start | bytes 2359304 | tf_op jit(solution)/shard_map/ppermute | solution.py:419
  123.1 1.9 copy-start.15
  123.1 11.5 %collective-permute-start.21 = (bf16[24,32,512]{2,1,0:T(8,128)(2,1)}, bf16[24,32,512]{2,1,0:T(8,128)(2,1)}, u32[]{:S(2)}, u32[]{:S(2)}) collective-permute-start(bf16[24,32,512]{2,1,0:T(8,128)(2,1)} %collective-permute-done.19.refs_3_), channel_id=1, source_target_pairs={{16,0},{9,1},{18,2},{11,3},{20,4},{13,5},{22,6},{15,7},{24,8},{1,9... | collective-permute-start | bytes 2359304 | tf_op jit(solution)/shard_map/ppermute | solution.py:418
  125.0 0.9 copy-start.16
  125.9 9.6 %collective-permute-start.11 = (bf16[24,32,512]{2,1,0:T(8,128)(2,1)}, bf16[24,32,512]{2,1,0:T(8,128)(2,1)}, u32[]{:S(2)}, u32[]{:S(2)}) collective-permute-start(bf16[24,32,512]{2,1,0:T(8,128)(2,1)} %collective-permute-done.7.refs_5_), channel_id=1, source_target_pairs={{1,0},{0,1},{3,2},{2,3},{5,4},{4,5},{7,6},{6,7},{9,8},{8,9},{11,10... | collective-permute-start | bytes 2359304 | tf_op jit(solution)/shard_map/ppermute | solution.py:419
  134.6 20.5 %collective-permute-start.22 = (bf16[24,32,512]{2,1,0:T(8,128)(2,1)}, bf16[24,32,512]{2,1,0:T(8,128)(2,1)}, u32[]{:S(2)}, u32[]{:S(2)}) collective-permute-start(bf16[24,32,512]{2,1,0:T(8,128)(2,1)} %copy-done.8), channel_id=1, source_target_pairs={{1,0},{0,1},{3,2},{2,3},{5,4},{4,5},{7,6},{6,7},{9,8},{8,9},{11,10... | collective-permute-start | bytes 2359304 | tf_op jit(solution)/shard_map/ppermute | solution.py:419
  135.5 20.0 %collective-permute-start.23 = (bf16[24,32,512]{2,1,0:T(8,128)(2,1)}, bf16[24,32,512]{2,1,0:T(8,128)(2,1)}, u32[]{:S(2)}, u32[]{:S(2)}) collective-permute-start(bf16[24,32,512]{2,1,0:T(8,128)(2,1)} %collective-permute-done.19.refs_3_), channel_id=1, source_target_pairs={{1,0},{0,1},{3,2},{2,3},{5,4},{4,5},{7,6},{6,7},{9,8},{8,9},{11,10... | collective-permute-start | bytes 2359304 | tf_op jit(solution)/shard_map/ppermute | solution.py:419
  135.5 20.0 %collective-permute-start.24 = (bf16[24,32,512]{2,1,0:T(8,128)(2,1)}, bf16[24,32,512]{2,1,0:T(8,128)(2,1)}, u32[]{:S(2)}, u32[]{:S(2)}) collective-permute-start(bf16[24,32,512]{2,1,0:T(8,128)(2,1)} %copy-done.12), channel_id=1, source_target_pairs={{1,0},{0,1},{3,2},{2,3},{5,4},{4,5},{7,6},{6,7},{9,8},{8,9},{11,10... | collective-permute-start | bytes 2359304 | tf_op jit(solution)/shard_map/ppermute | solution.py:419
  136.0 19.5 %collective-permute-start.25 = (bf16[24,32,512]{2,1,0:T(8,128)(2,1)}, bf16[24,32,512]{2,1,0:T(8,128)(2,1)}, u32[]{:S(2)}, u32[]{:S(2)}) collective-permute-start(bf16[24,32,512]{2,1,0:T(8,128)(2,1)} %collective-permute-done.21.refs_5_), channel_id=1, source_target_pairs={{1,0},{0,1},{3,2},{2,3},{5,4},{4,5},{7,6},{6,7},{9,8},{8,9},{11,10... | collective-permute-start | bytes 2359304 | tf_op jit(solution)/shard_map/ppermute | solution.py:419
  155.1 46.5 %copy-start.9 = (f32[512,512]{1,0:T(8,128)S(1)}, f32[512,512]{1,0:T(8,128)}, u32[]{:S(2)}) copy-start(f32[512,512]{1,0:T(8,128)} %get-tuple-element.21) | copy-start | bytes 3145732
  155.1 46.5 %collective-permute-start.38 = (f32[256,512]{1,0:T(8,128)}, f32[256,512]{1,0:T(8,128)S(1)}, u32[]{:S(2)}, u32[]{:S(2)}) collective-permute-start(f32[256,512]{1,0:T(8,128)} %constant_dynamic-slice_fusion.2), channel_id=1, source_target_pairs={{1,0},{0,1},{3,2},{2,3},{5,4},{4,5},{7,6},{6,7},{9,8},{8,9},{11,10... | collective-permute-start | bytes 1572872 | tf_op jit(solution)/shard_map/ppermute | solution.py:356
  172.7 29.2 %copy-start.10 = (f32[512,512]{1,0:T(8,128)S(1)}, f32[512,512]{1,0:T(8,128)}, u32[]{:S(2)}) copy-start(f32[512,512]{1,0:T(8,128)} %get-tuple-element.20) | copy-start | bytes 3145732
  174.7 27.2 %collective-permute-start.29 = (f32[256,512]{1,0:T(8,128)}, f32[256,512]{1,0:T(8,128)}, u32[]{:S(2)}, u32[]{:S(2)}) collective-permute-start(f32[256,512]{1,0:T(8,128)} %constant_dynamic-slice_fusion.5), channel_id=1, source_target_pairs={{1,0},{0,1},{3,2},{2,3},{5,4},{4,5},{7,6},{6,7},{9,8},{8,9},{11,10... | collective-permute-start | bytes 1572872 | tf_op jit(solution)/shard_map/ppermute | solution.py:356
  174.9 74.4 %collective-permute-start.26 = (s16[528,512]{1,0:T(8,128)(2,1)}, s16[528,512]{1,0:T(8,128)(2,1)S(1)}, u32[]{:S(2)}, u32[]{:S(2)}) collective-permute-start(s16[528,512]{1,0:T(8,128)(2,1)} %get-tuple-element.17), channel_id=1, source_target_pairs={{6,0},{7,1},{0,2},{1,3},{2,4},{3,5},{4,6},{5,7},{14,8},{15,9},{8,1... | collective-permute-start | bytes 1622024 | tf_op jit(solution)/shard_map/ppermute | solution.py:427
  201.8 5.6 %collective-permute-start.39 = (f32[128,512]{1,0:T(8,128)S(1)}, f32[128,512]{1,0:T(8,128)S(1)}, u32[]{:S(2)}, u32[]{:S(2)}) collective-permute-start(f32[128,512]{1,0:T(8,128)S(1)} %constant_dynamic-slice_fusion.1), channel_id=1, source_target_pairs={{8,0},{17,1},{10,2},{19,3},{12,4},{21,5},{14,6},{23,7},{0,8},{25,9... | collective-permute-start | bytes 786440 | tf_op jit(solution)/shard_map/ppermute | solution.py:359
  203.0 7.1 %collective-permute-start.30 = (f32[128,512]{1,0:T(8,128)S(1)}, f32[128,512]{1,0:T(8,128)S(1)}, u32[]{:S(2)}, u32[]{:S(2)}) collective-permute-start(f32[128,512]{1,0:T(8,128)S(1)} %constant_dynamic-slice_fusion.4), channel_id=1, source_target_pairs={{8,0},{17,1},{10,2},{19,3},{12,4},{21,5},{14,6},{23,7},{0,8},{25,9... | collective-permute-start | bytes 786440 | tf_op jit(solution)/shard_map/ppermute | solution.py:359
  207.4 5.4 %collective-permute-start.40 = (f32[64,512]{1,0:T(8,128)S(1)}, f32[64,512]{1,0:T(8,128)S(1)}, u32[]{:S(2)}, u32[]{:S(2)}) collective-permute-start(f32[64,512]{1,0:T(8,128)S(1)} %constant_dynamic-slice_fusion), channel_id=1, source_target_pairs={{16,0},{9,1},{18,2},{11,3},{20,4},{13,5},{22,6},{15,7},{24,8},{1,9... | collective-permute-start | bytes 393224 | tf_op jit(solution)/shard_map/ppermute | solution.py:359
  210.2 4.1 %collective-permute-start.31 = (f32[64,512]{1,0:T(8,128)S(1)}, f32[64,512]{1,0:T(8,128)S(1)}, u32[]{:S(2)}, u32[]{:S(2)}) collective-permute-start(f32[64,512]{1,0:T(8,128)S(1)} %constant_dynamic-slice_fusion.3), channel_id=1, source_target_pairs={{16,0},{9,1},{18,2},{11,3},{20,4},{13,5},{22,6},{15,7},{24,8},{1,9... | collective-permute-start | bytes 393224 | tf_op jit(solution)/shard_map/ppermute | solution.py:359
  212.8 5.6 %collective-permute-start.43 = (f32[64,512]{1,0:T(8,128)S(1)}, f32[64,512]{1,0:T(8,128)S(1)}, u32[]{:S(2)}, u32[]{:S(2)}) collective-permute-start(f32[64,512]{1,0:T(8,128)S(1)} %dynamic-slice_add_fusion.4), channel_id=1, source_target_pairs={{6,0},{7,1},{0,2},{1,3},{2,4},{3,5},{4,6},{5,7},{14,8},{15,9},{8,1... | collective-permute-start | bytes 393224 | tf_op jit(solution)/shard_map/ppermute | solution.py:360
  212.9 9.6 %collective-permute-start.42 = (f32[64,512]{1,0:T(8,128)S(1)}, f32[64,512]{1,0:T(8,128)S(1)}, u32[]{:S(2)}, u32[]{:S(2)}) collective-permute-start(f32[64,512]{1,0:T(8,128)S(1)} %dynamic-slice_add_fusion.4), channel_id=1, source_target_pairs={{4,0},{5,1},{6,2},{7,3},{0,4},{1,5},{2,6},{3,7},{12,8},{13,9},{14,... | collective-permute-start | bytes 393224 | tf_op jit(solution)/shard_map/ppermute | solution.py:360
  212.9 10.8 %collective-permute-start.41 = (f32[64,512]{1,0:T(8,128)S(1)}, f32[64,512]{1,0:T(8,128)S(1)}, u32[]{:S(2)}, u32[]{:S(2)}) collective-permute-start(f32[64,512]{1,0:T(8,128)S(1)} %dynamic-slice_add_fusion.4), channel_id=1, source_target_pairs={{2,0},{3,1},{4,2},{5,3},{6,4},{7,5},{0,6},{1,7},{10,8},{11,9},{12,... | collective-permute-start | bytes 393224 | tf_op jit(solution)/shard_map/ppermute | solution.py:360
  214.3 10.3 %collective-permute-start.34 = (f32[64,512]{1,0:T(8,128)S(1)}, f32[64,512]{1,0:T(8,128)S(1)}, u32[]{:S(2)}, u32[]{:S(2)}) collective-permute-start(f32[64,512]{1,0:T(8,128)S(1)} %dynamic-slice_add_fusion.5), channel_id=1, source_target_pairs={{6,0},{7,1},{0,2},{1,3},{2,4},{3,5},{4,6},{5,7},{14,8},{15,9},{8,1... | collective-permute-start | bytes 393224 | tf_op jit(solution)/shard_map/ppermute | solution.py:360
  218.4 16.6 %collective-permute-start.33 = (f32[64,512]{1,0:T(8,128)S(1)}, f32[64,512]{1,0:T(8,128)S(1)}, u32[]{:S(2)}, u32[]{:S(2)}) collective-permute-start(f32[64,512]{1,0:T(8,128)S(1)} %dynamic-slice_add_fusion.5), channel_id=1, source_target_pairs={{4,0},{5,1},{6,2},{7,3},{0,4},{1,5},{2,6},{3,7},{12,8},{13,9},{14,... | collective-permute-start | bytes 393224 | tf_op jit(solution)/shard_map/ppermute | solution.py:360
  222.4 12.7 %collective-permute-start.32 = (f32[64,512]{1,0:T(8,128)S(1)}, f32[64,512]{1,0:T(8,128)S(1)}, u32[]{:S(2)}, u32[]{:S(2)}) collective-permute-start(f32[64,512]{1,0:T(8,128)S(1)} %dynamic-slice_add_fusion.5), channel_id=1, source_target_pairs={{2,0},{3,1},{4,2},{5,3},{6,4},{7,5},{0,6},{1,7},{10,8},{11,9},{12,... | collective-permute-start | bytes 393224 | tf_op jit(solution)/shard_map/ppermute | solution.py:360
  223.8 15.8 %collective-permute-start.44 = (f32[64,512]{1,0:T(8,128)S(1)}, f32[64,512]{1,0:T(8,128)S(1)}, u32[]{:S(2)}, u32[]{:S(2)}) collective-permute-start(f32[64,512]{1,0:T(8,128)S(1)} %add_add_fusion), channel_id=1, source_target_pairs={{16,0},{9,1},{18,2},{11,3},{20,4},{13,5},{22,6},{15,7},{24,8},{1,9... | collective-permute-start | bytes 393224 | tf_op jit(solution)/shard_map/ppermute | solution.py:363
  235.1 4.6 %collective-permute-start.35 = (f32[64,512]{1,0:T(8,128)S(1)}, f32[64,512]{1,0:T(8,128)S(1)}, u32[]{:S(2)}, u32[]{:S(2)}) collective-permute-start(f32[64,512]{1,0:T(8,128)S(1)} %add_add_fusion.1), channel_id=1, source_target_pairs={{16,0},{9,1},{18,2},{11,3},{20,4},{13,5},{22,6},{15,7},{24,8},{1,9... | collective-permute-start | bytes 393224 | tf_op jit(solution)/shard_map/ppermute | solution.py:363
  235.2 40.9 %collective-permute-start.27 = (s16[528,512]{1,0:T(8,128)(2,1)}, s16[528,512]{1,0:T(8,128)(2,1)S(1)}, u32[]{:S(2)}, u32[]{:S(2)}) collective-permute-start(s16[528,512]{1,0:T(8,128)(2,1)} %get-tuple-element.18), channel_id=1, source_target_pairs={{4,0},{5,1},{6,2},{7,3},{0,4},{1,5},{2,6},{3,7},{12,8},{13,9},{14,... | collective-permute-start | bytes 1622024 | tf_op jit(solution)/shard_map/ppermute | solution.py:427
  239.6 37.9 %collective-permute-start.28 = (s16[528,512]{1,0:T(8,128)(2,1)}, s16[528,512]{1,0:T(8,128)(2,1)S(1)}, u32[]{:S(2)}, u32[]{:S(2)}) collective-permute-start(s16[528,512]{1,0:T(8,128)(2,1)} %get-tuple-element.19), channel_id=1, source_target_pairs={{2,0},{3,1},{4,2},{5,3},{6,4},{7,5},{0,6},{1,7},{10,8},{11,9},{12,... | collective-permute-start | bytes 1622024 | tf_op jit(solution)/shard_map/ppermute | solution.py:427
  239.6 5.6 %collective-permute-start.45 = (f32[128,512]{1,0:T(8,128)S(1)}, f32[128,512]{1,0:T(8,128)S(1)}, u32[]{:S(2)}, u32[]{:S(2)}) collective-permute-start(f32[128,512]{1,0:T(8,128)S(1)} %maximum_select_fusion.4), channel_id=1, source_target_pairs={{8,0},{17,1},{10,2},{19,3},{12,4},{21,5},{14,6},{23,7},{0,8},{25,9... | collective-permute-start | bytes 786440 | tf_op jit(solution)/shard_map/ppermute | solution.py:363
  239.7 9.6 %collective-permute-start.36 = (f32[128,512]{1,0:T(8,128)S(1)}, f32[128,512]{1,0:T(8,128)S(1)}, u32[]{:S(2)}, u32[]{:S(2)}) collective-permute-start(f32[128,512]{1,0:T(8,128)S(1)} %maximum_select_fusion.3), channel_id=1, source_target_pairs={{8,0},{17,1},{10,2},{19,3},{12,4},{21,5},{14,6},{23,7},{0,8},{25,9... | collective-permute-start | bytes 786440 | tf_op jit(solution)/shard_map/ppermute | solution.py:363
  245.2 35.8 %collective-permute-start.12 = (s16[528,512]{1,0:T(8,128)(2,1)}, s16[528,512]{1,0:T(8,128)(2,1)S(1)}, u32[]{:S(2)}, u32[]{:S(2)}) collective-permute-start(s16[528,512]{1,0:T(8,128)(2,1)} %get-tuple-element.13), channel_id=1, source_target_pairs={{6,0},{7,1},{0,2},{1,3},{2,4},{3,5},{4,6},{5,7},{14,8},{15,9},{8,1... | collective-permute-start | bytes 1622024 | tf_op jit(solution)/shard_map/ppermute | solution.py:427
  249.3 28.2 %copy-start.1 = (s16[528,512]{1,0:T(8,128)(2,1)}, s16[528,512]{1,0:T(8,128)(2,1)S(1)}, u32[]{:S(2)}) copy-start(s16[528,512]{1,0:T(8,128)(2,1)S(1)} %collective-permute-done.26.refs_0_.refs_3_) | copy-start | bytes 1622020
  249.3 72.6 %collective-permute-start.13 = (s16[528,512]{1,0:T(8,128)(2,1)}, s16[528,512]{1,0:T(8,128)(2,1)S(1)}, u32[]{:S(2)}, u32[]{:S(2)}) collective-permute-start(s16[528,512]{1,0:T(8,128)(2,1)} %get-tuple-element.14), channel_id=1, source_target_pairs={{4,0},{5,1},{6,2},{7,3},{0,4},{1,5},{2,6},{3,7},{12,8},{13,9},{14,... | collective-permute-start | bytes 1622024 | tf_op jit(solution)/shard_map/ppermute | solution.py:427
  250.1 71.9 %collective-permute-start.14 = (s16[528,512]{1,0:T(8,128)(2,1)}, s16[528,512]{1,0:T(8,128)(2,1)S(1)}, u32[]{:S(2)}, u32[]{:S(2)}) collective-permute-start(s16[528,512]{1,0:T(8,128)(2,1)} %get-tuple-element.15), channel_id=1, source_target_pairs={{2,0},{3,1},{4,2},{5,3},{6,4},{7,5},{0,6},{1,7},{10,8},{11,9},{12,... | collective-permute-start | bytes 1622024 | tf_op jit(solution)/shard_map/ppermute | solution.py:427
  276.1 1.5 copy-start.2
  276.1 49.6 %collective-permute-start.46 = (f32[256,512]{1,0:T(8,128)}, f32[256,512]{1,0:T(8,128)}, u32[]{:S(2)}, u32[]{:S(2)}) collective-permute-start(f32[256,512]{1,0:T(8,128)} %maximum_select_fusion.2), channel_id=1, source_target_pairs={{1,0},{0,1},{3,2},{2,3},{5,4},{4,5},{7,6},{6,7},{9,8},{8,9},{11,10... | collective-permute-start | bytes 1572872 | tf_op jit(solution)/shard_map/ppermute | solution.py:366
  277.5 0.8 copy-start.3
  277.5 48.2 %collective-permute-start.37 = (f32[256,512]{1,0:T(8,128)}, f32[256,512]{1,0:T(8,128)}, u32[]{:S(2)}, u32[]{:S(2)}) collective-permute-start(f32[256,512]{1,0:T(8,128)} %maximum_select_fusion.1), channel_id=1, source_target_pairs={{1,0},{0,1},{3,2},{2,3},{5,4},{4,5},{7,6},{6,7},{9,8},{8,9},{11,10... | collective-permute-start | bytes 1572872 | tf_op jit(solution)/shard_map/ppermute | solution.py:366
  281.0 40.9 %copy-start.4 = (s16[528,512]{1,0:T(8,128)(2,1)}, s16[528,512]{1,0:T(8,128)(2,1)S(1)}, u32[]{:S(2)}) copy-start(s16[528,512]{1,0:T(8,128)(2,1)S(1)} %collective-permute-done.12.refs_0_.refs_3_) | copy-start | bytes 1622020
  321.9 0.8 copy-start.5
  321.9 1.0 copy-start.6
  (1 other events, 0.7 us)

commit v2 on v1

--- a/solution.py
+++ b/solution.py
@@ -26,8 +26,26 @@
     ]
 
 
+def row_jump(n_row, n_col, directions):
+    bits = n_row.bit_length() - 1
+    masks = [sum(swap_bit(bits, p, b) for b in range(bits) if directions >> b & 1) for p in (0, 1)]
+    return [((r ^ masks[c % 2]) * n_col + c, r * n_col + c) for r in range(n_row) for c in range(n_col)]
+
+
 def core_swap(n_col):
     return [(c ^ 1, c) for c in range(n_col)]
+
+
+def line_swap(n_col, mask):
+    return [(c ^ (2 * mask), c) for c in range(n_col)]
+
+
+def inward(n_col):
+    return [(c, c + 2 if c < 2 else c - 2) for c in range(n_col) if c < 2 or c >= n_col - 2]
+
+
+def across(n_col):
+    return [(c, (c ^ 6)) for c in range(2, n_col - 2)]
 
 
 def line_shift(n_col, shift):
@@ -97,33 +115,63 @@
 def slot_of(dims, my_col, parity, at):
     _, n_col, _, max_rows, _, _ = dims
     in_chunk = max_rows // n_col
-    n_line = n_col // 2
-    chunk = 2 * lax.rem(lax.div(my_col, 2) + lax.div(at, in_chunk), n_line) + parity
+    chunk = 2 * (lax.div(my_col, 2) ^ lax.div(at, in_chunk)) + parity
     return chunk * in_chunk + lax.rem(at, in_chunk)
 
 
-def pack_kernel(tab, strip, out):
-    out[...] = strip[...]
-
-
-def pack_strips(tab, inverse, dims):
+def pack_kernel(dims, tab, inverse, packed, strips, in_sem, out_sem):
     _, _, _, max_rows, max_cols, _ = dims
     base = 2 * max_rows + 2 * max_cols
-    count = max_rows // 2
-    block = (BS, inverse.shape[1])
-
-    def strip(at, tab):
-        my_col = tab[base + 3]
-        return tab[max_rows + slot_of(dims, my_col, 1 - lax.rem(my_col, 2), at)], 0
-
+    n_rows, my_col = tab[base], tab[base + 3]
+    count, depth = max_rows // 2, strips.shape[0]
+
+    def position(at):
+        return slot_of(dims, my_col, 1 - lax.rem(my_col, 2), at)
+
+    def copy_in(at):
+        block = tab[max_rows + position(at)]
+        rows = inverse.at[pl.ds(pl.multiple_of(block * BS, BS), BS)]
+        return pltpu.make_async_copy(rows, strips.at[at % depth], in_sem.at[at % depth])
+
+    def copy_out(at):
+        return pltpu.make_async_copy(strips.at[at % depth], packed.at[pl.ds(at * BS, BS)], out_sem.at[at % depth])
+
+    def if_listed(at, act):
+        @pl.when(position(at) < n_rows)
+        def _():
+            act()
+
+    ahead = depth // 2
+    for at in range(count + depth):
+        if at < count:
+            if at >= depth:
+                if_listed(at - depth, copy_out(at - depth).wait)
+            if_listed(at, copy_in(at).start)
+        elif at - depth < count:
+            if_listed(at - depth, copy_out(at - depth).wait)
+        if 0 <= at - ahead < count:
+            if_listed(at - ahead, copy_in(at - ahead).wait)
+            if_listed(at - ahead, copy_out(at - ahead).start)
+
+
+def pack_strips(tab, inverse, dims):
+    max_rows = dims[3]
+    width = inverse.shape[1]
+    any_spec = pl.BlockSpec(memory_space=pl.ANY)
+    depth = min(8, max_rows // 2)
     return pl.pallas_call(
-        pack_kernel,
-        out_shape=jax.ShapeDtypeStruct((count * BS, inverse.shape[1]), inverse.dtype),
+        functools.partial(pack_kernel, dims),
+        out_shape=jax.ShapeDtypeStruct((max_rows // 2 * BS, width), inverse.dtype),
         grid_spec=pltpu.PrefetchScalarGridSpec(
             num_scalar_prefetch=1,
-            grid=(count,),
-            in_specs=[pl.BlockSpec(block, strip)],
-            out_specs=pl.BlockSpec(block, lambda at, tab: (at, 0)),
+            grid=(1,),
+            in_specs=[any_spec],
+            out_specs=any_spec,
+            scratch_shapes=[
+                pltpu.VMEM((depth, BS, width), inverse.dtype),
+                pltpu.SemaphoreType.DMA((depth,)),
+                pltpu.SemaphoreType.DMA((depth,)),
+            ],
         ),
         cost_estimate=pl.CostEstimate(flops=0, bytes_accessed=27 * 10**6, transcendentals=0),
         name="pack_strips",
@@ -136,8 +184,9 @@
     in_chunk = max_rows // n_col
     own = refs[0:2]
     pieces = (refs[2 : 2 + n_row], refs[2 + n_row : 2 + 2 * n_row])
-    first_ref, diag, *outs = refs[2 + 2 * n_row : -7]
-    total, cols_buf, rows_buf, strips, cols_sem, rows_sem, strip_sem = refs[-7:]
+    total_ref, *outs = refs[2 + 2 * n_row : -4]
+    cols_buf, strips, cols_sem, strip_sem = refs[-4:]
+    total = total_ref.at[0]
     step = pl.program_id(0)
     chunk_rows = in_chunk * BS
     group_rows = GROUP * BS
@@ -186,23 +235,9 @@
         for ahead in range(1, slots - 1):
             start_strips(ahead, ahead)
 
-        @pl.loop(0, n_line * in_chunk)
-        def _(at):
-            k = slot_of(dims, my_col, my_parity, at)
-
-            @pl.when(k < n_rows)
-            def _():
-                start_fetch(dims, supernode, my_row, my_col, own, pieces, tab[k], rows_buf, at, rows_sem.at[at])
-
-            @pl.when(k >= n_rows)
-            def _():
-                clear_block(rows_buf, at)
-
         @pl.loop(n_cols, lax.div(n_cols + GROUP - 1, GROUP) * GROUP)
         def _(j):
             clear_block(cols_buf, j)
-
-        diag[...] = jnp.zeros_like(diag)
 
         @pl.loop(0, n_cols)
         def _(j):
@@ -246,29 +281,18 @@
             def _(item=item):
                 total[pl.ds(item * BS, BS), :] = jnp.zeros((BS, total.shape[1]), total.dtype)
 
-            @pl.when(item < left)
-            def _(item=item):
-                wait_fetch(rows_buf, step * in_chunk + item, rows_sem.at[step * in_chunk + item])
-
-        sums = total[...]
-        high = sums.astype(jnp.bfloat16)
-        low = (sums - high.astype(jnp.float32)).astype(jnp.bfloat16)
-        rows = rows_buf[pl.ds(pl.multiple_of(step * chunk_rows, chunk_rows), chunk_rows), :].T
-        rows = jnp.concatenate([rows, rows], axis=1)
-        both = jnp.concatenate([high, low], axis=0)
-        diag[...] -= jnp.dot(rows, both, preferred_element_type=jnp.float32)
-
-    @pl.when(step == 0)
-    def _():
-        first_ref[...] = total[...]
-
-    for shift, out in enumerate(outs, 1):
-
-        @pl.when(step == shift)
+
+    for mask, out in zip(coded_masks(n_line), outs):
+
+        @pl.when(step == mask)
         def _(out=out):
             body, tail = encode(total[...])
             out[0:chunk_rows, :] = body
             out[chunk_rows:, :] = tail
+
+
+def coded_masks(n_line):
+    return (1, 3) if n_line == 4 else tuple(range(1, n_line))
 
 
 def products(tab, inverse, packed, own, pieces, dims, supernode):
@@ -283,23 +307,18 @@
     operands = [inverse, packed, *own, *pieces[0], *pieces[1]]
     return pl.pallas_call(
         functools.partial(product_kernel, dims, supernode),
-        out_shape=(
-            jax.ShapeDtypeStruct((chunk_rows, width), jnp.float32),
-            jax.ShapeDtypeStruct((width, width), jnp.float32),
-        )
-        + (jax.ShapeDtypeStruct(coded_shape, jnp.int16),) * (n_line - 1),
+        out_shape=(jax.ShapeDtypeStruct((n_line, chunk_rows, width), jnp.float32),)
+        + (jax.ShapeDtypeStruct(coded_shape, jnp.int16),) * len(coded_masks(n_line)),
         grid_spec=pltpu.PrefetchScalarGridSpec(
             num_scalar_prefetch=1,
             grid=(n_line,),
             in_specs=[any_spec] * len(operands),
-            out_specs=[whole((chunk_rows, width)), whole((width, width))] + [whole(coded_shape)] * (n_line - 1),
+            out_specs=[pl.BlockSpec((1, chunk_rows, width), lambda g, tab: (g, 0, 0))]
+            + [whole(coded_shape)] * len(coded_masks(n_line)),
             scratch_shapes=[
-                pltpu.VMEM((chunk_rows, width), jnp.float32),
                 pltpu.VMEM((max_cols * BS, width), jnp.bfloat16),
-                pltpu.VMEM((n_line * chunk_rows, width), jnp.bfloat16),
                 pltpu.VMEM((3, chunk_rows, 2 * inverse.shape[1]), jnp.bfloat16),
                 pltpu.SemaphoreType.DMA((max_cols,)),
-                pltpu.SemaphoreType.DMA((n_line * in_chunk,)),
                 pltpu.SemaphoreType.DMA((3, in_chunk, 2)),
             ],
         ),
@@ -308,21 +327,119 @@
     )(tab, *operands)
 
 
+def diag_kernel(dims, supernode, tab, total, *refs):
+    n_row, n_col, _, max_rows, max_cols, _ = dims
+    n_line = n_col // 2
+    in_chunk = max_rows // n_col
+    own = refs[0:2]
+    pieces = (refs[2 : 2 + n_row], refs[2 + n_row : 2 + 2 * n_row])
+    sent, kept, diag, rows_buf, rows_sem = refs[2 + 2 * n_row :]
+    step = pl.program_id(0)
+    chunk_rows = in_chunk * BS
+    base = 2 * max_rows + 2 * max_cols
+    n_rows, my_row, my_col = tab[base], tab[base + 2], tab[base + 3]
+    my_parity = lax.rem(my_col, 2)
+
+    @pl.when(step == 0)
+    def _():
+        @pl.loop(0, n_line * in_chunk)
+        def _(at):
+            k = slot_of(dims, my_col, my_parity, at)
+
+            @pl.when(k < n_rows)
+            def _():
+                start_fetch(dims, supernode, my_row, my_col, own, pieces, tab[k], rows_buf, at, rows_sem.at[at])
+
+            @pl.when(k >= n_rows)
+            def _():
+                clear_block(rows_buf, at)
+
+        diag[...] = jnp.zeros_like(diag)
+
+    left = n_rows - slot_of(dims, my_col, my_parity, step * in_chunk)
+
+    @pl.when(left > 0)
+    def _():
+        for item in range(in_chunk):
+
+            @pl.when(item < left)
+            def _(item=item):
+                wait_fetch(rows_buf, step * in_chunk + item, rows_sem.at[step * in_chunk + item])
+
+        sums = total[0]
+        high = sums.astype(jnp.bfloat16)
+        low = (sums - high.astype(jnp.float32)).astype(jnp.bfloat16)
+        rows = rows_buf[pl.ds(pl.multiple_of(step * chunk_rows, chunk_rows), chunk_rows), :].T
+        rows = jnp.concatenate([rows, rows], axis=1)
+        both = jnp.concatenate([high, low], axis=0)
+        diag[...] -= jnp.dot(rows, both, preferred_element_type=jnp.float32)
+
+    @pl.when(step == n_line - 1)
+    def _():
+        rows = sent.shape[0]
+        sent[...] = diag[pl.ds(pl.multiple_of((1 - my_parity) * rows, rows), rows), :]
+        kept[...] = diag[pl.ds(pl.multiple_of(my_parity * rows, rows), rows), :]
+
+
+def diag_terms(tab, total, own, pieces, dims, supernode):
+    n_line, chunk_rows, width = total.shape
+    any_spec = pl.BlockSpec(memory_space=pl.ANY)
+    operands = [*own, *pieces[0], *pieces[1]]
+    return pl.pallas_call(
+        functools.partial(diag_kernel, dims, supernode),
+        out_shape=(jax.ShapeDtypeStruct((width // 2, width), jnp.float32),) * 2,
+        grid_spec=pltpu.PrefetchScalarGridSpec(
+            num_scalar_prefetch=1,
+            grid=(n_line,),
+            in_specs=[pl.BlockSpec((1, chunk_rows, width), lambda g, tab: (g, 0, 0))] + [any_spec] * len(operands),
+            out_specs=[pl.BlockSpec((width // 2, width), lambda g, tab: (0, 0))] * 2,
+            scratch_shapes=[
+                pltpu.VMEM((width, width), jnp.float32),
+                pltpu.VMEM((n_line * chunk_rows, width), jnp.bfloat16),
+                pltpu.SemaphoreType.DMA((n_line * chunk_rows // BS,)),
+            ],
+        ),
+        cost_estimate=pl.CostEstimate(flops=3 * 10**9, bytes_accessed=7 * 10**6, transcendentals=0),
+        name="diag_terms",
+    )(tab, total, *operands)
+
+
+def join_kernel(total, far, out):
+    rows = total.shape[1]
+    body, tail = encode(total[0] + decode(far[0:rows, :], far[rows:, :]))
+    out[0:rows, :] = body
+    out[rows:, :] = tail
+
+
+def join_far(total, far):
+    _, chunk_rows, width = total.shape
+    coded = pl.BlockSpec(far.shape, lambda g: (0, 0))
+    return pl.pallas_call(
+        join_kernel,
+        out_shape=jax.ShapeDtypeStruct(far.shape, far.dtype),
+        grid=(1,),
+        in_specs=[pl.BlockSpec((1, chunk_rows, width), lambda g: (2, 0, 0)), coded],
+        out_specs=coded,
+        cost_estimate=pl.CostEstimate(flops=10**7, bytes_accessed=2 * 10**6, transcendentals=0),
+        name="join_far",
+    )(total, far)
+
+
 def final_kernel(count, first, *refs):
     out = refs[-1]
-    total = first[...]
+    total = first[0]
     for part in range(count):
         total = total + decode(refs[part][...], refs[count + part][...])
     out[0] = total
 
 
 def final_sums(supernodes, supernode, first, coded, earlier):
-    chunk_rows, width = first.shape
+    _, chunk_rows, width = first.shape
     rows = chunk_rows // 2
     tile = lambda: pl.BlockSpec((rows, width), lambda g: (g, 0))
     tail = lambda: pl.BlockSpec((TAIL, width), lambda g: (chunk_rows // TAIL, 0))
     operands = [first, *coded, *coded]
-    specs = [tile()] + [tile()] * len(coded) + [tail()] * len(coded)
+    specs = [pl.BlockSpec((1, rows, width), lambda g: (0, g, 0))] + [tile()] * len(coded) + [tail()] * len(coded)
     aliases = {}
     if earlier is not None:
         aliases = {len(operands): 0}
@@ -350,13 +467,16 @@
     return (my_row >> place) & 1
 
 
-def sum_over_all(part, n_row, n_col, my_row, my_parity):
+def sum_over_all(sent, kept, n_row, n_col, my_row, my_parity):
     bits = n_row.bit_length() - 1
     n_line = n_col // 2
-    part = half(part, my_parity) + lax.ppermute(half(part, 1 - my_parity), "col", core_swap(n_col))
+    got = lax.ppermute(sent, "col", core_swap(n_col))
     for step in range(bits):
         bit = row_bit(bits, step, my_row, my_parity)
-        part = half(part, bit) + lax.ppermute(half(part, 1 - bit), AXES, row_swap(n_row, n_col, step))
+        sent = half(kept, 1 - bit) + half(got, 1 - bit)
+        kept = half(kept, bit) + half(got, bit)
+        got = lax.ppermute(sent, AXES, row_swap(n_row, n_col, step))
+    part = kept + got
     got = [lax.ppermute(part, "col", line_shift(n_col, shift)) for shift in range(1, n_line)]
     whole = sum(got, part)
     for step in reversed(range(bits)):
@@ -364,6 +484,41 @@
         bit = row_bit(bits, step, my_row, my_parity)
         whole = jnp.where(bit == 0, jnp.concatenate([whole, other]), jnp.concatenate([other, whole]))
     return whole, lax.ppermute(whole, "col", core_swap(n_col))
+
+
+def place_kernel(parity, mine, other, *refs):
+    out = refs[-1]
+
+    @pl.when(pl.program_id(0) == parity[0])
+    def _():
+        out[0] = mine[...]
+
+    @pl.when(pl.program_id(0) != parity[0])
+    def _():
+        out[0] = other[...]
+
+
+def place_halves(supernodes, supernode, parity, mine, other, earlier):
+    rows, width = mine.shape
+    whole = pl.BlockSpec((rows, width), lambda g, parity: (0, 0))
+    operands, specs, aliases = [mine, other], [whole, whole], {}
+    if earlier is not None:
+        aliases = {3: 0}
+        operands.append(earlier)
+        specs.append(pl.BlockSpec(memory_space=pl.ANY))
+    return pl.pallas_call(
+        place_kernel,
+        out_shape=jax.ShapeDtypeStruct((supernodes, 2 * rows, width), jnp.float32),
+        grid_spec=pltpu.PrefetchScalarGridSpec(
+            num_scalar_prefetch=1,
+            grid=(2,),
+            in_specs=specs,
+            out_specs=pl.BlockSpec((1, rows, width), lambda g, parity: (supernode, g, 0)),
+        ),
+        input_output_aliases=aliases,
+        cost_estimate=pl.CostEstimate(flops=0, bytes_accessed=2 * 10**6, transcendentals=0),
+        name="place_halves",
+    )(parity, *operands)
 
 
 def local(inverse, panels, block_slot, list_ids):
@@ -415,21 +570,32 @@
         pieces = [line]
         for e in range(1, n_row):
             bit = e.bit_length() - 1
-            pieces.append(lax.ppermute(pieces[e ^ (1 << bit)], AXES, row_swap(n_row, n_col, bit)))
+            if s == 0:
+                source, pairs = pieces[e ^ (1 << bit)], row_swap(n_row, n_col, bit)
+            else:
+                source, pairs = line, row_jump(n_row, n_col, e)
+            pieces.append(lax.ppermute(source, AXES, pairs))
         other = [lax.ppermute(piece, "col", core_swap(n_col)) for piece in pieces]
         held.append((pieces, other))
     out = None
-    halves = []
+    diag = None
     for s in range(supernodes):
         packed = pack_strips(tables[s], inverse, dims)
         packed = lax.ppermute(packed, "col", core_swap(n_col))
-        first, diag, *coded = products(tables[s], inverse, packed, own, held[s], dims, s)
-        coded = [lax.ppermute(part, "col", line_shift(n_col, n_line - shift)) for shift, part in enumerate(coded, 1)]
-        halves.append(sum_over_all(diag, n_row, n_col, my_row, my_col % 2))
-        out = final_sums(supernodes, s, first, coded, out)
-    even = jnp.concatenate([part for mine, other in halves for part in (mine, other)])
-    odd = jnp.concatenate([part for mine, other in halves for part in (other, mine)])
-    return out, jnp.where(my_col % 2 == 0, even, odd).reshape(supernodes, width, width)
+        total, *coded = products(tables[s], inverse, packed, own, held[s], dims, s)
+        coded = dict(zip(coded_masks(n_line), coded))
+        if n_line == 4:
+            far = lax.ppermute(coded[3], "col", inward(n_col))
+            moved = [lax.ppermute(coded[3], "col", across(n_col)), lax.ppermute(coded[1], "col", line_swap(n_col, 1))]
+            joined = join_far(total, far)
+            moved.append(lax.ppermute(joined, "col", line_swap(n_col, 2)))
+        else:
+            moved = [lax.ppermute(part, "col", line_swap(n_col, mask)) for mask, part in coded.items()]
+        sent, kept = diag_terms(tables[s], total, own, held[s], dims, s)
+        mine, other = sum_over_all(sent, kept, n_row, n_col, my_row, my_col % 2)
+        diag = place_halves(supernodes, s, (my_col % 2).reshape(1), mine, other, diag)
+        out = final_sums(supernodes, s, total, moved, out)
+    return out, diag
 
 
 def solution(mesh):

time: 331 us -> 328 us (level)
  the two profiles are of different devices: /device:TPU:25 before, /device:TPU:0 now
where the time goes in v2:
time: 328 us; the launch traced here: 327 us
  waiting for transfers between devices  158 us (48%)
  Pallas kernels  96.1 us (29%)
  starting transfers between devices  56.9 us (17%)
  local copies, waits for them, and re-layouts  8.86 us (3%)
  other arithmetic  5.75 us (2%)
    ppermute x6, waiting for transfers between devices, local(): pieces.append(lax.ppermute(source, AXES, pairs))  49.3 us
    pallas_call x2, Pallas kernels, products(): pl.pallas_call(functools.partial(product_kernel, dims, supernode), out_sh...  44 us
    ppermute x2, waiting for transfers between devices, local(): moved.append(lax.ppermute(joined, 'col', line_swap(n_col, 2)))  35.9 us
    ppermute x6, waiting for transfers between devices, local(): lax.ppermute(mine, 'col', line_shift(n_col, shift))  35 us
    ppermute x6, waiting for transfers between devices, sum_over_all(): lax.ppermute(part, 'col', line_shift(n_col, shift))  25.3 us
    pallas_call x2, Pallas kernels, pack_strips(): pl.pallas_call(functools.partial(pack_kernel, dims), out_shape=jax.ShapeD...  21.2 us
    ppermute x6, starting transfers between devices, local(): lax.ppermute(mine, 'col', line_shift(n_col, shift))  18.1 us
    pallas_call x2, Pallas kernels, diag_terms(): pl.pallas_call(functools.partial(diag_kernel, dims, supernode), out_shape...  15.8 us
  transfers between devices with their start and end apart: 49, of which 19 were waited for; matrix products, arithmetic and copies ran while one was open for 2% of the time, Pallas kernels for 26%

profile of v2, /device:TPU:0, one launch (start us, length us, event | category | flops | bytes accessed | tf_op | source)
XLA Modules:
  0.0 326.9 jit_solution(9174030892515659599)
XLA Ops:
  0.7 0.9 select_reduce_fusion
  2.8 0.6 fusion.4
  3.4 10.5 %pack_strips.3 = bf16[2048,3328]{1,0:T(8,128)(2,1)} custom-call(s32[132]{0:T(256)} %bitcast.27, bf16[6656,3328]{1,0:T(8,128)(2,1)} %inverse.7), custom_call_target="tpu_custom_call" | custom-call | bytes 27000000 | tf_op jit(solution)/shard_map/pack_strips/pallas_call | solution.py:162
  13.9 0.6 collective-permute-start.16
  14.4 10.7 %pack_strips.2 = bf16[2048,3328]{1,0:T(8,128)(2,1)} custom-call(s32[132]{0:T(256)} %bitcast.24, bf16[6656,3328]{1,0:T(8,128)(2,1)} %inverse.7), custom_call_target="tpu_custom_call" | custom-call | bytes 27000000 | tf_op jit(solution)/shard_map/pack_strips/pallas_call | solution.py:162
  25.3 5.1 %collective-permute-start.17 = (bf16[8,32,512]{2,1,0:T(8,128)(2,1)S(1)}, bf16[8,32,512]{2,1,0:T(8,128)(2,1)S(1)}, u32[]{:S(2)}, u32[]{:S(2)}) collective-permute-start(bf16[8,32,512]{2,1,0:T(8,128)(2,1)S(1)} %get-tuple-element.29), channel_id=1, source_target_pairs={{2,0},{3,1},{4,2},{5,3},{6,4},{7,5},{0,6},{1,7},{10,8},{11,9},{12,... | collective-permute-start | bytes 786440 | tf_op jit(solution)/shard_map/ppermute | solution.py:568
  30.4 1.0 collective-permute-start.19
  31.4 5.8 %collective-permute-done.17 = bf16[8,32,512]{2,1,0:T(8,128)(2,1)S(1)} collective-permute-done((bf16[8,32,512]{2,1,0:T(8,128)(2,1)S(1)}, bf16[8,32,512]{2,1,0:T(8,128)(2,1)S(1)}, u32[]{:S(2)}, u32[]{:S(2)}) %collective-permute-start.17) | collective-permute-done | bytes 262176 | tf_op jit(solution)/shard_map/ppermute | solution.py:568
  37.1 4.3 %collective-permute-start.2 = (bf16[8,32,512]{2,1,0:T(8,128)(2,1)S(1)}, bf16[8,32,512]{2,1,0:T(8,128)(2,1)S(1)}, u32[]{:S(2)}, u32[]{:S(2)}) collective-permute-start(bf16[8,32,512]{2,1,0:T(8,128)(2,1)S(1)} %get-tuple-element.30), channel_id=1, source_target_pairs={{2,0},{3,1},{4,2},{5,3},{6,4},{7,5},{0,6},{1,7},{10,8},{11,9},{12,... | collective-permute-start | bytes 786440 | tf_op jit(solution)/shard_map/ppermute | solution.py:568
  41.5 12.3 %collective-permute-done.18 = bf16[8,32,512]{2,1,0:T(8,128)(2,1)S(1)} collective-permute-done((bf16[8,32,512]{2,1,0:T(8,128)(2,1)S(1)}, bf16[8,32,512]{2,1,0:T(8,128)(2,1)S(1)}, u32[]{:S(2)}, u32[]{:S(2)}) %collective-permute-start.18) | collective-permute-done | bytes 262176 | tf_op jit(solution)/shard_map/ppermute | solution.py:568
  54.0 7.6 %collective-permute-start.3 = (bf16[8,32,512]{2,1,0:T(8,128)(2,1)S(1)}, bf16[8,32,512]{2,1,0:T(8,128)(2,1)S(1)}, u32[]{:S(2)}, u32[]{:S(2)}) collective-permute-start(bf16[8,32,512]{2,1,0:T(8,128)(2,1)S(1)} %get-tuple-element.30), channel_id=1, source_target_pairs={{4,0},{5,1},{6,2},{7,3},{0,4},{1,5},{2,6},{3,7},{12,8},{13,9},{14,... | collective-permute-start | bytes 786440 | tf_op jit(solution)/shard_map/ppermute | solution.py:568
  61.6 16.8 %collective-permute-done.3 = bf16[8,32,512]{2,1,0:T(8,128)(2,1)S(1)} collective-permute-done((bf16[8,32,512]{2,1,0:T(8,128)(2,1)S(1)}, bf16[8,32,512]{2,1,0:T(8,128)(2,1)S(1)}, u32[]{:S(2)}, u32[]{:S(2)}) %collective-permute-start.3) | collective-permute-done | bytes 262176 | tf_op jit(solution)/shard_map/ppermute | solution.py:568
  78.5 0.7 constant_dynamic-update-slice_fusion.2
  79.2 0.7 constant_dynamic-update-slice_fusion.1
  79.9 0.7 constant_dynamic-update-slice_fusion.refs_2_
  80.6 2.0 collective-permute-start.6
  82.7 7.8 %collective-permute-done.21.refs_4_ = bf16[24,32,512]{2,1,0:T(8,128)(2,1)S(1)} collective-permute-done((bf16[24,32,512]{2,1,0:T(8,128)(2,1)S(1)}, bf16[24,32,512]{2,1,0:T(8,128)(2,1)S(1)}, u32[]{:S(2)}, u32[]{:S(2)}) %collective-permute-start.21) | collective-permute-done | bytes 786464 | tf_op jit(solution)/shard_map/ppermute | solution.py:577
  90.5 1.5 collective-permute-start.5
  91.9 30.4 %collective-permute-done.6.refs_4_ = bf16[24,32,512]{2,1,0:T(8,128)(2,1)} collective-permute-done((bf16[24,32,512]{2,1,0:T(8,128)(2,1)}, bf16[24,32,512]{2,1,0:T(8,128)(2,1)}, u32[]{:S(2)}, u32[]{:S(2)}) %collective-permute-start.6) | collective-permute-done | bytes 786464 | tf_op jit(solution)/shard_map/ppermute | solution.py:577
  122.4 0.8 collective-permute-done.5.refs_3_
  123.2 0.9 collective-permute-start.24
  124.1 10.3 %collective-permute-done.22.refs_5_ = bf16[24,32,512]{2,1,0:T(8,128)(2,1)S(1)} collective-permute-done((bf16[24,32,512]{2,1,0:T(8,128)(2,1)S(1)}, bf16[24,32,512]{2,1,0:T(8,128)(2,1)S(1)}, u32[]{:S(2)}, u32[]{:S(2)}) %collective-permute-start.22) | collective-permute-done | bytes 786464 | tf_op jit(solution)/shard_map/ppermute | solution.py:577
  134.9 1.8 collective-permute-done.25.refs_8_
  136.8 1.4 copy-done.1
  138.9 0.6 copy-done.11
  139.7 21.9 %products.3 = (f32[4,512,512]{2,1,0:T(8,128)}, s16[528,512]{1,0:T(8,128)(2,1)}, s16[528,512]{1,0:T(8,128)(2,1)}) custom-call(s32[132]{0:T(256)} %bitcast.28, bf16[6656,3328]{1,0:T(8,128)(2,1)} %inverse.7, bf16[2048,3328]{1,0:T(8,128)(2,1)} %collective-permute-done.16.packed, bf16[16,128,512]{2,1,0:T(8,128)(2,1)} %bitcast.18, ...), custom_call_target="tpu_custom_call" | custom-call | flops 10000000000 | bytes 30000000 | tf_op jit(solution)/shard_map/products/pallas_call | solution.py:308
  161.6 7.8 %diag_terms.3 = (f32[256,512]{1,0:T(8,128)}, f32[256,512]{1,0:T(8,128)}) custom-call(s32[132]{0:T(256)} %bitcast.29, f32[4,512,512]{2,1,0:T(8,128)} %get-tuple-element.15.total.first, bf16[16,128,512]{2,1,0:T(8,128)(2,1)} %bitcast.19, bf16[16,128,512]{2,1,0:T(8,128)(2,1)} %copy-done.1, bf16[24,32,512]{2,1,0:T(8,128)(2,1)} %copy-done.2, ...), custom_call_target="tpu_custom_call" | custom-call | flops 3000000000 | bytes 7000000 | tf_op jit(solution)/shard_map/diag_terms/pallas_call | solution.py:388
  169.8 0.9 copy-done.6
  171.0 22.0 %products.2 = (f32[4,512,512]{2,1,0:T(8,128)}, s16[528,512]{1,0:T(8,128)(2,1)}, s16[528,512]{1,0:T(8,128)(2,1)}) custom-call(s32[132]{0:T(256)} %bitcast.25, bf16[6656,3328]{1,0:T(8,128)(2,1)} %inverse.7, bf16[2048,3328]{1,0:T(8,128)(2,1)} %collective-permute-done.packed, bf16[16,128,512]{2,1,0:T(8,128)(2,1)} %bitcast.20, bf16[16,128,512]{2,1,0:T(8,128)(2,1)} %copy-done.1, ...), custom_call_target="tpu_custom_call" | custom-call | flops 10000000000 | bytes 30000000 | tf_op jit(solution)/shard_map/products/pallas_call | solution.py:308
  193.0 8.0 %diag_terms.2 = (f32[256,512]{1,0:T(8,128)}, f32[256,512]{1,0:T(8,128)}) custom-call(s32[132]{0:T(256)} %bitcast.26, f32[4,512,512]{2,1,0:T(8,128)} %get-tuple-element.12.total.first, bf16[16,128,512]{2,1,0:T(8,128)(2,1)} %bitcast.21, bf16[16,128,512]{2,1,0:T(8,128)(2,1)} %copy-done.1, bf16[24,32,512]{2,1,0:T(8,128)(2,1)} %constant_dynamic-update-slice_fusion.refs_2_, ...), custom_call_target="tpu_custom_call" | custom-call | flops 3000000000 | bytes 7000000 | tf_op jit(solution)/shard_map/diag_terms/pallas_call | solution.py:388
  201.5 1.6 collective-permute-done.31
  203.1 1.1 dynamic-slice_add_fusion.3
  204.7 3.2 collective-permute-done.41
  208.0 1.3 collective-permute-start.29
  209.3 1.3 collective-permute-start.14
  210.6 0.9 collective-permute-done.32
  211.5 1.2 collective-permute-start.33
  213.1 3.5 %collective-permute-done.33 = f32[64,512]{1,0:T(8,128)S(1)} collective-permute-done((f32[64,512]{1,0:T(8,128)S(1)}, f32[64,512]{1,0:T(8,128)S(1)}, u32[]{:S(2)}, u32[]{:S(2)}) %collective-permute-start.33) | collective-permute-done | bytes 131104 | tf_op jit(solution)/shard_map/ppermute | solution.py:478
  216.6 19.9 %collective-permute-done.43 = f32[64,512]{1,0:T(8,128)S(1)} collective-permute-done((f32[64,512]{1,0:T(8,128)S(1)}, f32[64,512]{1,0:T(8,128)S(1)}, u32[]{:S(2)}, u32[]{:S(2)}) %collective-permute-start.43) | collective-permute-done | bytes 131104 | tf_op jit(solution)/shard_map/ppermute | solution.py:480
  236.5 4.3 %collective-permute-start.34 = (f32[64,512]{1,0:T(8,128)S(1)}, f32[64,512]{1,0:T(8,128)S(1)}, u32[]{:S(2)}, u32[]{:S(2)}) collective-permute-start(f32[64,512]{1,0:T(8,128)S(1)} %add_add_fusion.3), channel_id=1, source_target_pairs={{2,0},{3,1},{4,2},{5,3},{6,4},{7,5},{0,6},{1,7},{10,8},{11,9},{12,... | collective-permute-start | bytes 393224 | tf_op jit(solution)/shard_map/ppermute | solution.py:480
  240.8 1.9 collective-permute-start.35
  242.7 1.9 collective-permute-start.36
  245.0 0.7 collective-permute-start.27
  245.7 5.0 %collective-permute-done.35 = f32[64,512]{1,0:T(8,128)S(1)} collective-permute-done((f32[64,512]{1,0:T(8,128)S(1)}, f32[64,512]{1,0:T(8,128)S(1)}, u32[]{:S(2)}, u32[]{:S(2)}) %collective-permute-start.35) | collective-permute-done | bytes 131104 | tf_op jit(solution)/shard_map/ppermute | solution.py:480
  250.7 2.3 collective-permute-start.46
  253.1 0.7 copy-done.19
  253.8 2.6 join_far.3
  256.5 3.3 %collective-permute-start.30 = (s16[528,512]{1,0:T(8,128)(2,1)}, s16[528,512]{1,0:T(8,128)(2,1)S(1)}, u32[]{:S(2)}, u32[]{:S(2)}) collective-permute-start(s16[528,512]{1,0:T(8,128)(2,1)} %join_far.3), channel_id=1, source_target_pairs={{4,0},{5,1},{6,2},{7,3},{0,4},{1,5},{2,6},{3,7},{12,8},{13,9},{14,... | collective-permute-start | bytes 1622024 | tf_op jit(solution)/shard_map/ppermute | solution.py:591
  260.4 1.6 collective-permute-start.38
  262.0 2.6 join_far.2
  264.7 1.6 collective-permute-done.47
  266.3 0.7 collective-permute-start.12
  267.0 0.9 maximum_select_fusion.1.mine
  267.8 7.3 %collective-permute-start.13 = (s16[528,512]{1,0:T(8,128)(2,1)}, s16[528,512]{1,0:T(8,128)(2,1)S(1)}, u32[]{:S(2)}, u32[]{:S(2)}) collective-permute-start(s16[528,512]{1,0:T(8,128)(2,1)} %get-tuple-element.14), channel_id=1, source_target_pairs={{2,0},{3,1},{0,2},{1,3},{6,4},{7,5},{4,6},{5,7},{10,8},{11,9},{8,1... | collective-permute-start | bytes 1622024 | tf_op jit(solution)/shard_map/ppermute | solution.py:589
  275.1 2.4 collective-permute-start.15
  277.5 1.9 maximum_select_fusion.mine
  279.4 11.8 %collective-permute-done.30.refs_2_.refs_5_ = s16[528,512]{1,0:T(8,128)(2,1)S(1)} collective-permute-done((s16[528,512]{1,0:T(8,128)(2,1)}, s16[528,512]{1,0:T(8,128)(2,1)S(1)}, u32[]{:S(2)}, u32[]{:S(2)}) %collective-permute-start.30) | collective-permute-done | bytes 540704 | tf_op jit(solution)/shard_map/ppermute | solution.py:591
  291.3 0.8 copy-done.14
  292.1 2.7 final_sums.2.refs_6_
  294.8 24.1 %collective-permute-done.15.refs_2_.refs_5_ = s16[528,512]{1,0:T(8,128)(2,1)S(1)} collective-permute-done((s16[528,512]{1,0:T(8,128)(2,1)}, s16[528,512]{1,0:T(8,128)(2,1)S(1)}, u32[]{:S(2)}, u32[]{:S(2)}) %collective-permute-start.15) | collective-permute-done | bytes 540704 | tf_op jit(solution)/shard_map/ppermute | solution.py:591
  318.9 0.8 copy-done.17
  319.7 2.7 final_sums.3
  322.5 2.2 place_halves.2.refs_0_
  324.7 2.2 place_halves.3
  (128 shorter events, 6.1 us)
Async XLA Ops:
  13.9 125.0 %collective-permute-start.16 = (bf16[2048,3328]{1,0:T(8,128)(2,1)}, bf16[2048,3328]{1,0:T(8,128)(2,1)}, u32[]{:S(2)}, u32[]{:S(2)}) collective-permute-start(bf16[2048,3328]{1,0:T(8,128)(2,1)} %pack_strips.3), channel_id=1, source_target_pairs={{1,0},{0,1},{3,2},{2,3},{5,4},{4,5},{7,6},{6,7},{9,8},{8,9},{11,10... | collective-permute-start | bytes 40894472 | tf_op jit(solution)/shard_map/ppermute | solution.py:584
  14.4 10.8 %copy-start = (bf16[2,1024,512]{2,1,0:T(8,128)(2,1)S(1)}, bf16[2,1024,512]{2,1,0:T(8,128)(2,1)}, u32[]{:S(2)}) copy-start(bf16[2,1024,512]{2,1,0:T(8,128)(2,1)} %param.5) | copy-start | bytes 6291460
  25.1 144.7 %collective-permute-start = (bf16[2048,3328]{1,0:T(8,128)(2,1)}, bf16[2048,3328]{1,0:T(8,128)(2,1)}, u32[]{:S(2)}, u32[]{:S(2)}) collective-permute-start(bf16[2048,3328]{1,0:T(8,128)(2,1)} %pack_strips.2), channel_id=1, source_target_pairs={{1,0},{0,1},{3,2},{2,3},{5,4},{4,5},{7,6},{6,7},{9,8},{8,9},{11,10... | collective-permute-start | bytes 40894472 | tf_op jit(solution)/shard_map/ppermute | solution.py:584
  25.3 11.9 %collective-permute-start.17 = (bf16[8,32,512]{2,1,0:T(8,128)(2,1)S(1)}, bf16[8,32,512]{2,1,0:T(8,128)(2,1)S(1)}, u32[]{:S(2)}, u32[]{:S(2)}) collective-permute-start(bf16[8,32,512]{2,1,0:T(8,128)(2,1)S(1)} %get-tuple-element.29), channel_id=1, source_target_pairs={{2,0},{3,1},{4,2},{5,3},{6,4},{7,5},{0,6},{1,7},{10,8},{11,9},{12,... | collective-permute-start | bytes 786440 | tf_op jit(solution)/shard_map/ppermute | solution.py:568
  30.4 23.5 %collective-permute-start.18 = (bf16[8,32,512]{2,1,0:T(8,128)(2,1)S(1)}, bf16[8,32,512]{2,1,0:T(8,128)(2,1)S(1)}, u32[]{:S(2)}, u32[]{:S(2)}) collective-permute-start(bf16[8,32,512]{2,1,0:T(8,128)(2,1)S(1)} %get-tuple-element.29), channel_id=1, source_target_pairs={{4,0},{5,1},{6,2},{7,3},{0,4},{1,5},{2,6},{3,7},{12,8},{13,9},{14,... | collective-permute-start | bytes 786440 | tf_op jit(solution)/shard_map/ppermute | solution.py:568
  30.4 23.5 %collective-permute-start.19 = (bf16[8,32,512]{2,1,0:T(8,128)(2,1)S(1)}, bf16[8,32,512]{2,1,0:T(8,128)(2,1)S(1)}, u32[]{:S(2)}, u32[]{:S(2)}) collective-permute-start(bf16[8,32,512]{2,1,0:T(8,128)(2,1)S(1)} %get-tuple-element.29), channel_id=1, source_target_pairs={{6,0},{7,1},{0,2},{1,3},{2,4},{3,5},{4,6},{5,7},{14,8},{15,9},{8,1... | collective-permute-start | bytes 786440 | tf_op jit(solution)/shard_map/ppermute | solution.py:568
  37.1 24.5 %collective-permute-start.2 = (bf16[8,32,512]{2,1,0:T(8,128)(2,1)S(1)}, bf16[8,32,512]{2,1,0:T(8,128)(2,1)S(1)}, u32[]{:S(2)}, u32[]{:S(2)}) collective-permute-start(bf16[8,32,512]{2,1,0:T(8,128)(2,1)S(1)} %get-tuple-element.30), channel_id=1, source_target_pairs={{2,0},{3,1},{4,2},{5,3},{6,4},{7,5},{0,6},{1,7},{10,8},{11,9},{12,... | collective-permute-start | bytes 786440 | tf_op jit(solution)/shard_map/ppermute | solution.py:568
  53.9 85.8 %copy-start.2 = (bf16[24,32,512]{2,1,0:T(8,128)(2,1)}, bf16[24,32,512]{2,1,0:T(8,128)(2,1)S(1)}, u32[]{:S(2)}) copy-start(bf16[24,32,512]{2,1,0:T(8,128)(2,1)S(1)} %constant_dynamic-update-slice_fusion.3.refs_2_) | copy-start | bytes 2359300
  53.9 26.7 %collective-permute-start.20 = (bf16[24,32,512]{2,1,0:T(8,128)(2,1)S(1)}, bf16[24,32,512]{2,1,0:T(8,128)(2,1)S(1)}, u32[]{:S(2)}, u32[]{:S(2)}) collective-permute-start(bf16[24,32,512]{2,1,0:T(8,128)(2,1)S(1)} %constant_dynamic-update-slice_fusion.3.refs_2_), channel_id=1, source_target_pairs={{8,0},{17,1},{10,2},{19,3},{12,4},{21,5},{14,6},{23,7},{0,8},{25,9... | collective-permute-start | bytes 2359304 | tf_op jit(solution)/shard_map/ppermute | solution.py:577
  54.0 24.5 %collective-permute-start.3 = (bf16[8,32,512]{2,1,0:T(8,128)(2,1)S(1)}, bf16[8,32,512]{2,1,0:T(8,128)(2,1)S(1)}, u32[]{:S(2)}, u32[]{:S(2)}) collective-permute-start(bf16[8,32,512]{2,1,0:T(8,128)(2,1)S(1)} %get-tuple-element.30), channel_id=1, source_target_pairs={{4,0},{5,1},{6,2},{7,3},{0,4},{1,5},{2,6},{3,7},{12,8},{13,9},{14,... | collective-permute-start | bytes 786440 | tf_op jit(solution)/shard_map/ppermute | solution.py:568
  61.6 16.9 %collective-permute-start.4 = (bf16[8,32,512]{2,1,0:T(8,128)(2,1)S(1)}, bf16[8,32,512]{2,1,0:T(8,128)(2,1)S(1)}, u32[]{:S(2)}, u32[]{:S(2)}) collective-permute-start(bf16[8,32,512]{2,1,0:T(8,128)(2,1)S(1)} %get-tuple-element.30), channel_id=1, source_target_pairs={{6,0},{7,1},{0,2},{1,3},{2,4},{3,5},{4,6},{5,7},{14,8},{15,9},{8,1... | collective-permute-start | bytes 786440 | tf_op jit(solution)/shard_map/ppermute | solution.py:568
  78.5 12.0 %collective-permute-start.21 = (bf16[24,32,512]{2,1,0:T(8,128)(2,1)S(1)}, bf16[24,32,512]{2,1,0:T(8,128)(2,1)S(1)}, u32[]{:S(2)}, u32[]{:S(2)}) collective-permute-start(bf16[24,32,512]{2,1,0:T(8,128)(2,1)S(1)} %constant_dynamic-update-slice_fusion.3.refs_2_), channel_id=1, source_target_pairs={{16,0},{9,1},{18,2},{11,3},{20,4},{13,5},{22,6},{15,7},{24,8},{1,9... | collective-permute-start | bytes 2359304 | tf_op jit(solution)/shard_map/ppermute | solution.py:577
  78.5 12.0 %collective-permute-start.23 = (bf16[24,32,512]{2,1,0:T(8,128)(2,1)S(1)}, bf16[24,32,512]{2,1,0:T(8,128)(2,1)S(1)}, u32[]{:S(2)}, u32[]{:S(2)}) collective-permute-start(bf16[24,32,512]{2,1,0:T(8,128)(2,1)S(1)} %constant_dynamic-update-slice_fusion.3.refs_2_), channel_id=1, source_target_pairs={{1,0},{0,1},{3,2},{2,3},{5,4},{4,5},{7,6},{6,7},{9,8},{8,9},{11,10... | collective-permute-start | bytes 2359304 | tf_op jit(solution)/shard_map/ppermute | solution.py:578
  80.6 57.8 %copy-start.3 = (bf16[24,32,512]{2,1,0:T(8,128)(2,1)}, bf16[24,32,512]{2,1,0:T(8,128)(2,1)S(1)}, u32[]{:S(2)}) copy-start(bf16[24,32,512]{2,1,0:T(8,128)(2,1)S(1)} %collective-permute-done.20.refs_3_) | copy-start | bytes 2359300
  80.6 41.7 %collective-permute-start.6 = (bf16[24,32,512]{2,1,0:T(8,128)(2,1)}, bf16[24,32,512]{2,1,0:T(8,128)(2,1)}, u32[]{:S(2)}, u32[]{:S(2)}) collective-permute-start(bf16[24,32,512]{2,1,0:T(8,128)(2,1)} %constant_dynamic-update-slice_fusion.refs_2_), channel_id=1, source_target_pairs={{16,0},{9,1},{18,2},{11,3},{20,4},{13,5},{22,6},{15,7},{24,8},{1,9... | collective-permute-start | bytes 2359304 | tf_op jit(solution)/shard_map/ppermute | solution.py:577
  90.5 48.0 %copy-start.4 = (bf16[24,32,512]{2,1,0:T(8,128)(2,1)}, bf16[24,32,512]{2,1,0:T(8,128)(2,1)S(1)}, u32[]{:S(2)}) copy-start(bf16[24,32,512]{2,1,0:T(8,128)(2,1)S(1)} %collective-permute-done.21.refs_4_) | copy-start | bytes 2359300
  90.5 31.9 %collective-permute-start.7 = (bf16[24,32,512]{2,1,0:T(8,128)(2,1)}, bf16[24,32,512]{2,1,0:T(8,128)(2,1)}, u32[]{:S(2)}, u32[]{:S(2)}) collective-permute-start(bf16[24,32,512]{2,1,0:T(8,128)(2,1)} %constant_dynamic-update-slice_fusion.refs_2_), channel_id=1, source_target_pairs={{24,0},{25,1},{26,2},{27,3},{28,4},{29,5},{30,6},{31,7},{16,8},{17... | collective-permute-start | bytes 2359304 | tf_op jit(solution)/shard_map/ppermute | solution.py:577
  90.5 48.4 %copy-start.5 = (bf16[24,32,512]{2,1,0:T(8,128)(2,1)}, bf16[24,32,512]{2,1,0:T(8,128)(2,1)S(1)}, u32[]{:S(2)}) copy-start(bf16[24,32,512]{2,1,0:T(8,128)(2,1)S(1)} %collective-permute-done.23.refs_6_) | copy-start | bytes 2359300
  90.5 32.7 %collective-permute-start.5 = (bf16[24,32,512]{2,1,0:T(8,128)(2,1)}, bf16[24,32,512]{2,1,0:T(8,128)(2,1)}, u32[]{:S(2)}, u32[]{:S(2)}) collective-permute-start(bf16[24,32,512]{2,1,0:T(8,128)(2,1)} %constant_dynamic-update-slice_fusion.refs_2_), channel_id=1, source_target_pairs={{8,0},{17,1},{10,2},{19,3},{12,4},{21,5},{14,6},{23,7},{0,8},{25,9... | collective-permute-start | bytes 2359304 | tf_op jit(solution)/shard_map/ppermute | solution.py:577
  122.4 14.4 %collective-permute-start.1 = (bf16[16,128,512]{2,1,0:T(8,128)(2,1)S(1)}, bf16[16,128,512]{2,1,0:T(8,128)(2,1)S(1)}, u32[]{:S(2)}, u32[]{:S(2)}) collective-permute-start(bf16[16,128,512]{2,1,0:T(8,128)(2,1)S(1)} %bitcast.23), channel_id=1, source_target_pairs={{1,0},{0,1},{3,2},{2,3},{5,4},{4,5},{7,6},{6,7},{9,8},{8,9},{11,10... | collective-permute-start | bytes 6291464 | tf_op jit(solution)/shard_map/ppermute | solution.py:560
  122.4 12.0 %collective-permute-start.22 = (bf16[24,32,512]{2,1,0:T(8,128)(2,1)S(1)}, bf16[24,32,512]{2,1,0:T(8,128)(2,1)S(1)}, u32[]{:S(2)}, u32[]{:S(2)}) collective-permute-start(bf16[24,32,512]{2,1,0:T(8,128)(2,1)S(1)} %collective-permute-done.20.refs_3_), channel_id=1, source_target_pairs={{16,0},{9,1},{18,2},{11,3},{20,4},{13,5},{22,6},{15,7},{24,8},{1,9... | collective-permute-start | bytes 2359304 | tf_op jit(solution)/shard_map/ppermute | solution.py:577
  123.2 11.2 %collective-permute-start.24 = (bf16[24,32,512]{2,1,0:T(8,128)(2,1)S(1)}, bf16[24,32,512]{2,1,0:T(8,128)(2,1)S(1)}, u32[]{:S(2)}, u32[]{:S(2)}) collective-permute-start(bf16[24,32,512]{2,1,0:T(8,128)(2,1)S(1)} %collective-permute-done.20.refs_3_), channel_id=1, source_target_pairs={{1,0},{0,1},{3,2},{2,3},{5,4},{4,5},{7,6},{6,7},{9,8},{8,9},{11,10... | collective-permute-start | bytes 2359304 | tf_op jit(solution)/shard_map/ppermute | solution.py:578
  134.4 4.5 %copy-start.7 = (bf16[24,32,512]{2,1,0:T(8,128)(2,1)}, bf16[24,32,512]{2,1,0:T(8,128)(2,1)S(1)}, u32[]{:S(2)}) copy-start(bf16[24,32,512]{2,1,0:T(8,128)(2,1)S(1)} %collective-permute-done.22.refs_5_) | copy-start | bytes 2359300
  134.4 2.3 collective-permute-start.25
  134.4 4.5 %copy-start.9 = (bf16[24,32,512]{2,1,0:T(8,128)(2,1)}, bf16[24,32,512]{2,1,0:T(8,128)(2,1)S(1)}, u32[]{:S(2)}) copy-start(bf16[24,32,512]{2,1,0:T(8,128)(2,1)S(1)} %collective-permute-done.24.refs_7_) | copy-start | bytes 2359300
  134.4 4.1 %collective-permute-start.26 = (bf16[24,32,512]{2,1,0:T(8,128)(2,1)S(1)}, bf16[24,32,512]{2,1,0:T(8,128)(2,1)S(1)}, u32[]{:S(2)}, u32[]{:S(2)}) collective-permute-start(bf16[24,32,512]{2,1,0:T(8,128)(2,1)S(1)} %collective-permute-done.22.refs_5_), channel_id=1, source_target_pairs={{1,0},{0,1},{3,2},{2,3},{5,4},{4,5},{7,6},{6,7},{9,8},{8,9},{11,10... | collective-permute-start | bytes 2359304 | tf_op jit(solution)/shard_map/ppermute | solution.py:578
  136.7 2.2 copy-start.10
  136.7 32.8 %collective-permute-start.8 = (bf16[24,32,512]{2,1,0:T(8,128)(2,1)}, bf16[24,32,512]{2,1,0:T(8,128)(2,1)}, u32[]{:S(2)}, u32[]{:S(2)}) collective-permute-start(bf16[24,32,512]{2,1,0:T(8,128)(2,1)} %constant_dynamic-update-slice_fusion.refs_2_), channel_id=1, source_target_pairs={{1,0},{0,1},{3,2},{2,3},{5,4},{4,5},{7,6},{6,7},{9,8},{8,9},{11,10... | collective-permute-start | bytes 2359304 | tf_op jit(solution)/shard_map/ppermute | solution.py:578
  136.8 1.4 copy-start.1
  138.2 31.5 %collective-permute-start.10 = (bf16[24,32,512]{2,1,0:T(8,128)(2,1)}, bf16[24,32,512]{2,1,0:T(8,128)(2,1)S(1)}, u32[]{:S(2)}, u32[]{:S(2)}) collective-permute-start(bf16[24,32,512]{2,1,0:T(8,128)(2,1)} %collective-permute-done.6.refs_4_), channel_id=1, source_target_pairs={{1,0},{0,1},{3,2},{2,3},{5,4},{4,5},{7,6},{6,7},{9,8},{8,9},{11,10... | collective-permute-start | bytes 2359304 | tf_op jit(solution)/shard_map/ppermute | solution.py:578
  138.5 31.2 %collective-permute-start.11 = (bf16[24,32,512]{2,1,0:T(8,128)(2,1)}, bf16[24,32,512]{2,1,0:T(8,128)(2,1)S(1)}, u32[]{:S(2)}, u32[]{:S(2)}) collective-permute-start(bf16[24,32,512]{2,1,0:T(8,128)(2,1)} %collective-permute-done.7.refs_5_), channel_id=1, source_target_pairs={{1,0},{0,1},{3,2},{2,3},{5,4},{4,5},{7,6},{6,7},{9,8},{8,9},{11,10... | collective-permute-start | bytes 2359304 | tf_op jit(solution)/shard_map/ppermute | solution.py:578
  139.4 30.3 %collective-permute-start.9 = (bf16[24,32,512]{2,1,0:T(8,128)(2,1)}, bf16[24,32,512]{2,1,0:T(8,128)(2,1)}, u32[]{:S(2)}, u32[]{:S(2)}) collective-permute-start(bf16[24,32,512]{2,1,0:T(8,128)(2,1)} %collective-permute-done.5.refs_3_), channel_id=1, source_target_pairs={{1,0},{0,1},{3,2},{2,3},{5,4},{4,5},{7,6},{6,7},{9,8},{8,9},{11,10... | collective-permute-start | bytes 2359304 | tf_op jit(solution)/shard_map/ppermute | solution.py:578
  169.5 31.9 %collective-permute-start.40 = (f32[256,512]{1,0:T(8,128)}, f32[256,512]{1,0:T(8,128)S(1)}, u32[]{:S(2)}, u32[]{:S(2)}) collective-permute-start(f32[256,512]{1,0:T(8,128)} %get-tuple-element.21), channel_id=1, source_target_pairs={{1,0},{0,1},{3,2},{2,3},{5,4},{4,5},{7,6},{6,7},{9,8},{8,9},{11,10... | collective-permute-start | bytes 1572872 | tf_op jit(solution)/shard_map/ppermute | solution.py:473
  193.0 8.4 %copy-start.20 = (f32[256,512]{1,0:T(8,128)S(1)}, f32[256,512]{1,0:T(8,128)}, u32[]{:S(2)}) copy-start(f32[256,512]{1,0:T(8,128)} %get-tuple-element.20) | copy-start | bytes 1572868
  201.0 2.2 collective-permute-start.31
  201.4 6.4 %collective-permute-start.41 = (f32[128,512]{1,0:T(8,128)S(1)}, f32[128,512]{1,0:T(8,128)S(1)}, u32[]{:S(2)}, u32[]{:S(2)}) collective-permute-start(f32[128,512]{1,0:T(8,128)S(1)} %get-tuple-element.32), channel_id=1, source_target_pairs={{8,0},{17,1},{10,2},{19,3},{12,4},{21,5},{14,6},{23,7},{0,8},{25,9... | collective-permute-start | bytes 786440 | tf_op jit(solution)/shard_map/ppermute | solution.py:478
  204.3 7.2 %collective-permute-start.32 = (f32[128,512]{1,0:T(8,128)S(1)}, f32[128,512]{1,0:T(8,128)S(1)}, u32[]{:S(2)}, u32[]{:S(2)}) collective-permute-start(f32[128,512]{1,0:T(8,128)S(1)} %get-tuple-element.34), channel_id=1, source_target_pairs={{8,0},{17,1},{10,2},{19,3},{12,4},{21,5},{14,6},{23,7},{0,8},{25,9... | collective-permute-start | bytes 786440 | tf_op jit(solution)/shard_map/ppermute | solution.py:478
  207.9 5.0 %collective-permute-start.42 = (f32[64,512]{1,0:T(8,128)S(1)}, f32[64,512]{1,0:T(8,128)S(1)}, u32[]{:S(2)}, u32[]{:S(2)}) collective-permute-start(f32[64,512]{1,0:T(8,128)S(1)} %dynamic-slice_add_fusion.4), channel_id=1, source_target_pairs={{16,0},{9,1},{18,2},{11,3},{20,4},{13,5},{22,6},{15,7},{24,8},{1,9... | collective-permute-start | bytes 393224 | tf_op jit(solution)/shard_map/ppermute | solution.py:478
  208.0 45.1 %collective-permute-start.29 = (s16[528,512]{1,0:T(8,128)(2,1)}, s16[528,512]{1,0:T(8,128)(2,1)S(1)}, u32[]{:S(2)}, u32[]{:S(2)}) collective-permute-start(s16[528,512]{1,0:T(8,128)(2,1)} %get-tuple-element.16), channel_id=1, source_target_pairs={{0,2},{1,3},{6,4},{7,5},{8,10},{9,11},{14,12},{15,13},{16,18},{17,... | collective-permute-start | bytes 1622024 | tf_op jit(solution)/shard_map/ppermute | solution.py:588
  209.3 51.1 %collective-permute-start.14 = (s16[528,512]{1,0:T(8,128)(2,1)}, s16[528,512]{1,0:T(8,128)(2,1)S(1)}, u32[]{:S(2)}, u32[]{:S(2)}) collective-permute-start(s16[528,512]{1,0:T(8,128)(2,1)} %get-tuple-element.13), channel_id=1, source_target_pairs={{0,2},{1,3},{6,4},{7,5},{8,10},{9,11},{14,12},{15,13},{16,18},{17,... | collective-permute-start | bytes 1622024 | tf_op jit(solution)/shard_map/ppermute | solution.py:588
  211.5 5.0 %collective-permute-start.33 = (f32[64,512]{1,0:T(8,128)S(1)}, f32[64,512]{1,0:T(8,128)S(1)}, u32[]{:S(2)}, u32[]{:S(2)}) collective-permute-start(f32[64,512]{1,0:T(8,128)S(1)} %dynamic-slice_add_fusion.5), channel_id=1, source_target_pairs={{16,0},{9,1},{18,2},{11,3},{20,4},{13,5},{22,6},{15,7},{24,8},{1,9... | collective-permute-start | bytes 393224 | tf_op jit(solution)/shard_map/ppermute | solution.py:478
  212.9 23.6 %collective-permute-start.43 = (f32[64,512]{1,0:T(8,128)S(1)}, f32[64,512]{1,0:T(8,128)S(1)}, u32[]{:S(2)}, u32[]{:S(2)}) collective-permute-start(f32[64,512]{1,0:T(8,128)S(1)} %add_add_fusion.1), channel_id=1, source_target_pairs={{2,0},{3,1},{4,2},{5,3},{6,4},{7,5},{0,6},{1,7},{10,8},{11,9},{12,... | collective-permute-start | bytes 393224 | tf_op jit(solution)/shard_map/ppermute | solution.py:480
  213.0 27.8 %collective-permute-start.44 = (f32[64,512]{1,0:T(8,128)S(1)}, f32[64,512]{1,0:T(8,128)S(1)}, u32[]{:S(2)}, u32[]{:S(2)}) collective-permute-start(f32[64,512]{1,0:T(8,128)S(1)} %add_add_fusion.1), channel_id=1, source_target_pairs={{4,0},{5,1},{6,2},{7,3},{0,4},{1,5},{2,6},{3,7},{12,8},{13,9},{14,... | collective-permute-start | bytes 393224 | tf_op jit(solution)/shard_map/ppermute | solution.py:480
  216.6 26.2 %collective-permute-start.45 = (f32[64,512]{1,0:T(8,128)S(1)}, f32[64,512]{1,0:T(8,128)S(1)}, u32[]{:S(2)}, u32[]{:S(2)}) collective-permute-start(f32[64,512]{1,0:T(8,128)S(1)} %add_add_fusion.1), channel_id=1, source_target_pairs={{6,0},{7,1},{0,2},{1,3},{2,4},{3,5},{4,6},{5,7},{14,8},{15,9},{8,1... | collective-permute-start | bytes 393224 | tf_op jit(solution)/shard_map/ppermute | solution.py:480
  236.5 8.5 %collective-permute-start.34 = (f32[64,512]{1,0:T(8,128)S(1)}, f32[64,512]{1,0:T(8,128)S(1)}, u32[]{:S(2)}, u32[]{:S(2)}) collective-permute-start(f32[64,512]{1,0:T(8,128)S(1)} %add_add_fusion.3), channel_id=1, source_target_pairs={{2,0},{3,1},{4,2},{5,3},{6,4},{7,5},{0,6},{1,7},{10,8},{11,9},{12,... | collective-permute-start | bytes 393224 | tf_op jit(solution)/shard_map/ppermute | solution.py:480
  240.8 9.9 %collective-permute-start.35 = (f32[64,512]{1,0:T(8,128)S(1)}, f32[64,512]{1,0:T(8,128)S(1)}, u32[]{:S(2)}, u32[]{:S(2)}) collective-permute-start(f32[64,512]{1,0:T(8,128)S(1)} %add_add_fusion.3), channel_id=1, source_target_pairs={{4,0},{5,1},{6,2},{7,3},{0,4},{1,5},{2,6},{3,7},{12,8},{13,9},{14,... | collective-permute-start | bytes 393224 | tf_op jit(solution)/shard_map/ppermute | solution.py:480
  242.7 8.0 %collective-permute-start.36 = (f32[64,512]{1,0:T(8,128)S(1)}, f32[64,512]{1,0:T(8,128)S(1)}, u32[]{:S(2)}, u32[]{:S(2)}) collective-permute-start(f32[64,512]{1,0:T(8,128)S(1)} %add_add_fusion.3), channel_id=1, source_target_pairs={{6,0},{7,1},{0,2},{1,3},{2,4},{3,5},{4,6},{5,7},{14,8},{15,9},{8,1... | collective-permute-start | bytes 393224 | tf_op jit(solution)/shard_map/ppermute | solution.py:480
  245.0 22.8 %collective-permute-start.27 = (s16[528,512]{1,0:T(8,128)(2,1)}, s16[528,512]{1,0:T(8,128)(2,1)S(1)}, u32[]{:S(2)}, u32[]{:S(2)}) collective-permute-start(s16[528,512]{1,0:T(8,128)(2,1)} %get-tuple-element.16), channel_id=1, source_target_pairs={{2,4},{3,5},{4,2},{5,3},{10,12},{11,13},{12,10},{13,11},{18,20},{1... | collective-permute-start | bytes 1622024 | tf_op jit(solution)/shard_map/ppermute | solution.py:589
  250.7 24.5 %collective-permute-start.28 = (s16[528,512]{1,0:T(8,128)(2,1)}, s16[528,512]{1,0:T(8,128)(2,1)S(1)}, u32[]{:S(2)}, u32[]{:S(2)}) collective-permute-start(s16[528,512]{1,0:T(8,128)(2,1)} %get-tuple-element.17), channel_id=1, source_target_pairs={{2,0},{3,1},{0,2},{1,3},{6,4},{7,5},{4,6},{5,7},{10,8},{11,9},{8,1... | collective-permute-start | bytes 1622024 | tf_op jit(solution)/shard_map/ppermute | solution.py:589
  250.7 5.8 %collective-permute-start.46 = (f32[64,512]{1,0:T(8,128)S(1)}, f32[64,512]{1,0:T(8,128)S(1)}, u32[]{:S(2)}, u32[]{:S(2)}) collective-permute-start(f32[64,512]{1,0:T(8,128)S(1)} %add_add_fusion), channel_id=1, source_target_pairs={{16,0},{9,1},{18,2},{11,3},{20,4},{13,5},{22,6},{15,7},{24,8},{1,9... | collective-permute-start | bytes 393224 | tf_op jit(solution)/shard_map/ppermute | solution.py:483
  253.1 6.8 %collective-permute-start.37 = (f32[64,512]{1,0:T(8,128)S(1)}, f32[64,512]{1,0:T(8,128)S(1)}, u32[]{:S(2)}, u32[]{:S(2)}) collective-permute-start(f32[64,512]{1,0:T(8,128)S(1)} %add_add_fusion.2), channel_id=1, source_target_pairs={{16,0},{9,1},{18,2},{11,3},{20,4},{13,5},{22,6},{15,7},{24,8},{1,9... | collective-permute-start | bytes 393224 | tf_op jit(solution)/shard_map/ppermute | solution.py:483
  256.5 34.8 %collective-permute-start.30 = (s16[528,512]{1,0:T(8,128)(2,1)}, s16[528,512]{1,0:T(8,128)(2,1)S(1)}, u32[]{:S(2)}, u32[]{:S(2)}) collective-permute-start(s16[528,512]{1,0:T(8,128)(2,1)} %join_far.3), channel_id=1, source_target_pairs={{4,0},{5,1},{6,2},{7,3},{0,4},{1,5},{2,6},{3,7},{12,8},{13,9},{14,... | collective-permute-start | bytes 1622024 | tf_op jit(solution)/shard_map/ppermute | solution.py:591
  259.8 6.4 %collective-permute-start.47 = (f32[128,512]{1,0:T(8,128)S(1)}, f32[128,512]{1,0:T(8,128)S(1)}, u32[]{:S(2)}, u32[]{:S(2)}) collective-permute-start(f32[128,512]{1,0:T(8,128)S(1)} %maximum_select_fusion.3), channel_id=1, source_target_pairs={{8,0},{17,1},{10,2},{19,3},{12,4},{21,5},{14,6},{23,7},{0,8},{25,9... | collective-permute-start | bytes 786440 | tf_op jit(solution)/shard_map/ppermute | solution.py:483
  260.4 1.7 copy-start.18
  260.4 17.1 %collective-permute-start.38 = (f32[128,512]{1,0:T(8,128)S(1)}, f32[128,512]{1,0:T(8,128)}, u32[]{:S(2)}, u32[]{:S(2)}) collective-permute-start(f32[128,512]{1,0:T(8,128)S(1)} %maximum_select_fusion.2), channel_id=1, source_target_pairs={{8,0},{17,1},{10,2},{19,3},{12,4},{21,5},{14,6},{23,7},{0,8},{25,9... | collective-permute-start | bytes 786440 | tf_op jit(solution)/shard_map/ppermute | solution.py:483
  266.3 28.5 %collective-permute-start.12 = (s16[528,512]{1,0:T(8,128)(2,1)}, s16[528,512]{1,0:T(8,128)(2,1)S(1)}, u32[]{:S(2)}, u32[]{:S(2)}) collective-permute-start(s16[528,512]{1,0:T(8,128)(2,1)} %get-tuple-element.13), channel_id=1, source_target_pairs={{2,4},{3,5},{4,2},{5,3},{10,12},{11,13},{12,10},{13,11},{18,20},{1... | collective-permute-start | bytes 1622024 | tf_op jit(solution)/shard_map/ppermute | solution.py:589
  267.8 23.5 %copy-start.12 = (s16[528,512]{1,0:T(8,128)(2,1)}, s16[528,512]{1,0:T(8,128)(2,1)S(1)}, u32[]{:S(2)}) copy-start(s16[528,512]{1,0:T(8,128)(2,1)S(1)} %collective-permute-done.27.refs_0_.refs_3_) | copy-start | bytes 1622020
  267.8 27.0 %collective-permute-start.13 = (s16[528,512]{1,0:T(8,128)(2,1)}, s16[528,512]{1,0:T(8,128)(2,1)S(1)}, u32[]{:S(2)}, u32[]{:S(2)}) collective-permute-start(s16[528,512]{1,0:T(8,128)(2,1)} %get-tuple-element.14), channel_id=1, source_target_pairs={{2,0},{3,1},{0,2},{1,3},{6,4},{7,5},{4,6},{5,7},{10,8},{11,9},{8,1... | collective-permute-start | bytes 1622024 | tf_op jit(solution)/shard_map/ppermute | solution.py:589
  275.1 16.1 %copy-start.13 = (s16[528,512]{1,0:T(8,128)(2,1)}, s16[528,512]{1,0:T(8,128)(2,1)S(1)}, u32[]{:S(2)}) copy-start(s16[528,512]{1,0:T(8,128)(2,1)S(1)} %collective-permute-done.28.refs_1_.refs_4_) | copy-start | bytes 1622020
  275.1 43.8 %collective-permute-start.15 = (s16[528,512]{1,0:T(8,128)(2,1)}, s16[528,512]{1,0:T(8,128)(2,1)S(1)}, u32[]{:S(2)}, u32[]{:S(2)}) collective-permute-start(s16[528,512]{1,0:T(8,128)(2,1)} %join_far.2), channel_id=1, source_target_pairs={{4,0},{5,1},{6,2},{7,3},{0,4},{1,5},{2,6},{3,7},{12,8},{13,9},{14,... | collective-permute-start | bytes 1622024 | tf_op jit(solution)/shard_map/ppermute | solution.py:591
  277.5 44.9 %collective-permute-start.48 = (f32[256,512]{1,0:T(8,128)}, f32[256,512]{1,0:T(8,128)}, u32[]{:S(2)}, u32[]{:S(2)}) collective-permute-start(f32[256,512]{1,0:T(8,128)} %maximum_select_fusion.1.mine), channel_id=1, source_target_pairs={{1,0},{0,1},{3,2},{2,3},{5,4},{4,5},{7,6},{6,7},{9,8},{8,9},{11,10... | collective-permute-start | bytes 1572872 | tf_op jit(solution)/shard_map/ppermute | solution.py:486
  291.3 33.4 %collective-permute-start.39 = (f32[256,512]{1,0:T(8,128)}, f32[256,512]{1,0:T(8,128)}, u32[]{:S(2)}, u32[]{:S(2)}) collective-permute-start(f32[256,512]{1,0:T(8,128)} %maximum_select_fusion.mine), channel_id=1, source_target_pairs={{1,0},{0,1},{3,2},{2,3},{5,4},{4,5},{7,6},{6,7},{9,8},{8,9},{11,10... | collective-permute-start | bytes 1572872 | tf_op jit(solution)/shard_map/ppermute | solution.py:486
  294.8 24.1 %copy-start.15 = (s16[528,512]{1,0:T(8,128)(2,1)}, s16[528,512]{1,0:T(8,128)(2,1)S(1)}, u32[]{:S(2)}) copy-start(s16[528,512]{1,0:T(8,128)(2,1)S(1)} %collective-permute-done.12.refs_0_.refs_3_) | copy-start | bytes 1622020
  294.8 24.1 %copy-start.16 = (s16[528,512]{1,0:T(8,128)(2,1)}, s16[528,512]{1,0:T(8,128)(2,1)S(1)}, u32[]{:S(2)}) copy-start(s16[528,512]{1,0:T(8,128)(2,1)S(1)} %collective-permute-done.13.refs_1_.refs_4_) | copy-start | bytes 1622020
  (6 other events, 5.5 us)

commit v3 on v2

--- a/solution.py
+++ b/solution.py
@@ -8,7 +8,7 @@
 from jax.sharding import PartitionSpec as P
 
 BS = 128
-GROUP = 4
+GROUP = 8
 TAIL = 16
 AXES = ("row", "col")
 
@@ -92,15 +92,23 @@
         def _(other=other):
             pltpu.make_async_copy(own[other].at[supernode * per_col + item], buf.at[pl.ds(start, BS)], sem).start()
 
-        @pl.when(mine & (shift != 0))
-        def _(other=other):
-            for e in range(n_row):
-                masks = [sum(swap_bit(bits, p, b) for b in range(bits) if e >> b & 1) for p in (0, 1)]
-                mask = jnp.where(parity == 0, masks[0], masks[1])
-                place = pl.multiple_of(start + (my_row ^ mask) * sub, sub)
-                pltpu.make_async_copy(
-                    pieces[other][e].at[(shift - 1) * per_col + item], buf.at[pl.ds(place, sub)], sem
-                ).start()
+        span = (n_line - 1) // len(pieces)
+        for part, sides in enumerate(pieces):
+            here = mine & (shift > part * span) & (shift <= (part + 1) * span)
+
+            @pl.when(here)
+            def _(side=sides[other], before=part * span + 1):
+                for e in range(n_row):
+                    masks = [sum(swap_bit(bits, p, b) for b in range(bits) if e >> b & 1) for p in (0, 1)]
+                    mask = jnp.where(parity == 0, masks[0], masks[1])
+                    place = pl.multiple_of(start + (my_row ^ mask) * sub, sub)
+                    source_ref = side[e].at[(shift - before) * per_col + item]
+                    pltpu.make_async_copy(source_ref, buf.at[pl.ds(place, sub)], sem).start()
+
+
+def panel_refs(refs, n_row, parts):
+    sides = [refs[2 + n_row * at : 2 + n_row * (at + 1)] for at in range(2 * parts)]
+    return refs[0:2], [sides[2 * part : 2 * part + 2] for part in range(parts)], refs[2 + 2 * n_row * parts :]
 
 
 def wait_fetch(buf, at, sem):
@@ -178,13 +186,12 @@
     )(tab, inverse)
 
 
-def product_kernel(dims, supernode, tab, inverse, packed, *refs):
+def product_kernel(dims, supernode, parts, tab, inverse, packed, *refs):
     n_row, n_col, _, max_rows, max_cols, _ = dims
     n_line = n_col // 2
     in_chunk = max_rows // n_col
-    own = refs[0:2]
-    pieces = (refs[2 : 2 + n_row], refs[2 + n_row : 2 + 2 * n_row])
-    total_ref, *outs = refs[2 + 2 * n_row : -4]
+    own, pieces, refs = panel_refs(refs, n_row, parts)
+    total_ref, *outs = refs[:-4]
     cols_buf, strips, cols_sem, strip_sem = refs[-4:]
     total = total_ref.at[0]
     step = pl.program_id(0)
@@ -304,9 +311,9 @@
     coded_shape = (chunk_rows + TAIL, width)
     any_spec = pl.BlockSpec(memory_space=pl.ANY)
     whole = lambda shape: pl.BlockSpec(shape, lambda g, tab: (0, 0))
-    operands = [inverse, packed, *own, *pieces[0], *pieces[1]]
-    return pl.pallas_call(
-        functools.partial(product_kernel, dims, supernode),
+    operands = [inverse, packed, *own, *(piece for sides in pieces for side in sides for piece in side)]
+    return pl.pallas_call(
+        functools.partial(product_kernel, dims, supernode, len(pieces)),
         out_shape=(jax.ShapeDtypeStruct((n_line, chunk_rows, width), jnp.float32),)
         + (jax.ShapeDtypeStruct(coded_shape, jnp.int16),) * len(coded_masks(n_line)),
         grid_spec=pltpu.PrefetchScalarGridSpec(
@@ -327,13 +334,12 @@
     )(tab, *operands)
 
 
-def diag_kernel(dims, supernode, tab, total, *refs):
+def diag_kernel(dims, supernode, parts, tab, total, *refs):
     n_row, n_col, _, max_rows, max_cols, _ = dims
     n_line = n_col // 2
     in_chunk = max_rows // n_col
-    own = refs[0:2]
-    pieces = (refs[2 : 2 + n_row], refs[2 + n_row : 2 + 2 * n_row])
-    sent, kept, diag, rows_buf, rows_sem = refs[2 + 2 * n_row :]
+    own, pieces, refs = panel_refs(refs, n_row, parts)
+    sent, kept, diag, rows_buf, rows_sem = refs
     step = pl.program_id(0)
     chunk_rows = in_chunk * BS
     base = 2 * max_rows + 2 * max_cols
@@ -384,9 +390,9 @@
 def diag_terms(tab, total, own, pieces, dims, supernode):
     n_line, chunk_rows, width = total.shape
     any_spec = pl.BlockSpec(memory_space=pl.ANY)
-    operands = [*own, *pieces[0], *pieces[1]]
-    return pl.pallas_call(
-        functools.partial(diag_kernel, dims, supernode),
+    operands = [*own, *(piece for sides in pieces for side in sides for piece in side)]
+    return pl.pallas_call(
+        functools.partial(diag_kernel, dims, supernode, len(pieces)),
         out_shape=(jax.ShapeDtypeStruct((width // 2, width), jnp.float32),) * 2,
         grid_spec=pltpu.PrefetchScalarGridSpec(
             num_scalar_prefetch=1,
@@ -467,58 +473,85 @@
     return (my_row >> place) & 1
 
 
-def sum_over_all(sent, kept, n_row, n_col, my_row, my_parity):
+def halve_sum(sent, kept, n_row, n_col, my_row, my_parity):
     bits = n_row.bit_length() - 1
-    n_line = n_col // 2
     got = lax.ppermute(sent, "col", core_swap(n_col))
     for step in range(bits):
         bit = row_bit(bits, step, my_row, my_parity)
         sent = half(kept, 1 - bit) + half(got, 1 - bit)
         kept = half(kept, bit) + half(got, bit)
         got = lax.ppermute(sent, AXES, row_swap(n_row, n_col, step))
-    part = kept + got
-    got = [lax.ppermute(part, "col", line_shift(n_col, shift)) for shift in range(1, n_line)]
-    whole = sum(got, part)
-    for step in reversed(range(bits)):
-        other = lax.ppermute(whole, AXES, row_swap(n_row, n_col, step))
-        bit = row_bit(bits, step, my_row, my_parity)
-        whole = jnp.where(bit == 0, jnp.concatenate([whole, other]), jnp.concatenate([other, whole]))
-    return whole, lax.ppermute(whole, "col", core_swap(n_col))
-
-
-def place_kernel(parity, mine, other, *refs):
+    return kept, got
+
+
+def fold_kernel(*refs):
+    total, coded = refs[-2:]
+    supernodes, rows, _ = total.shape
+    for s in range(supernodes):
+        total[s] = refs[2 * s][...] + refs[2 * s + 1][...]
+    body, tail = encode(total[...].reshape(supernodes * rows, total.shape[2]))
+    coded[0 : supernodes * rows, :] = body
+    coded[supernodes * rows :, :] = tail
+
+
+def fold_pieces(terms):
+    rows, width = terms[0].shape
+    supernodes = len(terms) // 2
+    return pl.pallas_call(
+        fold_kernel,
+        out_shape=(
+            jax.ShapeDtypeStruct((supernodes, rows, width), jnp.float32),
+            jax.ShapeDtypeStruct((supernodes * rows + TAIL, width), jnp.int16),
+        ),
+        cost_estimate=pl.CostEstimate(flops=10**6, bytes_accessed=10**6, transcendentals=0),
+        name="fold_pieces",
+    )(*terms)
+
+
+def line_kernel(total, *refs):
     out = refs[-1]
-
-    @pl.when(pl.program_id(0) == parity[0])
-    def _():
-        out[0] = mine[...]
-
-    @pl.when(pl.program_id(0) != parity[0])
-    def _():
-        out[0] = other[...]
-
-
-def place_halves(supernodes, supernode, parity, mine, other, earlier):
-    rows, width = mine.shape
-    whole = pl.BlockSpec((rows, width), lambda g, parity: (0, 0))
-    operands, specs, aliases = [mine, other], [whole, whole], {}
-    if earlier is not None:
-        aliases = {3: 0}
-        operands.append(earlier)
-        specs.append(pl.BlockSpec(memory_space=pl.ANY))
+    supernodes, rows, _ = out.shape
+    for s in range(supernodes):
+        piece = total[s]
+        for part in refs[:-1]:
+            piece = piece + decode(part[s * rows : (s + 1) * rows, :], part[supernodes * rows :, :])
+        out[s] = piece
+
+
+def line_sums(total, coded):
+    return pl.pallas_call(
+        line_kernel,
+        out_shape=jax.ShapeDtypeStruct(total.shape, jnp.float32),
+        cost_estimate=pl.CostEstimate(flops=10**6, bytes_accessed=10**6, transcendentals=0),
+        name="line_sums",
+    )(total, *coded)
+
+
+def place_kernel(parity, mine, other, out):
+    @pl.when(pl.program_id(1) == parity[0])
+    def _():
+        out[...] = mine[...]
+
+    @pl.when(pl.program_id(1) != parity[0])
+    def _():
+        out[...] = other[...]
+
+
+def place_halves(parity, mine, other):
+    supernodes, rows, width = mine.shape
+    block = pl.BlockSpec((1, rows, width), lambda s, g, parity: (s, 0, 0))
     return pl.pallas_call(
         place_kernel,
         out_shape=jax.ShapeDtypeStruct((supernodes, 2 * rows, width), jnp.float32),
         grid_spec=pltpu.PrefetchScalarGridSpec(
             num_scalar_prefetch=1,
-            grid=(2,),
-            in_specs=specs,
-            out_specs=pl.BlockSpec((1, rows, width), lambda g, parity: (supernode, g, 0)),
+            grid=(supernodes, 2),
+            in_specs=[block, block],
+            out_specs=pl.BlockSpec((1, rows, width), lambda s, g, parity: (s, g, 0)),
         ),
-        input_output_aliases=aliases,
-        cost_estimate=pl.CostEstimate(flops=0, bytes_accessed=2 * 10**6, transcendentals=0),
+        cost_estimate=pl.CostEstimate(flops=0, bytes_accessed=4 * 10**6, transcendentals=0),
         name="place_halves",
-    )(parity, *operands)
+    )(parity, mine, other)
 
 
 def local(inverse, panels, block_slot, list_ids):
@@ -561,24 +594,24 @@
     dims = (n_row, n_col, per_col, max_rows, max_cols, sub)
     held = []
     for s in range(supernodes):
-        mine = lax.dynamic_slice(
-            blocks, (s * per_col, my_row * sub, 0), (per_col, sub, width)
-        )
-        line = jnp.concatenate(
-            [lax.ppermute(mine, "col", line_shift(n_col, shift)) for shift in range(1, n_line)], axis=0
-        )
-        pieces = [line]
-        for e in range(1, n_row):
-            bit = e.bit_length() - 1
-            if s == 0:
-                source, pairs = pieces[e ^ (1 << bit)], row_swap(n_row, n_col, bit)
-            else:
-                source, pairs = line, row_jump(n_row, n_col, e)
-            pieces.append(lax.ppermute(source, AXES, pairs))
-        other = [lax.ppermute(piece, "col", core_swap(n_col)) for piece in pieces]
-        held.append((pieces, other))
+        mine = lax.dynamic_slice(blocks, (s * per_col, my_row * sub, 0), (per_col, sub, width))
+        got = [lax.ppermute(mine, "col", line_shift(n_col, shift)) for shift in range(1, n_line)]
+        if s > 0 or n_line > 4:
+            got = [jnp.concatenate(got, axis=0)]
+        held.append([])
+        for line in got:
+            pieces = [line]
+            for e in range(1, n_row):
+                bit = e.bit_length() - 1
+                if s == 0:
+                    source, pairs = pieces[e ^ (1 << bit)], row_swap(n_row, n_col, bit)
+                else:
+                    source, pairs = line, row_jump(n_row, n_col, e)
+                pieces.append(lax.ppermute(source, AXES, pairs))
+            other = [lax.ppermute(piece, "col", core_swap(n_col)) for piece in pieces]
+            held[s].append((pieces, other))
     out = None
-    diag = None
+    terms = []
     for s in range(supernodes):
         packed = pack_strips(tables[s], inverse, dims)
         packed = lax.ppermute(packed, "col", core_swap(n_col))
@@ -592,10 +625,20 @@
         else:
             moved = [lax.ppermute(part, "col", line_swap(n_col, mask)) for mask, part in coded.items()]
         sent, kept = diag_terms(tables[s], total, own, held[s], dims, s)
-        mine, other = sum_over_all(sent, kept, n_row, n_col, my_row, my_col % 2)
-        diag = place_halves(supernodes, s, (my_col % 2).reshape(1), mine, other, diag)
+        terms += halve_sum(sent, kept, n_row, n_col, my_row, my_col % 2)
         out = final_sums(supernodes, s, total, moved, out)
-    return out, diag
+    bits = n_row.bit_length() - 1
+    total, coded = fold_pieces(terms)
+    coded = [lax.ppermute(coded, "col", line_shift(n_col, shift)) for shift in range(1, n_line)]
+    whole = line_sums(total, coded)
+    for step in reversed(range(bits)):
+        other = lax.ppermute(whole, AXES, row_swap(n_row, n_col, step))
+        low = row_bit(bits, step, my_row, my_col % 2) == 0
+        whole = jnp.where(
+            low, jnp.concatenate([whole, other], axis=1), jnp.concatenate([other, whole], axis=1)
+        )
+    other = lax.ppermute(whole, "col", core_swap(n_col))
+    return out, place_halves((my_col % 2).reshape(1), whole, other)
 
 
 def solution(mesh):

time: 328 us -> 344 us (1.049)
  waiting for transfers between devices: 158 us -> 185 us
  starting transfers between devices: 56.9 us -> 50.9 us
    ppermute x2, waiting for transfers between devices: 0.01 us -> 22.5 us  [local(): far = lax.ppermute(coded[3], 'col', inward(n_col))]
    ppermute x6 -> x12, waiting for transfers between devices: 49.3 us -> 63 us  [local(): pieces.append(lax.ppermute(source, AXES, pairs))]
    ppermute x18 -> x12, starting transfers between devices: 15.2 us -> 3.49 us  [the longest x3 2.03 us: local(): lax.ppermute(coded, 'col', line_shift(n_col, shift))]
    ppermute x18 -> x12, waiting for transfers between devices: 36.2 us -> 28.1 us  [the longest x4 10.5 us: halve_sum(): got = lax.ppermute(sent, AXES, row_swap(n_row, n_col, step))]
    ppermute x6, waiting for transfers between devices: 35 us -> 28.5 us  [local(): lax.ppermute(mine, 'col', line_shift(n_col, shift))]
    ppermute x2, starting transfers between devices: 7.32 us -> 3.08 us  [local(): lax.ppermute(coded[1], 'col', line_swap(n_col, 1))]
    ppermute x6, starting transfers between devices: 18.1 us -> 21.6 us  [local(): lax.ppermute(mine, 'col', line_shift(n_col, shift))]
    ppermute x2, starting transfers between devices: 2.65 us -> 6.15 us  [local(): far = lax.ppermute(coded[3], 'col', inward(n_col))]
  transfers between devices with their start and end apart: 49 -> 57, of which waited for: 19 -> 27; matrix products, arithmetic and copies ran while one was open for 2% -> 1% of each run, Pallas kernels for 26% -> 22%
where the time goes in v3:
time: 344 us; the launch traced here: 343 us
  waiting for transfers between devices  185 us (54%)
  Pallas kernels  94.1 us (27%)
  starting transfers between devices  50.9 us (15%)
  other arithmetic  6.61 us (2%)
  local copies, waits for them, and re-layouts  5.63 us (2%)
    ppermute x12, waiting for transfers between devices, local(): pieces.append(lax.ppermute(source, AXES, pairs))  63 us
    ppermute x2, waiting for transfers between devices, local(): moved.append(lax.ppermute(joined, 'col', line_swap(n_col, 2)))  39 us
    pallas_call x2, Pallas kernels, products(): pl.pallas_call(functools.partial(product_kernel, dims, supernode, len(pie...  38.7 us
    ppermute x6, waiting for transfers between devices, local(): lax.ppermute(mine, 'col', line_shift(n_col, shift))  28.5 us
    ppermute x2, waiting for transfers between devices, local(): far = lax.ppermute(coded[3], 'col', inward(n_col))  22.5 us
    ppermute x6, starting transfers between devices, local(): lax.ppermute(mine, 'col', line_shift(n_col, shift))  21.6 us
    pallas_call x2, Pallas kernels, pack_strips(): pl.pallas_call(functools.partial(pack_kernel, dims), out_shape=jax.ShapeD...  21.2 us
    pallas_call x2, Pallas kernels, diag_terms(): pl.pallas_call(functools.partial(diag_kernel, dims, supernode, len(pieces...  15.8 us
  transfers between devices with their start and end apart: 57, of which 27 were waited for; matrix products, arithmetic and copies ran while one was open for 1% of the time, Pallas kernels for 22%

profile of v3, /device:TPU:0, one launch (start us, length us, event | category | flops | bytes accessed | tf_op | source)
XLA Modules:
  0.0 343.1 jit_solution(15231967890349067327)
XLA Ops:
  0.7 0.9 select_reduce_fusion
  3.4 10.6 %pack_strips.2 = bf16[2048,3328]{1,0:T(8,128)(2,1)} custom-call(s32[132]{0:T(256)} %bitcast.27, bf16[6656,3328]{1,0:T(8,128)(2,1)} %inverse.7), custom_call_target="tpu_custom_call" | custom-call | bytes 27000000 | tf_op jit(solution)/shard_map/pack_strips/pallas_call | solution.py:170
  14.5 10.6 %pack_strips.3 = bf16[2048,3328]{1,0:T(8,128)(2,1)} custom-call(s32[132]{0:T(256)} %bitcast.24, bf16[6656,3328]{1,0:T(8,128)(2,1)} %inverse.7), custom_call_target="tpu_custom_call" | custom-call | bytes 27000000 | tf_op jit(solution)/shard_map/pack_strips/pallas_call | solution.py:170
  25.3 5.1 %collective-permute-start.2 = (bf16[8,32,512]{2,1,0:T(8,128)(2,1)S(1)}, bf16[8,32,512]{2,1,0:T(8,128)(2,1)S(1)}, u32[]{:S(2)}, u32[]{:S(2)}) collective-permute-start(bf16[8,32,512]{2,1,0:T(8,128)(2,1)S(1)} %get-tuple-element.34), channel_id=1, source_target_pairs={{2,0},{3,1},{4,2},{5,3},{6,4},{7,5},{0,6},{1,7},{10,8},{11,9},{12,... | collective-permute-start | bytes 786440 | tf_op jit(solution)/shard_map/ppermute | solution.py:598
  30.4 1.0 collective-permute-start.4
  31.4 5.8 %collective-permute-done.2 = bf16[8,32,512]{2,1,0:T(8,128)(2,1)S(1)} collective-permute-done((bf16[8,32,512]{2,1,0:T(8,128)(2,1)S(1)}, bf16[8,32,512]{2,1,0:T(8,128)(2,1)S(1)}, u32[]{:S(2)}, u32[]{:S(2)}) %collective-permute-start.2) | collective-permute-done | bytes 262176 | tf_op jit(solution)/shard_map/ppermute | solution.py:598
  37.2 4.3 %collective-permute-start.17 = (bf16[8,32,512]{2,1,0:T(8,128)(2,1)S(1)}, bf16[8,32,512]{2,1,0:T(8,128)(2,1)S(1)}, u32[]{:S(2)}, u32[]{:S(2)}) collective-permute-start(bf16[8,32,512]{2,1,0:T(8,128)(2,1)S(1)} %get-tuple-element.33), channel_id=1, source_target_pairs={{2,0},{3,1},{4,2},{5,3},{6,4},{7,5},{0,6},{1,7},{10,8},{11,9},{12,... | collective-permute-start | bytes 786440 | tf_op jit(solution)/shard_map/ppermute | solution.py:598
  41.5 13.2 %collective-permute-done.3 = bf16[8,32,512]{2,1,0:T(8,128)(2,1)S(1)} collective-permute-done((bf16[8,32,512]{2,1,0:T(8,128)(2,1)S(1)}, bf16[8,32,512]{2,1,0:T(8,128)(2,1)S(1)}, u32[]{:S(2)}, u32[]{:S(2)}) %collective-permute-start.3) | collective-permute-done | bytes 262176 | tf_op jit(solution)/shard_map/ppermute | solution.py:598
  54.7 11.2 %collective-permute-start.33 = (bf16[8,32,512]{2,1,0:T(8,128)(2,1)S(1)}, bf16[8,32,512]{2,1,0:T(8,128)(2,1)S(1)}, u32[]{:S(2)}, u32[]{:S(2)}) collective-permute-start(bf16[8,32,512]{2,1,0:T(8,128)(2,1)S(1)} %get-tuple-element.33), channel_id=1, source_target_pairs={{6,0},{7,1},{0,2},{1,3},{2,4},{3,5},{4,6},{5,7},{14,8},{15,9},{8,1... | collective-permute-start | bytes 786440 | tf_op jit(solution)/shard_map/ppermute | solution.py:598
  65.8 9.6 %collective-permute-done.25.refs_10_ = bf16[8,32,512]{2,1,0:T(8,128)(2,1)S(1)} collective-permute-done((bf16[8,32,512]{2,1,0:T(8,128)(2,1)S(1)}, bf16[8,32,512]{2,1,0:T(8,128)(2,1)S(1)}, u32[]{:S(2)}, u32[]{:S(2)}) %collective-permute-start.25) | collective-permute-done | bytes 262176 | tf_op jit(solution)/shard_map/ppermute | solution.py:598
  75.4 2.0 collective-permute-start.34
  77.4 7.2 %collective-permute-done.26.refs_11_ = bf16[8,32,512]{2,1,0:T(8,128)(2,1)} collective-permute-done((bf16[8,32,512]{2,1,0:T(8,128)(2,1)S(1)}, bf16[8,32,512]{2,1,0:T(8,128)(2,1)}, u32[]{:S(2)}, u32[]{:S(2)}) %collective-permute-start.26) | collective-permute-done | bytes 262176 | tf_op jit(solution)/shard_map/ppermute | solution.py:610
  84.7 5.6 %collective-permute-done.34.refs_19_ = bf16[8,32,512]{2,1,0:T(8,128)(2,1)} collective-permute-done((bf16[8,32,512]{2,1,0:T(8,128)(2,1)S(1)}, bf16[8,32,512]{2,1,0:T(8,128)(2,1)}, u32[]{:S(2)}, u32[]{:S(2)}) %collective-permute-start.34) | collective-permute-done | bytes 262176 | tf_op jit(solution)/shard_map/ppermute | solution.py:610
  90.3 0.8 collective-permute-done.27.refs_12_
  91.2 5.5 %collective-permute-done.35.refs_20_ = bf16[8,32,512]{2,1,0:T(8,128)(2,1)S(1)} collective-permute-done((bf16[8,32,512]{2,1,0:T(8,128)(2,1)S(1)}, bf16[8,32,512]{2,1,0:T(8,128)(2,1)S(1)}, u32[]{:S(2)}, u32[]{:S(2)}) %collective-permute-start.35) | collective-permute-done | bytes 262176 | tf_op jit(solution)/shard_map/ppermute | solution.py:610
  96.7 0.7 copy-done.19
  97.5 2.0 collective-permute-start.28
  99.8 4.1 %collective-permute-done.20.refs_5_ = bf16[8,32,512]{2,1,0:T(8,128)(2,1)S(1)} collective-permute-done((bf16[8,32,512]{2,1,0:T(8,128)(2,1)S(1)}, bf16[8,32,512]{2,1,0:T(8,128)(2,1)S(1)}, u32[]{:S(2)}, u32[]{:S(2)}) %collective-permute-start.20) | collective-permute-done | bytes 262176 | tf_op jit(solution)/shard_map/ppermute | solution.py:610
  103.9 2.8 collective-permute-done.28.refs_13_
  106.7 11.3 %collective-permute-done.36.refs_21_ = bf16[8,32,512]{2,1,0:T(8,128)(2,1)} collective-permute-done((bf16[8,32,512]{2,1,0:T(8,128)(2,1)}, bf16[8,32,512]{2,1,0:T(8,128)(2,1)}, u32[]{:S(2)}, u32[]{:S(2)}) %collective-permute-start.36) | collective-permute-done | bytes 262176 | tf_op jit(solution)/shard_map/ppermute | solution.py:610
  118.0 1.5 collective-permute-start.5
  119.5 18.6 %collective-permute-done.7.refs_5_ = bf16[24,32,512]{2,1,0:T(8,128)(2,1)S(1)} collective-permute-done((bf16[24,32,512]{2,1,0:T(8,128)(2,1)S(1)}, bf16[24,32,512]{2,1,0:T(8,128)(2,1)S(1)}, u32[]{:S(2)}, u32[]{:S(2)}) %collective-permute-start.7) | collective-permute-done | bytes 786464 | tf_op jit(solution)/shard_map/ppermute | solution.py:610
  138.1 6.9 %collective-permute-done.5.refs_3_ = bf16[24,32,512]{2,1,0:T(8,128)(2,1)S(1)} collective-permute-done((bf16[24,32,512]{2,1,0:T(8,128)(2,1)S(1)}, bf16[24,32,512]{2,1,0:T(8,128)(2,1)S(1)}, u32[]{:S(2)}, u32[]{:S(2)}) %collective-permute-start.5) | collective-permute-done | bytes 786464 | tf_op jit(solution)/shard_map/ppermute | solution.py:610
  145.6 1.8 collective-permute-done.10.refs_8_
  147.7 0.8 collective-permute-done.11.refs_9_
  148.8 0.8 collective-permute-done.9.refs_7_
  150.0 1.3 copy-done.1
  152.0 19.4 %products.2 = (f32[4,512,512]{2,1,0:T(8,128)}, s16[528,512]{1,0:T(8,128)(2,1)}, s16[528,512]{1,0:T(8,128)(2,1)}) custom-call(s32[132]{0:T(256)} %bitcast.28, bf16[6656,3328]{1,0:T(8,128)(2,1)} %inverse.7, bf16[2048,3328]{1,0:T(8,128)(2,1)} %collective-permute-done.packed, bf16[16,128,512]{2,1,0:T(8,128)(2,1)} %bitcast.18, bf16[16,128,512]{2,1,0:T(8,128)(2,1)} %copy-done.1, ...), custom_call_target="tpu_custom_call" | custom-call | flops 10000000000 | bytes 30000000 | tf_op jit(solution)/shard_map/products/pallas_call | solution.py:315
  172.6 7.8 %diag_terms.3 = (f32[256,512]{1,0:T(8,128)}, f32[256,512]{1,0:T(8,128)}) custom-call(s32[132]{0:T(256)} %bitcast.29, f32[4,512,512]{2,1,0:T(8,128)} %get-tuple-element.14.total.first, bf16[16,128,512]{2,1,0:T(8,128)(2,1)} %bitcast.19, bf16[16,128,512]{2,1,0:T(8,128)(2,1)} %copy-done.1, bf16[24,32,512]{2,1,0:T(8,128)(2,1)} %copy-done.2, ...), custom_call_target="tpu_custom_call" | custom-call | flops 3000000000 | bytes 7000000 | tf_op jit(solution)/shard_map/diag_terms/pallas_call | solution.py:394
  181.7 19.3 %products.3 = (f32[4,512,512]{2,1,0:T(8,128)}, s16[528,512]{1,0:T(8,128)(2,1)}, s16[528,512]{1,0:T(8,128)(2,1)}) custom-call(s32[132]{0:T(256)} %bitcast.25, bf16[6656,3328]{1,0:T(8,128)(2,1)} %inverse.7, bf16[2048,3328]{1,0:T(8,128)(2,1)} %collective-permute-done.16.packed, bf16[16,128,512]{2,1,0:T(8,128)(2,1)} %bitcast.20, ...), custom_call_target="tpu_custom_call" | custom-call | flops 10000000000 | bytes 30000000 | tf_op jit(solution)/shard_map/products/pallas_call | solution.py:315
  201.0 8.0 %diag_terms.2 = (f32[256,512]{1,0:T(8,128)}, f32[256,512]{1,0:T(8,128)}) custom-call(s32[132]{0:T(256)} %bitcast.26, f32[4,512,512]{2,1,0:T(8,128)} %get-tuple-element.17.total.first, bf16[16,128,512]{2,1,0:T(8,128)(2,1)} %bitcast.21, bf16[16,128,512]{2,1,0:T(8,128)(2,1)} %copy-done.1, bf16[8,32,512]{2,1,0:T(8,128)(2,1)} %copy-done.15, ...), custom_call_target="tpu_custom_call" | custom-call | flops 3000000000 | bytes 7000000 | tf_op jit(solution)/shard_map/diag_terms/pallas_call | solution.py:394
  209.4 1.7 collective-permute-done.45
  211.1 1.1 dynamic-slice_add_fusion.3
  212.6 3.2 collective-permute-done.49
  215.8 0.7 dynamic-slice_add_fusion.4
  216.5 2.4 collective-permute-done.46
  218.9 0.7 dynamic-slice_add_fusion.6
  219.6 1.9 collective-permute-done.50.refs_3_
  221.5 3.1 collective-permute-done.47.refs_1_
  225.2 1.9 fold_pieces.1
  227.1 2.0 collective-permute-start.53
  229.1 4.9 %collective-permute-done.51.refs_0_ = s16[144,512]{1,0:T(8,128)(2,1)S(1)} collective-permute-done((s16[144,512]{1,0:T(8,128)(2,1)}, s16[144,512]{1,0:T(8,128)(2,1)S(1)}, u32[]{:S(2)}, u32[]{:S(2)}) %collective-permute-start.51) | collective-permute-done | bytes 147488 | tf_op jit(solution)/shard_map/ppermute | solution.py:632
  234.0 4.4 %collective-permute-done.52.refs_1_ = s16[144,512]{1,0:T(8,128)(2,1)S(1)} collective-permute-done((s16[144,512]{1,0:T(8,128)(2,1)}, s16[144,512]{1,0:T(8,128)(2,1)S(1)}, u32[]{:S(2)}, u32[]{:S(2)}) %collective-permute-start.52) | collective-permute-done | bytes 147488 | tf_op jit(solution)/shard_map/ppermute | solution.py:632
  238.4 0.7 copy-done.36
  239.1 2.0 line_sums.1
  241.1 6.6 %collective-permute-done.54 = f32[2,64,512]{2,1,0:T(8,128)S(1)} collective-permute-done((f32[2,64,512]{2,1,0:T(8,128)}, f32[2,64,512]{2,1,0:T(8,128)S(1)}, u32[]{:S(2)}, u32[]{:S(2)}) %collective-permute-start.54) | collective-permute-done | bytes 262176 | tf_op jit(solution)/shard_map/ppermute | solution.py:635
  247.6 1.1 maximum_select_fusion.1
  249.1 3.4 collective-permute-start.43
  252.5 0.9 collective-permute-start.41
  253.4 3.0 collective-permute-start.42
  256.4 2.7 collective-permute-start.14
  259.1 1.4 maximum_select_fusion.mine
  260.6 4.9 %collective-permute-done.43.far = s16[528,512]{1,0:T(8,128)(2,1)S(1)} collective-permute-done((s16[528,512]{1,0:T(8,128)(2,1)}, s16[528,512]{1,0:T(8,128)(2,1)S(1)}, u32[]{:S(2)}, u32[]{:S(2)}) %collective-permute-start.43) | collective-permute-done | bytes 540704 | tf_op jit(solution)/shard_map/ppermute | solution.py:621
  265.4 0.7 collective-permute-start.12
  266.2 2.6 join_far.3
  268.9 17.7 %collective-permute-done.14.far = s16[528,512]{1,0:T(8,128)(2,1)} collective-permute-done((s16[528,512]{1,0:T(8,128)(2,1)}, s16[528,512]{1,0:T(8,128)(2,1)}, u32[]{:S(2)}, u32[]{:S(2)}) %collective-permute-start.14) | collective-permute-done | bytes 540704 | tf_op jit(solution)/shard_map/ppermute | solution.py:621
  286.6 4.3 %collective-permute-start.44 = (s16[528,512]{1,0:T(8,128)(2,1)}, s16[528,512]{1,0:T(8,128)(2,1)}, u32[]{:S(2)}, u32[]{:S(2)}) collective-permute-start(s16[528,512]{1,0:T(8,128)(2,1)} %join_far.3), channel_id=1, source_target_pairs={{4,0},{5,1},{6,2},{7,3},{0,4},{1,5},{2,6},{3,7},{12,8},{13,9},{14,... | collective-permute-start | bytes 1622024 | tf_op jit(solution)/shard_map/ppermute | solution.py:624
  290.8 2.7 join_far.2
  293.6 1.1 collective-permute-start.15
  294.7 21.8 %collective-permute-done.44.refs_2_.refs_5_ = s16[528,512]{1,0:T(8,128)(2,1)} collective-permute-done((s16[528,512]{1,0:T(8,128)(2,1)}, s16[528,512]{1,0:T(8,128)(2,1)}, u32[]{:S(2)}, u32[]{:S(2)}) %collective-permute-start.44) | collective-permute-done | bytes 540704 | tf_op jit(solution)/shard_map/ppermute | solution.py:624
  316.5 2.7 final_sums.2.refs_6_
  319.3 17.1 %collective-permute-done.15.refs_2_.refs_5_ = s16[528,512]{1,0:T(8,128)(2,1)} collective-permute-done((s16[528,512]{1,0:T(8,128)(2,1)}, s16[528,512]{1,0:T(8,128)(2,1)}, u32[]{:S(2)}, u32[]{:S(2)}) %collective-permute-start.15) | collective-permute-done | bytes 540704 | tf_op jit(solution)/shard_map/ppermute | solution.py:624
  336.5 2.7 final_sums.3
  339.2 3.9 %place_halves.1 = f32[2,512,512]{2,1,0:T(8,128)} custom-call(s32[1]{0:T(128)} %bitcast.9.parity, f32[2,256,512]{2,1,0:T(8,128)} %copy-done.3, f32[2,256,512]{2,1,0:T(8,128)} %collective-permute-done.56.other), custom_call_target="tpu_custom_call" | custom-call | bytes 4000000 | tf_op jit(solution)/shard_map/place_halves/pallas_call | solution.py:543
  (174 shorter events, 9.6 us)
Async XLA Ops:
  13.9 137.6 %collective-permute-start = (bf16[2048,3328]{1,0:T(8,128)(2,1)}, bf16[2048,3328]{1,0:T(8,128)(2,1)}, u32[]{:S(2)}, u32[]{:S(2)}) collective-permute-start(bf16[2048,3328]{1,0:T(8,128)(2,1)} %pack_strips.2), channel_id=1, source_target_pairs={{1,0},{0,1},{3,2},{2,3},{5,4},{4,5},{7,6},{6,7},{9,8},{8,9},{11,10... | collective-permute-start | bytes 40894472 | tf_op jit(solution)/shard_map/ppermute | solution.py:617
  25.1 155.7 %collective-permute-start.16 = (bf16[2048,3328]{1,0:T(8,128)(2,1)}, bf16[2048,3328]{1,0:T(8,128)(2,1)}, u32[]{:S(2)}, u32[]{:S(2)}) collective-permute-start(bf16[2048,3328]{1,0:T(8,128)(2,1)} %pack_strips.3), channel_id=1, source_target_pairs={{1,0},{0,1},{3,2},{2,3},{5,4},{4,5},{7,6},{6,7},{9,8},{8,9},{11,10... | collective-permute-start | bytes 40894472 | tf_op jit(solution)/shard_map/ppermute | solution.py:617
  25.3 11.9 %collective-permute-start.2 = (bf16[8,32,512]{2,1,0:T(8,128)(2,1)S(1)}, bf16[8,32,512]{2,1,0:T(8,128)(2,1)S(1)}, u32[]{:S(2)}, u32[]{:S(2)}) collective-permute-start(bf16[8,32,512]{2,1,0:T(8,128)(2,1)S(1)} %get-tuple-element.34), channel_id=1, source_target_pairs={{2,0},{3,1},{4,2},{5,3},{6,4},{7,5},{0,6},{1,7},{10,8},{11,9},{12,... | collective-permute-start | bytes 786440 | tf_op jit(solution)/shard_map/ppermute | solution.py:598
  30.4 24.3 %collective-permute-start.3 = (bf16[8,32,512]{2,1,0:T(8,128)(2,1)S(1)}, bf16[8,32,512]{2,1,0:T(8,128)(2,1)S(1)}, u32[]{:S(2)}, u32[]{:S(2)}) collective-permute-start(bf16[8,32,512]{2,1,0:T(8,128)(2,1)S(1)} %get-tuple-element.34), channel_id=1, source_target_pairs={{4,0},{5,1},{6,2},{7,3},{0,4},{1,5},{2,6},{3,7},{12,8},{13,9},{14,... | collective-permute-start | bytes 786440 | tf_op jit(solution)/shard_map/ppermute | solution.py:598
  30.4 24.3 %collective-permute-start.4 = (bf16[8,32,512]{2,1,0:T(8,128)(2,1)S(1)}, bf16[8,32,512]{2,1,0:T(8,128)(2,1)S(1)}, u32[]{:S(2)}, u32[]{:S(2)}) collective-permute-start(bf16[8,32,512]{2,1,0:T(8,128)(2,1)S(1)} %get-tuple-element.34), channel_id=1, source_target_pairs={{6,0},{7,1},{0,2},{1,3},{2,4},{3,5},{4,6},{5,7},{14,8},{15,9},{8,1... | collective-permute-start | bytes 786440 | tf_op jit(solution)/shard_map/ppermute | solution.py:598
  37.2 28.7 %collective-permute-start.17 = (bf16[8,32,512]{2,1,0:T(8,128)(2,1)S(1)}, bf16[8,32,512]{2,1,0:T(8,128)(2,1)S(1)}, u32[]{:S(2)}, u32[]{:S(2)}) collective-permute-start(bf16[8,32,512]{2,1,0:T(8,128)(2,1)S(1)} %get-tuple-element.33), channel_id=1, source_target_pairs={{2,0},{3,1},{4,2},{5,3},{6,4},{7,5},{0,6},{1,7},{10,8},{11,9},{12,... | collective-permute-start | bytes 786440 | tf_op jit(solution)/shard_map/ppermute | solution.py:598
  54.7 20.7 %collective-permute-start.25 = (bf16[8,32,512]{2,1,0:T(8,128)(2,1)S(1)}, bf16[8,32,512]{2,1,0:T(8,128)(2,1)S(1)}, u32[]{:S(2)}, u32[]{:S(2)}) collective-permute-start(bf16[8,32,512]{2,1,0:T(8,128)(2,1)S(1)} %get-tuple-element.33), channel_id=1, source_target_pairs={{4,0},{5,1},{6,2},{7,3},{0,4},{1,5},{2,6},{3,7},{12,8},{13,9},{14,... | collective-permute-start | bytes 786440 | tf_op jit(solution)/shard_map/ppermute | solution.py:598
  54.7 20.7 %collective-permute-start.33 = (bf16[8,32,512]{2,1,0:T(8,128)(2,1)S(1)}, bf16[8,32,512]{2,1,0:T(8,128)(2,1)S(1)}, u32[]{:S(2)}, u32[]{:S(2)}) collective-permute-start(bf16[8,32,512]{2,1,0:T(8,128)(2,1)S(1)} %get-tuple-element.33), channel_id=1, source_target_pairs={{6,0},{7,1},{0,2},{1,3},{2,4},{3,5},{4,6},{5,7},{14,8},{15,9},{8,1... | collective-permute-start | bytes 786440 | tf_op jit(solution)/shard_map/ppermute | solution.py:598
  65.8 105.6 %copy-start.15 = (bf16[8,32,512]{2,1,0:T(8,128)(2,1)}, bf16[8,32,512]{2,1,0:T(8,128)(2,1)S(1)}, u32[]{:S(2)}) copy-start(bf16[8,32,512]{2,1,0:T(8,128)(2,1)S(1)} %collective-permute-done.17.refs_2_) | copy-start | bytes 786436
  65.8 11.6 %collective-permute-start.18 = (bf16[8,32,512]{2,1,0:T(8,128)(2,1)S(1)}, bf16[8,32,512]{2,1,0:T(8,128)(2,1)S(1)}, u32[]{:S(2)}, u32[]{:S(2)}) collective-permute-start(bf16[8,32,512]{2,1,0:T(8,128)(2,1)S(1)} %collective-permute-done.17.refs_2_), channel_id=1, source_target_pairs={{8,0},{17,1},{10,2},{19,3},{12,4},{21,5},{14,6},{23,7},{0,8},{25,9... | collective-permute-start | bytes 786440 | tf_op jit(solution)/shard_map/ppermute | solution.py:610
  75.4 96.0 %copy-start.16 = (bf16[8,32,512]{2,1,0:T(8,128)(2,1)}, bf16[8,32,512]{2,1,0:T(8,128)(2,1)S(1)}, u32[]{:S(2)}) copy-start(bf16[8,32,512]{2,1,0:T(8,128)(2,1)S(1)} %collective-permute-done.25.refs_10_) | copy-start | bytes 786436
  75.4 9.3 %collective-permute-start.26 = (bf16[8,32,512]{2,1,0:T(8,128)(2,1)S(1)}, bf16[8,32,512]{2,1,0:T(8,128)(2,1)}, u32[]{:S(2)}, u32[]{:S(2)}) collective-permute-start(bf16[8,32,512]{2,1,0:T(8,128)(2,1)S(1)} %collective-permute-done.25.refs_10_), channel_id=1, source_target_pairs={{8,0},{17,1},{10,2},{19,3},{12,4},{21,5},{14,6},{23,7},{0,8},{25,9... | collective-permute-start | bytes 786440 | tf_op jit(solution)/shard_map/ppermute | solution.py:610
  75.4 76.1 %copy-start.17 = (bf16[8,32,512]{2,1,0:T(8,128)(2,1)}, bf16[8,32,512]{2,1,0:T(8,128)(2,1)S(1)}, u32[]{:S(2)}) copy-start(bf16[8,32,512]{2,1,0:T(8,128)(2,1)S(1)} %collective-permute-done.33.refs_18_) | copy-start | bytes 786436
  75.4 14.9 %collective-permute-start.34 = (bf16[8,32,512]{2,1,0:T(8,128)(2,1)S(1)}, bf16[8,32,512]{2,1,0:T(8,128)(2,1)}, u32[]{:S(2)}, u32[]{:S(2)}) collective-permute-start(bf16[8,32,512]{2,1,0:T(8,128)(2,1)S(1)} %collective-permute-done.33.refs_18_), channel_id=1, source_target_pairs={{8,0},{17,1},{10,2},{19,3},{12,4},{21,5},{14,6},{23,7},{0,8},{25,9... | collective-permute-start | bytes 786440 | tf_op jit(solution)/shard_map/ppermute | solution.py:610
  77.4 74.1 %copy-start.18 = (bf16[8,32,512]{2,1,0:T(8,128)(2,1)}, bf16[8,32,512]{2,1,0:T(8,128)(2,1)S(1)}, u32[]{:S(2)}) copy-start(bf16[8,32,512]{2,1,0:T(8,128)(2,1)S(1)} %collective-permute-done.18.refs_3_) | copy-start | bytes 786436
  77.4 12.9 %collective-permute-start.19 = (bf16[8,32,512]{2,1,0:T(8,128)(2,1)S(1)}, bf16[8,32,512]{2,1,0:T(8,128)(2,1)}, u32[]{:S(2)}, u32[]{:S(2)}) collective-permute-start(bf16[8,32,512]{2,1,0:T(8,128)(2,1)S(1)} %collective-permute-done.17.refs_2_), channel_id=1, source_target_pairs={{16,0},{9,1},{18,2},{11,3},{20,4},{13,5},{22,6},{15,7},{24,8},{1,9... | collective-permute-start | bytes 786440 | tf_op jit(solution)/shard_map/ppermute | solution.py:610
  84.7 6.5 %collective-permute-start.27 = (bf16[8,32,512]{2,1,0:T(8,128)(2,1)S(1)}, bf16[8,32,512]{2,1,0:T(8,128)(2,1)}, u32[]{:S(2)}, u32[]{:S(2)}) collective-permute-start(bf16[8,32,512]{2,1,0:T(8,128)(2,1)S(1)} %collective-permute-done.25.refs_10_), channel_id=1, source_target_pairs={{16,0},{9,1},{18,2},{11,3},{20,4},{13,5},{22,6},{15,7},{24,8},{1,9... | collective-permute-start | bytes 786440 | tf_op jit(solution)/shard_map/ppermute | solution.py:610
  90.3 6.4 %collective-permute-start.35 = (bf16[8,32,512]{2,1,0:T(8,128)(2,1)S(1)}, bf16[8,32,512]{2,1,0:T(8,128)(2,1)S(1)}, u32[]{:S(2)}, u32[]{:S(2)}) collective-permute-start(bf16[8,32,512]{2,1,0:T(8,128)(2,1)S(1)} %collective-permute-done.33.refs_18_), channel_id=1, source_target_pairs={{16,0},{9,1},{18,2},{11,3},{20,4},{13,5},{22,6},{15,7},{24,8},{1,9... | collective-permute-start | bytes 786440 | tf_op jit(solution)/shard_map/ppermute | solution.py:610
  90.3 7.1 %collective-permute-start.21 = (bf16[8,32,512]{2,1,0:T(8,128)(2,1)S(1)}, bf16[8,32,512]{2,1,0:T(8,128)(2,1)S(1)}, u32[]{:S(2)}, u32[]{:S(2)}) collective-permute-start(bf16[8,32,512]{2,1,0:T(8,128)(2,1)S(1)} %collective-permute-done.17.refs_2_), channel_id=1, source_target_pairs={{1,0},{0,1},{3,2},{2,3},{5,4},{4,5},{7,6},{6,7},{9,8},{8,9},{11,10... | collective-permute-start | bytes 786440 | tf_op jit(solution)/shard_map/ppermute | solution.py:611
  91.2 6.4 %collective-permute-start.29 = (bf16[8,32,512]{2,1,0:T(8,128)(2,1)S(1)}, bf16[8,32,512]{2,1,0:T(8,128)(2,1)S(1)}, u32[]{:S(2)}, u32[]{:S(2)}) collective-permute-start(bf16[8,32,512]{2,1,0:T(8,128)(2,1)S(1)} %collective-permute-done.25.refs_10_), channel_id=1, source_target_pairs={{1,0},{0,1},{3,2},{2,3},{5,4},{4,5},{7,6},{6,7},{9,8},{8,9},{11,10... | collective-permute-start | bytes 786440 | tf_op jit(solution)/shard_map/ppermute | solution.py:611
  97.4 2.2 collective-permute-start.37
  97.4 54.1 %copy-start.20 = (bf16[8,32,512]{2,1,0:T(8,128)(2,1)}, bf16[8,32,512]{2,1,0:T(8,128)(2,1)S(1)}, u32[]{:S(2)}) copy-start(bf16[8,32,512]{2,1,0:T(8,128)(2,1)S(1)} %collective-permute-done.21.refs_6_) | copy-start | bytes 786436
  97.4 6.4 %collective-permute-start.20 = (bf16[8,32,512]{2,1,0:T(8,128)(2,1)S(1)}, bf16[8,32,512]{2,1,0:T(8,128)(2,1)S(1)}, u32[]{:S(2)}, u32[]{:S(2)}) collective-permute-start(bf16[8,32,512]{2,1,0:T(8,128)(2,1)S(1)} %collective-permute-done.18.refs_3_), channel_id=1, source_target_pairs={{16,0},{9,1},{18,2},{11,3},{20,4},{13,5},{22,6},{15,7},{24,8},{1,9... | collective-permute-start | bytes 786440 | tf_op jit(solution)/shard_map/ppermute | solution.py:610
  97.5 54.0 %copy-start.21 = (bf16[8,32,512]{2,1,0:T(8,128)(2,1)}, bf16[8,32,512]{2,1,0:T(8,128)(2,1)S(1)}, u32[]{:S(2)}) copy-start(bf16[8,32,512]{2,1,0:T(8,128)(2,1)S(1)} %collective-permute-done.29.refs_14_) | copy-start | bytes 786436
  97.5 9.1 %collective-permute-start.28 = (bf16[8,32,512]{2,1,0:T(8,128)(2,1)}, bf16[8,32,512]{2,1,0:T(8,128)(2,1)S(1)}, u32[]{:S(2)}, u32[]{:S(2)}) collective-permute-start(bf16[8,32,512]{2,1,0:T(8,128)(2,1)} %collective-permute-done.26.refs_11_), channel_id=1, source_target_pairs={{16,0},{9,1},{18,2},{11,3},{20,4},{13,5},{22,6},{15,7},{24,8},{1,9... | collective-permute-start | bytes 786440 | tf_op jit(solution)/shard_map/ppermute | solution.py:610
  99.6 52.4 %copy-start.2 = (bf16[24,32,512]{2,1,0:T(8,128)(2,1)}, bf16[24,32,512]{2,1,0:T(8,128)(2,1)S(1)}, u32[]{:S(2)}) copy-start(bf16[24,32,512]{2,1,0:T(8,128)(2,1)S(1)} %constant_dynamic-update-slice_fusion.refs_2_) | copy-start | bytes 2359300
  99.6 19.9 %collective-permute-start.6 = (bf16[24,32,512]{2,1,0:T(8,128)(2,1)S(1)}, bf16[24,32,512]{2,1,0:T(8,128)(2,1)S(1)}, u32[]{:S(2)}, u32[]{:S(2)}) collective-permute-start(bf16[24,32,512]{2,1,0:T(8,128)(2,1)S(1)} %constant_dynamic-update-slice_fusion.refs_2_), channel_id=1, source_target_pairs={{16,0},{9,1},{18,2},{11,3},{20,4},{13,5},{22,6},{15,7},{24,8},{1,9... | collective-permute-start | bytes 2359304 | tf_op jit(solution)/shard_map/ppermute | solution.py:610
  103.9 14.1 %collective-permute-start.36 = (bf16[8,32,512]{2,1,0:T(8,128)(2,1)}, bf16[8,32,512]{2,1,0:T(8,128)(2,1)}, u32[]{:S(2)}, u32[]{:S(2)}) collective-permute-start(bf16[8,32,512]{2,1,0:T(8,128)(2,1)} %collective-permute-done.34.refs_19_), channel_id=1, source_target_pairs={{16,0},{9,1},{18,2},{11,3},{20,4},{13,5},{22,6},{15,7},{24,8},{1,9... | collective-permute-start | bytes 786440 | tf_op jit(solution)/shard_map/ppermute | solution.py:610
  106.7 11.3 %collective-permute-start.22 = (bf16[8,32,512]{2,1,0:T(8,128)(2,1)S(1)}, bf16[8,32,512]{2,1,0:T(8,128)(2,1)}, u32[]{:S(2)}, u32[]{:S(2)}) collective-permute-start(bf16[8,32,512]{2,1,0:T(8,128)(2,1)S(1)} %collective-permute-done.18.refs_3_), channel_id=1, source_target_pairs={{1,0},{0,1},{3,2},{2,3},{5,4},{4,5},{7,6},{6,7},{9,8},{8,9},{11,10... | collective-permute-start | bytes 786440 | tf_op jit(solution)/shard_map/ppermute | solution.py:611
  118.0 20.1 %collective-permute-start.7 = (bf16[24,32,512]{2,1,0:T(8,128)(2,1)S(1)}, bf16[24,32,512]{2,1,0:T(8,128)(2,1)S(1)}, u32[]{:S(2)}, u32[]{:S(2)}) collective-permute-start(bf16[24,32,512]{2,1,0:T(8,128)(2,1)S(1)} %constant_dynamic-update-slice_fusion.refs_2_), channel_id=1, source_target_pairs={{24,0},{25,1},{26,2},{27,3},{28,4},{29,5},{30,6},{31,7},{16,8},{17... | collective-permute-start | bytes 2359304 | tf_op jit(solution)/shard_map/ppermute | solution.py:610
  118.0 27.0 %collective-permute-start.5 = (bf16[24,32,512]{2,1,0:T(8,128)(2,1)S(1)}, bf16[24,32,512]{2,1,0:T(8,128)(2,1)S(1)}, u32[]{:S(2)}, u32[]{:S(2)}) collective-permute-start(bf16[24,32,512]{2,1,0:T(8,128)(2,1)S(1)} %constant_dynamic-update-slice_fusion.refs_2_), channel_id=1, source_target_pairs={{8,0},{17,1},{10,2},{19,3},{12,4},{21,5},{14,6},{23,7},{0,8},{25,9... | collective-permute-start | bytes 2359304 | tf_op jit(solution)/shard_map/ppermute | solution.py:610
  119.5 30.5 %collective-permute-start.1 = (bf16[16,128,512]{2,1,0:T(8,128)(2,1)S(1)}, bf16[16,128,512]{2,1,0:T(8,128)(2,1)S(1)}, u32[]{:S(2)}, u32[]{:S(2)}) collective-permute-start(bf16[16,128,512]{2,1,0:T(8,128)(2,1)S(1)} %bitcast.23), channel_id=1, source_target_pairs={{1,0},{0,1},{3,2},{2,3},{5,4},{4,5},{7,6},{6,7},{9,8},{8,9},{11,10... | collective-permute-start | bytes 6291464 | tf_op jit(solution)/shard_map/ppermute | solution.py:593
  138.1 7.3 %collective-permute-start.8 = (bf16[24,32,512]{2,1,0:T(8,128)(2,1)S(1)}, bf16[24,32,512]{2,1,0:T(8,128)(2,1)S(1)}, u32[]{:S(2)}, u32[]{:S(2)}) collective-permute-start(bf16[24,32,512]{2,1,0:T(8,128)(2,1)S(1)} %constant_dynamic-update-slice_fusion.refs_2_), channel_id=1, source_target_pairs={{1,0},{0,1},{3,2},{2,3},{5,4},{4,5},{7,6},{6,7},{9,8},{8,9},{11,10... | collective-permute-start | bytes 2359304 | tf_op jit(solution)/shard_map/ppermute | solution.py:611
  145.0 2.3 collective-permute-start.10
  145.4 3.1 collective-permute-start.11
  147.3 2.3 collective-permute-start.9
  148.5 23.0 %collective-permute-start.30 = (bf16[8,32,512]{2,1,0:T(8,128)(2,1)}, bf16[8,32,512]{2,1,0:T(8,128)(2,1)}, u32[]{:S(2)}, u32[]{:S(2)}) collective-permute-start(bf16[8,32,512]{2,1,0:T(8,128)(2,1)} %collective-permute-done.26.refs_11_), channel_id=1, source_target_pairs={{1,0},{0,1},{3,2},{2,3},{5,4},{4,5},{7,6},{6,7},{9,8},{8,9},{11,10... | collective-permute-start | bytes 786440 | tf_op jit(solution)/shard_map/ppermute | solution.py:611
  149.6 22.1 %collective-permute-start.38 = (bf16[8,32,512]{2,1,0:T(8,128)(2,1)}, bf16[8,32,512]{2,1,0:T(8,128)(2,1)}, u32[]{:S(2)}, u32[]{:S(2)}) collective-permute-start(bf16[8,32,512]{2,1,0:T(8,128)(2,1)} %collective-permute-done.34.refs_19_), channel_id=1, source_target_pairs={{1,0},{0,1},{3,2},{2,3},{5,4},{4,5},{7,6},{6,7},{9,8},{8,9},{11,10... | collective-permute-start | bytes 786440 | tf_op jit(solution)/shard_map/ppermute | solution.py:611
  151.3 20.7 %collective-permute-start.23 = (bf16[8,32,512]{2,1,0:T(8,128)(2,1)}, bf16[8,32,512]{2,1,0:T(8,128)(2,1)S(1)}, u32[]{:S(2)}, u32[]{:S(2)}) collective-permute-start(bf16[8,32,512]{2,1,0:T(8,128)(2,1)} %collective-permute-done.19.refs_4_), channel_id=1, source_target_pairs={{1,0},{0,1},{3,2},{2,3},{5,4},{4,5},{7,6},{6,7},{9,8},{8,9},{11,10... | collective-permute-start | bytes 786440 | tf_op jit(solution)/shard_map/ppermute | solution.py:611
  151.7 20.6 %collective-permute-start.31 = (bf16[8,32,512]{2,1,0:T(8,128)(2,1)}, bf16[8,32,512]{2,1,0:T(8,128)(2,1)S(1)}, u32[]{:S(2)}, u32[]{:S(2)}) collective-permute-start(bf16[8,32,512]{2,1,0:T(8,128)(2,1)} %collective-permute-done.27.refs_12_), channel_id=1, source_target_pairs={{1,0},{0,1},{3,2},{2,3},{5,4},{4,5},{7,6},{6,7},{9,8},{8,9},{11,10... | collective-permute-start | bytes 786440 | tf_op jit(solution)/shard_map/ppermute | solution.py:611
  171.4 9.0 %collective-permute-start.39 = (bf16[8,32,512]{2,1,0:T(8,128)(2,1)}, bf16[8,32,512]{2,1,0:T(8,128)(2,1)S(1)}, u32[]{:S(2)}, u32[]{:S(2)}) collective-permute-start(bf16[8,32,512]{2,1,0:T(8,128)(2,1)} %copy-done.19), channel_id=1, source_target_pairs={{1,0},{0,1},{3,2},{2,3},{5,4},{4,5},{7,6},{6,7},{9,8},{8,9},{11,10... | collective-permute-start | bytes 786440 | tf_op jit(solution)/shard_map/ppermute | solution.py:611
  171.7 9.0 %collective-permute-start.24 = (bf16[8,32,512]{2,1,0:T(8,128)(2,1)S(1)}, bf16[8,32,512]{2,1,0:T(8,128)(2,1)S(1)}, u32[]{:S(2)}, u32[]{:S(2)}) collective-permute-start(bf16[8,32,512]{2,1,0:T(8,128)(2,1)S(1)} %copy-done.24), channel_id=1, source_target_pairs={{1,0},{0,1},{3,2},{2,3},{5,4},{4,5},{7,6},{6,7},{9,8},{8,9},{11,10... | collective-permute-start | bytes 786440 | tf_op jit(solution)/shard_map/ppermute | solution.py:611
  172.0 8.7 %collective-permute-start.32 = (bf16[8,32,512]{2,1,0:T(8,128)(2,1)S(1)}, bf16[8,32,512]{2,1,0:T(8,128)(2,1)S(1)}, u32[]{:S(2)}, u32[]{:S(2)}) collective-permute-start(bf16[8,32,512]{2,1,0:T(8,128)(2,1)S(1)} %copy-done.26), channel_id=1, source_target_pairs={{1,0},{0,1},{3,2},{2,3},{5,4},{4,5},{7,6},{6,7},{9,8},{8,9},{11,10... | collective-permute-start | bytes 786440 | tf_op jit(solution)/shard_map/ppermute | solution.py:611
  172.3 8.5 %collective-permute-start.40 = (bf16[8,32,512]{2,1,0:T(8,128)(2,1)}, bf16[8,32,512]{2,1,0:T(8,128)(2,1)S(1)}, u32[]{:S(2)}, u32[]{:S(2)}) collective-permute-start(bf16[8,32,512]{2,1,0:T(8,128)(2,1)} %collective-permute-done.36.refs_21_), channel_id=1, source_target_pairs={{1,0},{0,1},{3,2},{2,3},{5,4},{4,5},{7,6},{6,7},{9,8},{8,9},{11,10... | collective-permute-start | bytes 786440 | tf_op jit(solution)/shard_map/ppermute | solution.py:611
  180.5 28.8 %collective-permute-start.48 = (f32[256,512]{1,0:T(8,128)}, f32[256,512]{1,0:T(8,128)S(1)}, u32[]{:S(2)}, u32[]{:S(2)}) collective-permute-start(f32[256,512]{1,0:T(8,128)} %get-tuple-element.23), channel_id=1, source_target_pairs={{1,0},{0,1},{3,2},{2,3},{5,4},{4,5},{7,6},{6,7},{9,8},{8,9},{11,10... | collective-permute-start | bytes 1572872 | tf_op jit(solution)/shard_map/ppermute | solution.py:478
  209.0 2.2 collective-permute-start.45
  209.3 6.4 %collective-permute-start.49 = (f32[128,512]{1,0:T(8,128)S(1)}, f32[128,512]{1,0:T(8,128)S(1)}, u32[]{:S(2)}, u32[]{:S(2)}) collective-permute-start(f32[128,512]{1,0:T(8,128)S(1)} %get-tuple-element.36), channel_id=1, source_target_pairs={{8,0},{17,1},{10,2},{19,3},{12,4},{21,5},{14,6},{23,7},{0,8},{25,9... | collective-permute-start | bytes 786440 | tf_op jit(solution)/shard_map/ppermute | solution.py:483
  212.3 6.6 %collective-permute-start.46 = (f32[128,512]{1,0:T(8,128)S(1)}, f32[128,512]{1,0:T(8,128)S(1)}, u32[]{:S(2)}, u32[]{:S(2)}) collective-permute-start(f32[128,512]{1,0:T(8,128)S(1)} %get-tuple-element.38), channel_id=1, source_target_pairs={{8,0},{17,1},{10,2},{19,3},{12,4},{21,5},{14,6},{23,7},{0,8},{25,9... | collective-permute-start | bytes 786440 | tf_op jit(solution)/shard_map/ppermute | solution.py:483
  216.5 5.0 %collective-permute-start.50 = (f32[64,512]{1,0:T(8,128)S(1)}, f32[64,512]{1,0:T(8,128)S(1)}, u32[]{:S(2)}, u32[]{:S(2)}) collective-permute-start(f32[64,512]{1,0:T(8,128)S(1)} %get-tuple-element.39), channel_id=1, source_target_pairs={{16,0},{9,1},{18,2},{11,3},{20,4},{13,5},{22,6},{15,7},{24,8},{1,9... | collective-permute-start | bytes 393224 | tf_op jit(solution)/shard_map/ppermute | solution.py:483
  219.6 5.0 %collective-permute-start.47 = (f32[64,512]{1,0:T(8,128)S(1)}, f32[64,512]{1,0:T(8,128)S(1)}, u32[]{:S(2)}, u32[]{:S(2)}) collective-permute-start(f32[64,512]{1,0:T(8,128)S(1)} %get-tuple-element.41), channel_id=1, source_target_pairs={{16,0},{9,1},{18,2},{11,3},{20,4},{13,5},{22,6},{15,7},{24,8},{1,9... | collective-permute-start | bytes 393224 | tf_op jit(solution)/shard_map/ppermute | solution.py:483
  227.0 6.9 %collective-permute-start.51 = (s16[144,512]{1,0:T(8,128)(2,1)}, s16[144,512]{1,0:T(8,128)(2,1)S(1)}, u32[]{:S(2)}, u32[]{:S(2)}) collective-permute-start(s16[144,512]{1,0:T(8,128)(2,1)} %get-tuple-element.25), channel_id=1, source_target_pairs={{2,0},{3,1},{4,2},{5,3},{6,4},{7,5},{0,6},{1,7},{10,8},{11,9},{12,... | collective-permute-start | bytes 442376 | tf_op jit(solution)/shard_map/ppermute | solution.py:632
  227.1 11.3 %collective-permute-start.52 = (s16[144,512]{1,0:T(8,128)(2,1)}, s16[144,512]{1,0:T(8,128)(2,1)S(1)}, u32[]{:S(2)}, u32[]{:S(2)}) collective-permute-start(s16[144,512]{1,0:T(8,128)(2,1)} %get-tuple-element.25), channel_id=1, source_target_pairs={{4,0},{5,1},{6,2},{7,3},{0,4},{1,5},{2,6},{3,7},{12,8},{13,9},{14,... | collective-permute-start | bytes 442376 | tf_op jit(solution)/shard_map/ppermute | solution.py:632
  227.1 11.3 %collective-permute-start.53 = (s16[144,512]{1,0:T(8,128)(2,1)}, s16[144,512]{1,0:T(8,128)(2,1)S(1)}, u32[]{:S(2)}, u32[]{:S(2)}) collective-permute-start(s16[144,512]{1,0:T(8,128)(2,1)} %get-tuple-element.25), channel_id=1, source_target_pairs={{6,0},{7,1},{0,2},{1,3},{2,4},{3,5},{4,6},{5,7},{14,8},{15,9},{8,1... | collective-permute-start | bytes 442376 | tf_op jit(solution)/shard_map/ppermute | solution.py:632
  241.1 6.6 %collective-permute-start.54 = (f32[2,64,512]{2,1,0:T(8,128)}, f32[2,64,512]{2,1,0:T(8,128)S(1)}, u32[]{:S(2)}, u32[]{:S(2)}) collective-permute-start(f32[2,64,512]{2,1,0:T(8,128)} %line_sums.1), channel_id=1, source_target_pairs={{16,0},{9,1},{18,2},{11,3},{20,4},{13,5},{22,6},{15,7},{24,8},{1,9... | collective-permute-start | bytes 786440 | tf_op jit(solution)/shard_map/ppermute | solution.py:635
  248.7 10.4 %collective-permute-start.55 = (f32[2,128,512]{2,1,0:T(8,128)S(1)}, f32[2,128,512]{2,1,0:T(8,128)}, u32[]{:S(2)}, u32[]{:S(2)}) collective-permute-start(f32[2,128,512]{2,1,0:T(8,128)S(1)} %maximum_select_fusion.1), channel_id=1, source_target_pairs={{8,0},{17,1},{10,2},{19,3},{12,4},{21,5},{14,6},{23,7},{0,8},{25,9... | collective-permute-start | bytes 1572872 | tf_op jit(solution)/shard_map/ppermute | solution.py:635
  249.1 16.4 %collective-permute-start.43 = (s16[528,512]{1,0:T(8,128)(2,1)}, s16[528,512]{1,0:T(8,128)(2,1)S(1)}, u32[]{:S(2)}, u32[]{:S(2)}) collective-permute-start(s16[528,512]{1,0:T(8,128)(2,1)} %get-tuple-element.18), channel_id=1, source_target_pairs={{0,2},{1,3},{6,4},{7,5},{8,10},{9,11},{14,12},{15,13},{16,18},{17,... | collective-permute-start | bytes 1622024 | tf_op jit(solution)/shard_map/ppermute | solution.py:621
  252.5 41.0 %collective-permute-start.41 = (s16[528,512]{1,0:T(8,128)(2,1)}, s16[528,512]{1,0:T(8,128)(2,1)S(1)}, u32[]{:S(2)}, u32[]{:S(2)}) collective-permute-start(s16[528,512]{1,0:T(8,128)(2,1)} %get-tuple-element.18), channel_id=1, source_target_pairs={{2,4},{3,5},{4,2},{5,3},{10,12},{11,13},{12,10},{13,11},{18,20},{1... | collective-permute-start | bytes 1622024 | tf_op jit(solution)/shard_map/ppermute | solution.py:622
  253.4 40.2 %collective-permute-start.42 = (s16[528,512]{1,0:T(8,128)(2,1)}, s16[528,512]{1,0:T(8,128)(2,1)S(1)}, u32[]{:S(2)}, u32[]{:S(2)}) collective-permute-start(s16[528,512]{1,0:T(8,128)(2,1)} %get-tuple-element.19), channel_id=1, source_target_pairs={{2,0},{3,1},{0,2},{1,3},{6,4},{7,5},{4,6},{5,7},{10,8},{11,9},{8,1... | collective-permute-start | bytes 1622024 | tf_op jit(solution)/shard_map/ppermute | solution.py:622
  256.4 30.2 %collective-permute-start.14 = (s16[528,512]{1,0:T(8,128)(2,1)}, s16[528,512]{1,0:T(8,128)(2,1)}, u32[]{:S(2)}, u32[]{:S(2)}) collective-permute-start(s16[528,512]{1,0:T(8,128)(2,1)} %get-tuple-element.15), channel_id=1, source_target_pairs={{0,2},{1,3},{6,4},{7,5},{8,10},{9,11},{14,12},{15,13},{16,18},{17,... | collective-permute-start | bytes 1622024 | tf_op jit(solution)/shard_map/ppermute | solution.py:621
  260.5 78.7 %collective-permute-start.56 = (f32[2,256,512]{2,1,0:T(8,128)S(1)}, f32[2,256,512]{2,1,0:T(8,128)}, u32[]{:S(2)}, u32[]{:S(2)}) collective-permute-start(f32[2,256,512]{2,1,0:T(8,128)S(1)} %maximum_select_fusion.mine), channel_id=1, source_target_pairs={{1,0},{0,1},{3,2},{2,3},{5,4},{4,5},{7,6},{6,7},{9,8},{8,9},{11,10... | collective-permute-start | bytes 3145736 | tf_op jit(solution)/shard_map/ppermute | solution.py:640
  265.4 53.8 %collective-permute-start.12 = (s16[528,512]{1,0:T(8,128)(2,1)}, s16[528,512]{1,0:T(8,128)(2,1)S(1)}, u32[]{:S(2)}, u32[]{:S(2)}) collective-permute-start(s16[528,512]{1,0:T(8,128)(2,1)} %get-tuple-element.15), channel_id=1, source_target_pairs={{2,4},{3,5},{4,2},{5,3},{10,12},{11,13},{12,10},{13,11},{18,20},{1... | collective-permute-start | bytes 1622024 | tf_op jit(solution)/shard_map/ppermute | solution.py:622
  286.6 30.0 %collective-permute-start.44 = (s16[528,512]{1,0:T(8,128)(2,1)}, s16[528,512]{1,0:T(8,128)(2,1)}, u32[]{:S(2)}, u32[]{:S(2)}) collective-permute-start(s16[528,512]{1,0:T(8,128)(2,1)} %join_far.3), channel_id=1, source_target_pairs={{4,0},{5,1},{6,2},{7,3},{0,4},{1,5},{2,6},{3,7},{12,8},{13,9},{14,... | collective-permute-start | bytes 1622024 | tf_op jit(solution)/shard_map/ppermute | solution.py:624
  293.5 25.8 %collective-permute-start.13 = (s16[528,512]{1,0:T(8,128)(2,1)}, s16[528,512]{1,0:T(8,128)(2,1)S(1)}, u32[]{:S(2)}, u32[]{:S(2)}) collective-permute-start(s16[528,512]{1,0:T(8,128)(2,1)} %get-tuple-element.16), channel_id=1, source_target_pairs={{2,0},{3,1},{0,2},{1,3},{6,4},{7,5},{4,6},{5,7},{10,8},{11,9},{8,1... | collective-permute-start | bytes 1622024 | tf_op jit(solution)/shard_map/ppermute | solution.py:622
  293.6 42.8 %collective-permute-start.15 = (s16[528,512]{1,0:T(8,128)(2,1)}, s16[528,512]{1,0:T(8,128)(2,1)}, u32[]{:S(2)}, u32[]{:S(2)}) collective-permute-start(s16[528,512]{1,0:T(8,128)(2,1)} %join_far.2), channel_id=1, source_target_pairs={{4,0},{5,1},{6,2},{7,3},{0,4},{1,5},{2,6},{3,7},{12,8},{13,9},{14,... | collective-permute-start | bytes 1622024 | tf_op jit(solution)/shard_map/ppermute | solution.py:624
  (33 other events, 416.6 us)

commit v4 on v3

--- a/solution.py
+++ b/solution.py
@@ -8,7 +8,7 @@
 from jax.sharding import PartitionSpec as P
 
 BS = 128
-GROUP = 8
+GROUP = 16
 TAIL = 16
 AXES = ("row", "col")
 
@@ -527,31 +527,31 @@
     )(total, *coded)
 
 
-def place_kernel(parity, mine, other, out):
-    @pl.when(pl.program_id(1) == parity[0])
-    def _():
-        out[...] = mine[...]
-
-    @pl.when(pl.program_id(1) != parity[0])
-    def _():
-        out[...] = other[...]
-
-
-def place_halves(parity, mine, other):
-    supernodes, rows, width = mine.shape
-    block = pl.BlockSpec((1, rows, width), lambda s, g, parity: (s, 0, 0))
+def place_kernel(at, piece, *refs):
+    refs[-1][...] = piece[...]
+
+
+def place_half(at, piece, earlier):
+    supernodes, rows, width = piece.shape
+    operands, aliases = [piece], {}
+    specs = [pl.BlockSpec(piece.shape, lambda g, at: (0, 0, 0))]
+    if earlier is not None:
+        aliases = {2: 0}
+        operands.append(earlier)
+        specs.append(pl.BlockSpec(memory_space=pl.ANY))
     return pl.pallas_call(
         place_kernel,
         out_shape=jax.ShapeDtypeStruct((supernodes, 2 * rows, width), jnp.float32),
         grid_spec=pltpu.PrefetchScalarGridSpec(
             num_scalar_prefetch=1,
-            grid=(supernodes, 2),
-            in_specs=[block, block],
-            out_specs=pl.BlockSpec((1, rows, width), lambda s, g, parity: (s, g, 0)),
+            grid=(1,),
+            in_specs=specs,
+            out_specs=pl.BlockSpec(piece.shape, lambda g, at: (0, at[0], 0)),
         ),
-        cost_estimate=pl.CostEstimate(flops=0, bytes_accessed=4 * 10**6, transcendentals=0),
-        name="place_halves",
-    )(parity, mine, other)
+        input_output_aliases=aliases,
+        cost_estimate=pl.CostEstimate(flops=0, bytes_accessed=2 * 10**6, transcendentals=0),
+        name="place_half",
+    )(at, *operands)
 
 
 def local(inverse, panels, block_slot, list_ids):
@@ -638,7 +638,8 @@
             low, jnp.concatenate([whole, other], axis=1), jnp.concatenate([other, whole], axis=1)
         )
     other = lax.ppermute(whole, "col", core_swap(n_col))
-    return out, place_halves((my_col % 2).reshape(1), whole, other)
+    diag = place_half((my_col % 2).reshape(1), whole, None)
+    return out, place_half((1 - my_col % 2).reshape(1), other, diag)
 
 
 def solution(mesh):

time: 344 us -> 342 us (level)
  no operation moved by 1% of the time
where the time goes in v4:
time: 342 us; the launch traced here: 341 us
  waiting for transfers between devices  185 us (54%)
  Pallas kernels  92.1 us (27%)
  starting transfers between devices  50.7 us (15%)
  other arithmetic  6.61 us (2%)
  local copies, waits for them, and re-layouts  5.63 us (2%)
    ppermute x12, waiting for transfers between devices, local(): pieces.append(lax.ppermute(source, AXES, pairs))  63 us
    ppermute x2, waiting for transfers between devices, local(): moved.append(lax.ppermute(joined, 'col', line_swap(n_col, 2)))  39 us
    pallas_call x2, Pallas kernels, products(): pl.pallas_call(functools.partial(product_kernel, dims, supernode, len(pie...  36 us
    ppermute x6, waiting for transfers between devices, local(): lax.ppermute(mine, 'col', line_shift(n_col, shift))  28.5 us
    ppermute x2, waiting for transfers between devices, local(): far = lax.ppermute(coded[3], 'col', inward(n_col))  22.7 us
    ppermute x6, starting transfers between devices, local(): lax.ppermute(mine, 'col', line_shift(n_col, shift))  21.6 us
    pallas_call x2, Pallas kernels, pack_strips(): pl.pallas_call(functools.partial(pack_kernel, dims), out_shape=jax.ShapeD...  21.2 us
    pallas_call x2, Pallas kernels, diag_terms(): pl.pallas_call(functools.partial(diag_kernel, dims, supernode, len(pieces...  15.8 us
  transfers between devices with their start and end apart: 57, of which 27 were waited for; matrix products, arithmetic and copies ran while one was open for 1% of the time, Pallas kernels for 22%

profile of v4, /device:TPU:0, one launch (start us, length us, event | category | flops | bytes accessed | tf_op | source)
XLA Modules:
  0.0 341.0 jit_solution(11212918265673053968)
XLA Ops:
  0.7 0.9 select_reduce_fusion
  3.4 10.6 %pack_strips.2 = bf16[2048,3328]{1,0:T(8,128)(2,1)} custom-call(s32[132]{0:T(256)} %bitcast.28, bf16[6656,3328]{1,0:T(8,128)(2,1)} %inverse.7), custom_call_target="tpu_custom_call" | custom-call | bytes 27000000 | tf_op jit(solution)/shard_map/pack_strips/pallas_call | solution.py:170
  14.5 10.6 %pack_strips.3 = bf16[2048,3328]{1,0:T(8,128)(2,1)} custom-call(s32[132]{0:T(256)} %bitcast.25, bf16[6656,3328]{1,0:T(8,128)(2,1)} %inverse.7), custom_call_target="tpu_custom_call" | custom-call | bytes 27000000 | tf_op jit(solution)/shard_map/pack_strips/pallas_call | solution.py:170
  25.3 5.1 %collective-permute-start.2 = (bf16[8,32,512]{2,1,0:T(8,128)(2,1)S(1)}, bf16[8,32,512]{2,1,0:T(8,128)(2,1)S(1)}, u32[]{:S(2)}, u32[]{:S(2)}) collective-permute-start(bf16[8,32,512]{2,1,0:T(8,128)(2,1)S(1)} %get-tuple-element.34), channel_id=1, source_target_pairs={{2,0},{3,1},{4,2},{5,3},{6,4},{7,5},{0,6},{1,7},{10,8},{11,9},{12,... | collective-permute-start | bytes 786440 | tf_op jit(solution)/shard_map/ppermute | solution.py:598
  30.4 1.0 collective-permute-start.4
  31.4 5.8 %collective-permute-done.2 = bf16[8,32,512]{2,1,0:T(8,128)(2,1)S(1)} collective-permute-done((bf16[8,32,512]{2,1,0:T(8,128)(2,1)S(1)}, bf16[8,32,512]{2,1,0:T(8,128)(2,1)S(1)}, u32[]{:S(2)}, u32[]{:S(2)}) %collective-permute-start.2) | collective-permute-done | bytes 262176 | tf_op jit(solution)/shard_map/ppermute | solution.py:598
  37.2 4.3 %collective-permute-start.17 = (bf16[8,32,512]{2,1,0:T(8,128)(2,1)S(1)}, bf16[8,32,512]{2,1,0:T(8,128)(2,1)S(1)}, u32[]{:S(2)}, u32[]{:S(2)}) collective-permute-start(bf16[8,32,512]{2,1,0:T(8,128)(2,1)S(1)} %get-tuple-element.33), channel_id=1, source_target_pairs={{2,0},{3,1},{4,2},{5,3},{6,4},{7,5},{0,6},{1,7},{10,8},{11,9},{12,... | collective-permute-start | bytes 786440 | tf_op jit(solution)/shard_map/ppermute | solution.py:598
  41.5 13.2 %collective-permute-done.3 = bf16[8,32,512]{2,1,0:T(8,128)(2,1)S(1)} collective-permute-done((bf16[8,32,512]{2,1,0:T(8,128)(2,1)S(1)}, bf16[8,32,512]{2,1,0:T(8,128)(2,1)S(1)}, u32[]{:S(2)}, u32[]{:S(2)}) %collective-permute-start.3) | collective-permute-done | bytes 262176 | tf_op jit(solution)/shard_map/ppermute | solution.py:598
  54.7 11.2 %collective-permute-start.33 = (bf16[8,32,512]{2,1,0:T(8,128)(2,1)S(1)}, bf16[8,32,512]{2,1,0:T(8,128)(2,1)S(1)}, u32[]{:S(2)}, u32[]{:S(2)}) collective-permute-start(bf16[8,32,512]{2,1,0:T(8,128)(2,1)S(1)} %get-tuple-element.33), channel_id=1, source_target_pairs={{6,0},{7,1},{0,2},{1,3},{2,4},{3,5},{4,6},{5,7},{14,8},{15,9},{8,1... | collective-permute-start | bytes 786440 | tf_op jit(solution)/shard_map/ppermute | solution.py:598
  65.8 9.6 %collective-permute-done.25.refs_10_ = bf16[8,32,512]{2,1,0:T(8,128)(2,1)S(1)} collective-permute-done((bf16[8,32,512]{2,1,0:T(8,128)(2,1)S(1)}, bf16[8,32,512]{2,1,0:T(8,128)(2,1)S(1)}, u32[]{:S(2)}, u32[]{:S(2)}) %collective-permute-start.25) | collective-permute-done | bytes 262176 | tf_op jit(solution)/shard_map/ppermute | solution.py:598
  75.4 2.0 collective-permute-start.34
  77.4 7.2 %collective-permute-done.26.refs_11_ = bf16[8,32,512]{2,1,0:T(8,128)(2,1)} collective-permute-done((bf16[8,32,512]{2,1,0:T(8,128)(2,1)S(1)}, bf16[8,32,512]{2,1,0:T(8,128)(2,1)}, u32[]{:S(2)}, u32[]{:S(2)}) %collective-permute-start.26) | collective-permute-done | bytes 262176 | tf_op jit(solution)/shard_map/ppermute | solution.py:610
  84.7 5.6 %collective-permute-done.34.refs_19_ = bf16[8,32,512]{2,1,0:T(8,128)(2,1)} collective-permute-done((bf16[8,32,512]{2,1,0:T(8,128)(2,1)S(1)}, bf16[8,32,512]{2,1,0:T(8,128)(2,1)}, u32[]{:S(2)}, u32[]{:S(2)}) %collective-permute-start.34) | collective-permute-done | bytes 262176 | tf_op jit(solution)/shard_map/ppermute | solution.py:610
  90.3 0.8 collective-permute-done.27.refs_12_
  91.2 5.5 %collective-permute-done.35.refs_20_ = bf16[8,32,512]{2,1,0:T(8,128)(2,1)S(1)} collective-permute-done((bf16[8,32,512]{2,1,0:T(8,128)(2,1)S(1)}, bf16[8,32,512]{2,1,0:T(8,128)(2,1)S(1)}, u32[]{:S(2)}, u32[]{:S(2)}) %collective-permute-start.35) | collective-permute-done | bytes 262176 | tf_op jit(solution)/shard_map/ppermute | solution.py:610
  96.7 0.7 copy-done.19
  97.5 2.0 collective-permute-start.28
  99.8 4.1 %collective-permute-done.20.refs_5_ = bf16[8,32,512]{2,1,0:T(8,128)(2,1)S(1)} collective-permute-done((bf16[8,32,512]{2,1,0:T(8,128)(2,1)S(1)}, bf16[8,32,512]{2,1,0:T(8,128)(2,1)S(1)}, u32[]{:S(2)}, u32[]{:S(2)}) %collective-permute-start.20) | collective-permute-done | bytes 262176 | tf_op jit(solution)/shard_map/ppermute | solution.py:610
  103.9 2.8 collective-permute-done.28.refs_13_
  106.7 11.3 %collective-permute-done.36.refs_21_ = bf16[8,32,512]{2,1,0:T(8,128)(2,1)} collective-permute-done((bf16[8,32,512]{2,1,0:T(8,128)(2,1)}, bf16[8,32,512]{2,1,0:T(8,128)(2,1)}, u32[]{:S(2)}, u32[]{:S(2)}) %collective-permute-start.36) | collective-permute-done | bytes 262176 | tf_op jit(solution)/shard_map/ppermute | solution.py:610
  118.0 1.5 collective-permute-start.5
  119.5 18.6 %collective-permute-done.7.refs_5_ = bf16[24,32,512]{2,1,0:T(8,128)(2,1)S(1)} collective-permute-done((bf16[24,32,512]{2,1,0:T(8,128)(2,1)S(1)}, bf16[24,32,512]{2,1,0:T(8,128)(2,1)S(1)}, u32[]{:S(2)}, u32[]{:S(2)}) %collective-permute-start.7) | collective-permute-done | bytes 786464 | tf_op jit(solution)/shard_map/ppermute | solution.py:610
  138.1 6.9 %collective-permute-done.5.refs_3_ = bf16[24,32,512]{2,1,0:T(8,128)(2,1)S(1)} collective-permute-done((bf16[24,32,512]{2,1,0:T(8,128)(2,1)S(1)}, bf16[24,32,512]{2,1,0:T(8,128)(2,1)S(1)}, u32[]{:S(2)}, u32[]{:S(2)}) %collective-permute-start.5) | collective-permute-done | bytes 786464 | tf_op jit(solution)/shard_map/ppermute | solution.py:610
  145.6 1.8 collective-permute-done.10.refs_8_
  147.7 0.8 collective-permute-done.11.refs_9_
  148.8 0.8 collective-permute-done.9.refs_7_
  150.0 1.3 copy-done.1
  152.0 18.0 %products.2 = (f32[4,512,512]{2,1,0:T(8,128)}, s16[528,512]{1,0:T(8,128)(2,1)}, s16[528,512]{1,0:T(8,128)(2,1)}) custom-call(s32[132]{0:T(256)} %bitcast.29, bf16[6656,3328]{1,0:T(8,128)(2,1)} %inverse.7, bf16[2048,3328]{1,0:T(8,128)(2,1)} %collective-permute-done.packed, bf16[16,128,512]{2,1,0:T(8,128)(2,1)} %bitcast.19, bf16[16,128,512]{2,1,0:T(8,128)(2,1)} %copy-done.1, ...), custom_call_target="tpu_custom_call" | custom-call | flops 10000000000 | bytes 30000000 | tf_op jit(solution)/shard_map/products/pallas_call | solution.py:315
  171.2 7.8 %diag_terms.3 = (f32[256,512]{1,0:T(8,128)}, f32[256,512]{1,0:T(8,128)}) custom-call(s32[132]{0:T(256)} %bitcast.30, f32[4,512,512]{2,1,0:T(8,128)} %get-tuple-element.14.total.first, bf16[16,128,512]{2,1,0:T(8,128)(2,1)} %bitcast.20, bf16[16,128,512]{2,1,0:T(8,128)(2,1)} %copy-done.1, bf16[24,32,512]{2,1,0:T(8,128)(2,1)} %copy-done.2, ...), custom_call_target="tpu_custom_call" | custom-call | flops 3000000000 | bytes 7000000 | tf_op jit(solution)/shard_map/diag_terms/pallas_call | solution.py:394
  180.3 17.9 %products.3 = (f32[4,512,512]{2,1,0:T(8,128)}, s16[528,512]{1,0:T(8,128)(2,1)}, s16[528,512]{1,0:T(8,128)(2,1)}) custom-call(s32[132]{0:T(256)} %bitcast.26, bf16[6656,3328]{1,0:T(8,128)(2,1)} %inverse.7, bf16[2048,3328]{1,0:T(8,128)(2,1)} %collective-permute-done.16.packed, bf16[16,128,512]{2,1,0:T(8,128)(2,1)} %bitcast.21, ...), custom_call_target="tpu_custom_call" | custom-call | flops 10000000000 | bytes 30000000 | tf_op jit(solution)/shard_map/products/pallas_call | solution.py:315
  198.3 8.0 %diag_terms.2 = (f32[256,512]{1,0:T(8,128)}, f32[256,512]{1,0:T(8,128)}) custom-call(s32[132]{0:T(256)} %bitcast.27, f32[4,512,512]{2,1,0:T(8,128)} %get-tuple-element.17.total.first, bf16[16,128,512]{2,1,0:T(8,128)(2,1)} %bitcast.22, bf16[16,128,512]{2,1,0:T(8,128)(2,1)} %copy-done.1, bf16[8,32,512]{2,1,0:T(8,128)(2,1)} %copy-done.15, ...), custom_call_target="tpu_custom_call" | custom-call | flops 3000000000 | bytes 7000000 | tf_op jit(solution)/shard_map/diag_terms/pallas_call | solution.py:394
  206.7 1.7 collective-permute-done.45
  208.4 1.1 dynamic-slice_add_fusion.3
  209.9 3.2 collective-permute-done.49
  213.1 0.7 dynamic-slice_add_fusion.4
  213.8 2.4 collective-permute-done.46
  216.2 0.7 dynamic-slice_add_fusion.6
  216.8 1.9 collective-permute-done.50.refs_3_
  218.7 3.1 collective-permute-done.47.refs_1_
  222.5 1.9 fold_pieces.1
  224.3 2.0 collective-permute-start.53
  226.4 4.9 %collective-permute-done.51.refs_0_ = s16[144,512]{1,0:T(8,128)(2,1)S(1)} collective-permute-done((s16[144,512]{1,0:T(8,128)(2,1)}, s16[144,512]{1,0:T(8,128)(2,1)S(1)}, u32[]{:S(2)}, u32[]{:S(2)}) %collective-permute-start.51) | collective-permute-done | bytes 147488 | tf_op jit(solution)/shard_map/ppermute | solution.py:632
  231.3 4.4 %collective-permute-done.52.refs_1_ = s16[144,512]{1,0:T(8,128)(2,1)S(1)} collective-permute-done((s16[144,512]{1,0:T(8,128)(2,1)}, s16[144,512]{1,0:T(8,128)(2,1)S(1)}, u32[]{:S(2)}, u32[]{:S(2)}) %collective-permute-start.52) | collective-permute-done | bytes 147488 | tf_op jit(solution)/shard_map/ppermute | solution.py:632
  236.4 2.0 line_sums.1
  238.3 6.6 %collective-permute-done.54 = f32[2,64,512]{2,1,0:T(8,128)S(1)} collective-permute-done((f32[2,64,512]{2,1,0:T(8,128)}, f32[2,64,512]{2,1,0:T(8,128)S(1)}, u32[]{:S(2)}, u32[]{:S(2)}) %collective-permute-start.54) | collective-permute-done | bytes 262176 | tf_op jit(solution)/shard_map/ppermute | solution.py:635
  244.9 1.1 maximum_select_fusion.1
  246.3 3.4 %collective-permute-start.43 = (s16[528,512]{1,0:T(8,128)(2,1)}, s16[528,512]{1,0:T(8,128)(2,1)S(1)}, u32[]{:S(2)}, u32[]{:S(2)}) collective-permute-start(s16[528,512]{1,0:T(8,128)(2,1)} %get-tuple-element.18), channel_id=1, source_target_pairs={{0,2},{1,3},{6,4},{7,5},{8,10},{9,11},{14,12},{15,13},{16,18},{17,... | collective-permute-start | bytes 1622024 | tf_op jit(solution)/shard_map/ppermute | solution.py:621
  249.8 0.7 collective-permute-start.41
  250.5 3.0 collective-permute-start.42
  253.5 2.7 collective-permute-start.14
  256.2 1.4 maximum_select_fusion.piece
  257.7 5.0 %collective-permute-done.43.far = s16[528,512]{1,0:T(8,128)(2,1)S(1)} collective-permute-done((s16[528,512]{1,0:T(8,128)(2,1)}, s16[528,512]{1,0:T(8,128)(2,1)S(1)}, u32[]{:S(2)}, u32[]{:S(2)}) %collective-permute-start.43) | collective-permute-done | bytes 540704 | tf_op jit(solution)/shard_map/ppermute | solution.py:621
  262.7 0.7 collective-permute-start.12
  263.5 2.6 join_far.3
  266.2 17.7 %collective-permute-done.14.far = s16[528,512]{1,0:T(8,128)(2,1)} collective-permute-done((s16[528,512]{1,0:T(8,128)(2,1)}, s16[528,512]{1,0:T(8,128)(2,1)}, u32[]{:S(2)}, u32[]{:S(2)}) %collective-permute-start.14) | collective-permute-done | bytes 540704 | tf_op jit(solution)/shard_map/ppermute | solution.py:621
  283.8 4.3 %collective-permute-start.44 = (s16[528,512]{1,0:T(8,128)(2,1)}, s16[528,512]{1,0:T(8,128)(2,1)}, u32[]{:S(2)}, u32[]{:S(2)}) collective-permute-start(s16[528,512]{1,0:T(8,128)(2,1)} %join_far.3), channel_id=1, source_target_pairs={{4,0},{5,1},{6,2},{7,3},{0,4},{1,5},{2,6},{3,7},{12,8},{13,9},{14,... | collective-permute-start | bytes 1622024 | tf_op jit(solution)/shard_map/ppermute | solution.py:624
  288.1 2.7 join_far.2
  290.9 1.1 collective-permute-start.15
  292.0 21.8 %collective-permute-done.44.refs_2_.refs_5_ = s16[528,512]{1,0:T(8,128)(2,1)} collective-permute-done((s16[528,512]{1,0:T(8,128)(2,1)}, s16[528,512]{1,0:T(8,128)(2,1)}, u32[]{:S(2)}, u32[]{:S(2)}) %collective-permute-start.44) | collective-permute-done | bytes 540704 | tf_op jit(solution)/shard_map/ppermute | solution.py:624
  313.8 2.7 final_sums.2.refs_6_
  316.6 17.1 %collective-permute-done.15.refs_2_.refs_5_ = s16[528,512]{1,0:T(8,128)(2,1)} collective-permute-done((s16[528,512]{1,0:T(8,128)(2,1)}, s16[528,512]{1,0:T(8,128)(2,1)}, u32[]{:S(2)}, u32[]{:S(2)}) %collective-permute-start.15) | collective-permute-done | bytes 540704 | tf_op jit(solution)/shard_map/ppermute | solution.py:624
  333.7 2.7 final_sums.3
  336.5 2.3 place_half.2.refs_0_
  338.7 2.3 place_half.3
  (175 shorter events, 10.2 us)
Async XLA Ops:
  13.9 137.6 %collective-permute-start = (bf16[2048,3328]{1,0:T(8,128)(2,1)}, bf16[2048,3328]{1,0:T(8,128)(2,1)}, u32[]{:S(2)}, u32[]{:S(2)}) collective-permute-start(bf16[2048,3328]{1,0:T(8,128)(2,1)} %pack_strips.2), channel_id=1, source_target_pairs={{1,0},{0,1},{3,2},{2,3},{5,4},{4,5},{7,6},{6,7},{9,8},{8,9},{11,10... | collective-permute-start | bytes 40894472 | tf_op jit(solution)/shard_map/ppermute | solution.py:617
  25.1 154.3 %collective-permute-start.16 = (bf16[2048,3328]{1,0:T(8,128)(2,1)}, bf16[2048,3328]{1,0:T(8,128)(2,1)}, u32[]{:S(2)}, u32[]{:S(2)}) collective-permute-start(bf16[2048,3328]{1,0:T(8,128)(2,1)} %pack_strips.3), channel_id=1, source_target_pairs={{1,0},{0,1},{3,2},{2,3},{5,4},{4,5},{7,6},{6,7},{9,8},{8,9},{11,10... | collective-permute-start | bytes 40894472 | tf_op jit(solution)/shard_map/ppermute | solution.py:617
  25.3 11.9 %collective-permute-start.2 = (bf16[8,32,512]{2,1,0:T(8,128)(2,1)S(1)}, bf16[8,32,512]{2,1,0:T(8,128)(2,1)S(1)}, u32[]{:S(2)}, u32[]{:S(2)}) collective-permute-start(bf16[8,32,512]{2,1,0:T(8,128)(2,1)S(1)} %get-tuple-element.34), channel_id=1, source_target_pairs={{2,0},{3,1},{4,2},{5,3},{6,4},{7,5},{0,6},{1,7},{10,8},{11,9},{12,... | collective-permute-start | bytes 786440 | tf_op jit(solution)/shard_map/ppermute | solution.py:598
  30.4 24.3 %collective-permute-start.3 = (bf16[8,32,512]{2,1,0:T(8,128)(2,1)S(1)}, bf16[8,32,512]{2,1,0:T(8,128)(2,1)S(1)}, u32[]{:S(2)}, u32[]{:S(2)}) collective-permute-start(bf16[8,32,512]{2,1,0:T(8,128)(2,1)S(1)} %get-tuple-element.34), channel_id=1, source_target_pairs={{4,0},{5,1},{6,2},{7,3},{0,4},{1,5},{2,6},{3,7},{12,8},{13,9},{14,... | collective-permute-start | bytes 786440 | tf_op jit(solution)/shard_map/ppermute | solution.py:598
  30.4 24.3 %collective-permute-start.4 = (bf16[8,32,512]{2,1,0:T(8,128)(2,1)S(1)}, bf16[8,32,512]{2,1,0:T(8,128)(2,1)S(1)}, u32[]{:S(2)}, u32[]{:S(2)}) collective-permute-start(bf16[8,32,512]{2,1,0:T(8,128)(2,1)S(1)} %get-tuple-element.34), channel_id=1, source_target_pairs={{6,0},{7,1},{0,2},{1,3},{2,4},{3,5},{4,6},{5,7},{14,8},{15,9},{8,1... | collective-permute-start | bytes 786440 | tf_op jit(solution)/shard_map/ppermute | solution.py:598
  37.2 28.7 %collective-permute-start.17 = (bf16[8,32,512]{2,1,0:T(8,128)(2,1)S(1)}, bf16[8,32,512]{2,1,0:T(8,128)(2,1)S(1)}, u32[]{:S(2)}, u32[]{:S(2)}) collective-permute-start(bf16[8,32,512]{2,1,0:T(8,128)(2,1)S(1)} %get-tuple-element.33), channel_id=1, source_target_pairs={{2,0},{3,1},{4,2},{5,3},{6,4},{7,5},{0,6},{1,7},{10,8},{11,9},{12,... | collective-permute-start | bytes 786440 | tf_op jit(solution)/shard_map/ppermute | solution.py:598
  54.7 20.7 %collective-permute-start.25 = (bf16[8,32,512]{2,1,0:T(8,128)(2,1)S(1)}, bf16[8,32,512]{2,1,0:T(8,128)(2,1)S(1)}, u32[]{:S(2)}, u32[]{:S(2)}) collective-permute-start(bf16[8,32,512]{2,1,0:T(8,128)(2,1)S(1)} %get-tuple-element.33), channel_id=1, source_target_pairs={{4,0},{5,1},{6,2},{7,3},{0,4},{1,5},{2,6},{3,7},{12,8},{13,9},{14,... | collective-permute-start | bytes 786440 | tf_op jit(solution)/shard_map/ppermute | solution.py:598
  54.7 20.7 %collective-permute-start.33 = (bf16[8,32,512]{2,1,0:T(8,128)(2,1)S(1)}, bf16[8,32,512]{2,1,0:T(8,128)(2,1)S(1)}, u32[]{:S(2)}, u32[]{:S(2)}) collective-permute-start(bf16[8,32,512]{2,1,0:T(8,128)(2,1)S(1)} %get-tuple-element.33), channel_id=1, source_target_pairs={{6,0},{7,1},{0,2},{1,3},{2,4},{3,5},{4,6},{5,7},{14,8},{15,9},{8,1... | collective-permute-start | bytes 786440 | tf_op jit(solution)/shard_map/ppermute | solution.py:598
  65.8 104.2 %copy-start.15 = (bf16[8,32,512]{2,1,0:T(8,128)(2,1)}, bf16[8,32,512]{2,1,0:T(8,128)(2,1)S(1)}, u32[]{:S(2)}) copy-start(bf16[8,32,512]{2,1,0:T(8,128)(2,1)S(1)} %collective-permute-done.17.refs_2_) | copy-start | bytes 786436
  65.8 11.6 %collective-permute-start.18 = (bf16[8,32,512]{2,1,0:T(8,128)(2,1)S(1)}, bf16[8,32,512]{2,1,0:T(8,128)(2,1)S(1)}, u32[]{:S(2)}, u32[]{:S(2)}) collective-permute-start(bf16[8,32,512]{2,1,0:T(8,128)(2,1)S(1)} %collective-permute-done.17.refs_2_), channel_id=1, source_target_pairs={{8,0},{17,1},{10,2},{19,3},{12,4},{21,5},{14,6},{23,7},{0,8},{25,9... | collective-permute-start | bytes 786440 | tf_op jit(solution)/shard_map/ppermute | solution.py:610
  75.4 94.6 %copy-start.16 = (bf16[8,32,512]{2,1,0:T(8,128)(2,1)}, bf16[8,32,512]{2,1,0:T(8,128)(2,1)S(1)}, u32[]{:S(2)}) copy-start(bf16[8,32,512]{2,1,0:T(8,128)(2,1)S(1)} %collective-permute-done.25.refs_10_) | copy-start | bytes 786436
  75.4 9.3 %collective-permute-start.26 = (bf16[8,32,512]{2,1,0:T(8,128)(2,1)S(1)}, bf16[8,32,512]{2,1,0:T(8,128)(2,1)}, u32[]{:S(2)}, u32[]{:S(2)}) collective-permute-start(bf16[8,32,512]{2,1,0:T(8,128)(2,1)S(1)} %collective-permute-done.25.refs_10_), channel_id=1, source_target_pairs={{8,0},{17,1},{10,2},{19,3},{12,4},{21,5},{14,6},{23,7},{0,8},{25,9... | collective-permute-start | bytes 786440 | tf_op jit(solution)/shard_map/ppermute | solution.py:610
  75.4 76.1 %copy-start.17 = (bf16[8,32,512]{2,1,0:T(8,128)(2,1)}, bf16[8,32,512]{2,1,0:T(8,128)(2,1)S(1)}, u32[]{:S(2)}) copy-start(bf16[8,32,512]{2,1,0:T(8,128)(2,1)S(1)} %collective-permute-done.33.refs_18_) | copy-start | bytes 786436
  75.4 14.9 %collective-permute-start.34 = (bf16[8,32,512]{2,1,0:T(8,128)(2,1)S(1)}, bf16[8,32,512]{2,1,0:T(8,128)(2,1)}, u32[]{:S(2)}, u32[]{:S(2)}) collective-permute-start(bf16[8,32,512]{2,1,0:T(8,128)(2,1)S(1)} %collective-permute-done.33.refs_18_), channel_id=1, source_target_pairs={{8,0},{17,1},{10,2},{19,3},{12,4},{21,5},{14,6},{23,7},{0,8},{25,9... | collective-permute-start | bytes 786440 | tf_op jit(solution)/shard_map/ppermute | solution.py:610
  77.4 74.1 %copy-start.18 = (bf16[8,32,512]{2,1,0:T(8,128)(2,1)}, bf16[8,32,512]{2,1,0:T(8,128)(2,1)S(1)}, u32[]{:S(2)}) copy-start(bf16[8,32,512]{2,1,0:T(8,128)(2,1)S(1)} %collective-permute-done.18.refs_3_) | copy-start | bytes 786436
  77.4 12.9 %collective-permute-start.19 = (bf16[8,32,512]{2,1,0:T(8,128)(2,1)S(1)}, bf16[8,32,512]{2,1,0:T(8,128)(2,1)}, u32[]{:S(2)}, u32[]{:S(2)}) collective-permute-start(bf16[8,32,512]{2,1,0:T(8,128)(2,1)S(1)} %collective-permute-done.17.refs_2_), channel_id=1, source_target_pairs={{16,0},{9,1},{18,2},{11,3},{20,4},{13,5},{22,6},{15,7},{24,8},{1,9... | collective-permute-start | bytes 786440 | tf_op jit(solution)/shard_map/ppermute | solution.py:610
  84.7 6.5 %collective-permute-start.27 = (bf16[8,32,512]{2,1,0:T(8,128)(2,1)S(1)}, bf16[8,32,512]{2,1,0:T(8,128)(2,1)}, u32[]{:S(2)}, u32[]{:S(2)}) collective-permute-start(bf16[8,32,512]{2,1,0:T(8,128)(2,1)S(1)} %collective-permute-done.25.refs_10_), channel_id=1, source_target_pairs={{16,0},{9,1},{18,2},{11,3},{20,4},{13,5},{22,6},{15,7},{24,8},{1,9... | collective-permute-start | bytes 786440 | tf_op jit(solution)/shard_map/ppermute | solution.py:610
  90.3 6.4 %collective-permute-start.35 = (bf16[8,32,512]{2,1,0:T(8,128)(2,1)S(1)}, bf16[8,32,512]{2,1,0:T(8,128)(2,1)S(1)}, u32[]{:S(2)}, u32[]{:S(2)}) collective-permute-start(bf16[8,32,512]{2,1,0:T(8,128)(2,1)S(1)} %collective-permute-done.33.refs_18_), channel_id=1, source_target_pairs={{16,0},{9,1},{18,2},{11,3},{20,4},{13,5},{22,6},{15,7},{24,8},{1,9... | collective-permute-start | bytes 786440 | tf_op jit(solution)/shard_map/ppermute | solution.py:610
  90.3 7.1 %collective-permute-start.21 = (bf16[8,32,512]{2,1,0:T(8,128)(2,1)S(1)}, bf16[8,32,512]{2,1,0:T(8,128)(2,1)S(1)}, u32[]{:S(2)}, u32[]{:S(2)}) collective-permute-start(bf16[8,32,512]{2,1,0:T(8,128)(2,1)S(1)} %collective-permute-done.17.refs_2_), channel_id=1, source_target_pairs={{1,0},{0,1},{3,2},{2,3},{5,4},{4,5},{7,6},{6,7},{9,8},{8,9},{11,10... | collective-permute-start | bytes 786440 | tf_op jit(solution)/shard_map/ppermute | solution.py:611
  91.2 6.4 %collective-permute-start.29 = (bf16[8,32,512]{2,1,0:T(8,128)(2,1)S(1)}, bf16[8,32,512]{2,1,0:T(8,128)(2,1)S(1)}, u32[]{:S(2)}, u32[]{:S(2)}) collective-permute-start(bf16[8,32,512]{2,1,0:T(8,128)(2,1)S(1)} %collective-permute-done.25.refs_10_), channel_id=1, source_target_pairs={{1,0},{0,1},{3,2},{2,3},{5,4},{4,5},{7,6},{6,7},{9,8},{8,9},{11,10... | collective-permute-start | bytes 786440 | tf_op jit(solution)/shard_map/ppermute | solution.py:611
  97.4 2.2 collective-permute-start.37
  97.4 54.1 %copy-start.20 = (bf16[8,32,512]{2,1,0:T(8,128)(2,1)}, bf16[8,32,512]{2,1,0:T(8,128)(2,1)S(1)}, u32[]{:S(2)}) copy-start(bf16[8,32,512]{2,1,0:T(8,128)(2,1)S(1)} %collective-permute-done.21.refs_6_) | copy-start | bytes 786436
  97.4 6.4 %collective-permute-start.20 = (bf16[8,32,512]{2,1,0:T(8,128)(2,1)S(1)}, bf16[8,32,512]{2,1,0:T(8,128)(2,1)S(1)}, u32[]{:S(2)}, u32[]{:S(2)}) collective-permute-start(bf16[8,32,512]{2,1,0:T(8,128)(2,1)S(1)} %collective-permute-done.18.refs_3_), channel_id=1, source_target_pairs={{16,0},{9,1},{18,2},{11,3},{20,4},{13,5},{22,6},{15,7},{24,8},{1,9... | collective-permute-start | bytes 786440 | tf_op jit(solution)/shard_map/ppermute | solution.py:610
  97.5 54.0 %copy-start.21 = (bf16[8,32,512]{2,1,0:T(8,128)(2,1)}, bf16[8,32,512]{2,1,0:T(8,128)(2,1)S(1)}, u32[]{:S(2)}) copy-start(bf16[8,32,512]{2,1,0:T(8,128)(2,1)S(1)} %collective-permute-done.29.refs_14_) | copy-start | bytes 786436
  97.5 9.1 %collective-permute-start.28 = (bf16[8,32,512]{2,1,0:T(8,128)(2,1)}, bf16[8,32,512]{2,1,0:T(8,128)(2,1)S(1)}, u32[]{:S(2)}, u32[]{:S(2)}) collective-permute-start(bf16[8,32,512]{2,1,0:T(8,128)(2,1)} %collective-permute-done.26.refs_11_), channel_id=1, source_target_pairs={{16,0},{9,1},{18,2},{11,3},{20,4},{13,5},{22,6},{15,7},{24,8},{1,9... | collective-permute-start | bytes 786440 | tf_op jit(solution)/shard_map/ppermute | solution.py:610
  99.6 52.4 %copy-start.2 = (bf16[24,32,512]{2,1,0:T(8,128)(2,1)}, bf16[24,32,512]{2,1,0:T(8,128)(2,1)S(1)}, u32[]{:S(2)}) copy-start(bf16[24,32,512]{2,1,0:T(8,128)(2,1)S(1)} %constant_dynamic-update-slice_fusion.refs_2_) | copy-start | bytes 2359300
  99.6 19.9 %collective-permute-start.6 = (bf16[24,32,512]{2,1,0:T(8,128)(2,1)S(1)}, bf16[24,32,512]{2,1,0:T(8,128)(2,1)S(1)}, u32[]{:S(2)}, u32[]{:S(2)}) collective-permute-start(bf16[24,32,512]{2,1,0:T(8,128)(2,1)S(1)} %constant_dynamic-update-slice_fusion.refs_2_), channel_id=1, source_target_pairs={{16,0},{9,1},{18,2},{11,3},{20,4},{13,5},{22,6},{15,7},{24,8},{1,9... | collective-permute-start | bytes 2359304 | tf_op jit(solution)/shard_map/ppermute | solution.py:610
  103.9 14.1 %collective-permute-start.36 = (bf16[8,32,512]{2,1,0:T(8,128)(2,1)}, bf16[8,32,512]{2,1,0:T(8,128)(2,1)}, u32[]{:S(2)}, u32[]{:S(2)}) collective-permute-start(bf16[8,32,512]{2,1,0:T(8,128)(2,1)} %collective-permute-done.34.refs_19_), channel_id=1, source_target_pairs={{16,0},{9,1},{18,2},{11,3},{20,4},{13,5},{22,6},{15,7},{24,8},{1,9... | collective-permute-start | bytes 786440 | tf_op jit(solution)/shard_map/ppermute | solution.py:610
  106.7 11.3 %collective-permute-start.22 = (bf16[8,32,512]{2,1,0:T(8,128)(2,1)S(1)}, bf16[8,32,512]{2,1,0:T(8,128)(2,1)}, u32[]{:S(2)}, u32[]{:S(2)}) collective-permute-start(bf16[8,32,512]{2,1,0:T(8,128)(2,1)S(1)} %collective-permute-done.18.refs_3_), channel_id=1, source_target_pairs={{1,0},{0,1},{3,2},{2,3},{5,4},{4,5},{7,6},{6,7},{9,8},{8,9},{11,10... | collective-permute-start | bytes 786440 | tf_op jit(solution)/shard_map/ppermute | solution.py:611
  118.0 20.1 %collective-permute-start.7 = (bf16[24,32,512]{2,1,0:T(8,128)(2,1)S(1)}, bf16[24,32,512]{2,1,0:T(8,128)(2,1)S(1)}, u32[]{:S(2)}, u32[]{:S(2)}) collective-permute-start(bf16[24,32,512]{2,1,0:T(8,128)(2,1)S(1)} %constant_dynamic-update-slice_fusion.refs_2_), channel_id=1, source_target_pairs={{24,0},{25,1},{26,2},{27,3},{28,4},{29,5},{30,6},{31,7},{16,8},{17... | collective-permute-start | bytes 2359304 | tf_op jit(solution)/shard_map/ppermute | solution.py:610
  118.0 27.0 %collective-permute-start.5 = (bf16[24,32,512]{2,1,0:T(8,128)(2,1)S(1)}, bf16[24,32,512]{2,1,0:T(8,128)(2,1)S(1)}, u32[]{:S(2)}, u32[]{:S(2)}) collective-permute-start(bf16[24,32,512]{2,1,0:T(8,128)(2,1)S(1)} %constant_dynamic-update-slice_fusion.refs_2_), channel_id=1, source_target_pairs={{8,0},{17,1},{10,2},{19,3},{12,4},{21,5},{14,6},{23,7},{0,8},{25,9... | collective-permute-start | bytes 2359304 | tf_op jit(solution)/shard_map/ppermute | solution.py:610
  119.5 30.5 %collective-permute-start.1 = (bf16[16,128,512]{2,1,0:T(8,128)(2,1)S(1)}, bf16[16,128,512]{2,1,0:T(8,128)(2,1)S(1)}, u32[]{:S(2)}, u32[]{:S(2)}) collective-permute-start(bf16[16,128,512]{2,1,0:T(8,128)(2,1)S(1)} %bitcast.24), channel_id=1, source_target_pairs={{1,0},{0,1},{3,2},{2,3},{5,4},{4,5},{7,6},{6,7},{9,8},{8,9},{11,10... | collective-permute-start | bytes 6291464 | tf_op jit(solution)/shard_map/ppermute | solution.py:593
  138.1 7.3 %collective-permute-start.8 = (bf16[24,32,512]{2,1,0:T(8,128)(2,1)S(1)}, bf16[24,32,512]{2,1,0:T(8,128)(2,1)S(1)}, u32[]{:S(2)}, u32[]{:S(2)}) collective-permute-start(bf16[24,32,512]{2,1,0:T(8,128)(2,1)S(1)} %constant_dynamic-update-slice_fusion.refs_2_), channel_id=1, source_target_pairs={{1,0},{0,1},{3,2},{2,3},{5,4},{4,5},{7,6},{6,7},{9,8},{8,9},{11,10... | collective-permute-start | bytes 2359304 | tf_op jit(solution)/shard_map/ppermute | solution.py:611
  145.0 2.3 collective-permute-start.10
  145.4 3.1 collective-permute-start.11
  147.3 2.3 collective-permute-start.9
  148.5 21.6 %collective-permute-start.30 = (bf16[8,32,512]{2,1,0:T(8,128)(2,1)}, bf16[8,32,512]{2,1,0:T(8,128)(2,1)}, u32[]{:S(2)}, u32[]{:S(2)}) collective-permute-start(bf16[8,32,512]{2,1,0:T(8,128)(2,1)} %collective-permute-done.26.refs_11_), channel_id=1, source_target_pairs={{1,0},{0,1},{3,2},{2,3},{5,4},{4,5},{7,6},{6,7},{9,8},{8,9},{11,10... | collective-permute-start | bytes 786440 | tf_op jit(solution)/shard_map/ppermute | solution.py:611
  149.6 20.7 %collective-permute-start.38 = (bf16[8,32,512]{2,1,0:T(8,128)(2,1)}, bf16[8,32,512]{2,1,0:T(8,128)(2,1)}, u32[]{:S(2)}, u32[]{:S(2)}) collective-permute-start(bf16[8,32,512]{2,1,0:T(8,128)(2,1)} %collective-permute-done.34.refs_19_), channel_id=1, source_target_pairs={{1,0},{0,1},{3,2},{2,3},{5,4},{4,5},{7,6},{6,7},{9,8},{8,9},{11,10... | collective-permute-start | bytes 786440 | tf_op jit(solution)/shard_map/ppermute | solution.py:611
  151.3 19.4 %collective-permute-start.23 = (bf16[8,32,512]{2,1,0:T(8,128)(2,1)}, bf16[8,32,512]{2,1,0:T(8,128)(2,1)S(1)}, u32[]{:S(2)}, u32[]{:S(2)}) collective-permute-start(bf16[8,32,512]{2,1,0:T(8,128)(2,1)} %collective-permute-done.19.refs_4_), channel_id=1, source_target_pairs={{1,0},{0,1},{3,2},{2,3},{5,4},{4,5},{7,6},{6,7},{9,8},{8,9},{11,10... | collective-permute-start | bytes 786440 | tf_op jit(solution)/shard_map/ppermute | solution.py:611
  151.7 19.3 %collective-permute-start.31 = (bf16[8,32,512]{2,1,0:T(8,128)(2,1)}, bf16[8,32,512]{2,1,0:T(8,128)(2,1)S(1)}, u32[]{:S(2)}, u32[]{:S(2)}) collective-permute-start(bf16[8,32,512]{2,1,0:T(8,128)(2,1)} %collective-permute-done.27.refs_12_), channel_id=1, source_target_pairs={{1,0},{0,1},{3,2},{2,3},{5,4},{4,5},{7,6},{6,7},{9,8},{8,9},{11,10... | collective-permute-start | bytes 786440 | tf_op jit(solution)/shard_map/ppermute | solution.py:611
  170.1 9.0 %collective-permute-start.39 = (bf16[8,32,512]{2,1,0:T(8,128)(2,1)}, bf16[8,32,512]{2,1,0:T(8,128)(2,1)S(1)}, u32[]{:S(2)}, u32[]{:S(2)}) collective-permute-start(bf16[8,32,512]{2,1,0:T(8,128)(2,1)} %copy-done.19), channel_id=1, source_target_pairs={{1,0},{0,1},{3,2},{2,3},{5,4},{4,5},{7,6},{6,7},{9,8},{8,9},{11,10... | collective-permute-start | bytes 786440 | tf_op jit(solution)/shard_map/ppermute | solution.py:611
  170.4 9.0 %collective-permute-start.24 = (bf16[8,32,512]{2,1,0:T(8,128)(2,1)S(1)}, bf16[8,32,512]{2,1,0:T(8,128)(2,1)S(1)}, u32[]{:S(2)}, u32[]{:S(2)}) collective-permute-start(bf16[8,32,512]{2,1,0:T(8,128)(2,1)S(1)} %copy-done.24), channel_id=1, source_target_pairs={{1,0},{0,1},{3,2},{2,3},{5,4},{4,5},{7,6},{6,7},{9,8},{8,9},{11,10... | collective-permute-start | bytes 786440 | tf_op jit(solution)/shard_map/ppermute | solution.py:611
  170.7 8.7 %collective-permute-start.32 = (bf16[8,32,512]{2,1,0:T(8,128)(2,1)S(1)}, bf16[8,32,512]{2,1,0:T(8,128)(2,1)S(1)}, u32[]{:S(2)}, u32[]{:S(2)}) collective-permute-start(bf16[8,32,512]{2,1,0:T(8,128)(2,1)S(1)} %copy-done.26), channel_id=1, source_target_pairs={{1,0},{0,1},{3,2},{2,3},{5,4},{4,5},{7,6},{6,7},{9,8},{8,9},{11,10... | collective-permute-start | bytes 786440 | tf_op jit(solution)/shard_map/ppermute | solution.py:611
  170.9 8.5 %collective-permute-start.40 = (bf16[8,32,512]{2,1,0:T(8,128)(2,1)}, bf16[8,32,512]{2,1,0:T(8,128)(2,1)S(1)}, u32[]{:S(2)}, u32[]{:S(2)}) collective-permute-start(bf16[8,32,512]{2,1,0:T(8,128)(2,1)} %collective-permute-done.36.refs_21_), channel_id=1, source_target_pairs={{1,0},{0,1},{3,2},{2,3},{5,4},{4,5},{7,6},{6,7},{9,8},{8,9},{11,10... | collective-permute-start | bytes 786440 | tf_op jit(solution)/shard_map/ppermute | solution.py:611
  179.1 27.4 %collective-permute-start.48 = (f32[256,512]{1,0:T(8,128)}, f32[256,512]{1,0:T(8,128)S(1)}, u32[]{:S(2)}, u32[]{:S(2)}) collective-permute-start(f32[256,512]{1,0:T(8,128)} %get-tuple-element.23), channel_id=1, source_target_pairs={{1,0},{0,1},{3,2},{2,3},{5,4},{4,5},{7,6},{6,7},{9,8},{8,9},{11,10... | collective-permute-start | bytes 1572872 | tf_op jit(solution)/shard_map/ppermute | solution.py:478
  206.2 2.2 collective-permute-start.45
  206.6 6.4 %collective-permute-start.49 = (f32[128,512]{1,0:T(8,128)S(1)}, f32[128,512]{1,0:T(8,128)S(1)}, u32[]{:S(2)}, u32[]{:S(2)}) collective-permute-start(f32[128,512]{1,0:T(8,128)S(1)} %get-tuple-element.36), channel_id=1, source_target_pairs={{8,0},{17,1},{10,2},{19,3},{12,4},{21,5},{14,6},{23,7},{0,8},{25,9... | collective-permute-start | bytes 786440 | tf_op jit(solution)/shard_map/ppermute | solution.py:483
  209.5 6.6 %collective-permute-start.46 = (f32[128,512]{1,0:T(8,128)S(1)}, f32[128,512]{1,0:T(8,128)S(1)}, u32[]{:S(2)}, u32[]{:S(2)}) collective-permute-start(f32[128,512]{1,0:T(8,128)S(1)} %get-tuple-element.38), channel_id=1, source_target_pairs={{8,0},{17,1},{10,2},{19,3},{12,4},{21,5},{14,6},{23,7},{0,8},{25,9... | collective-permute-start | bytes 786440 | tf_op jit(solution)/shard_map/ppermute | solution.py:483
  213.8 5.0 %collective-permute-start.50 = (f32[64,512]{1,0:T(8,128)S(1)}, f32[64,512]{1,0:T(8,128)S(1)}, u32[]{:S(2)}, u32[]{:S(2)}) collective-permute-start(f32[64,512]{1,0:T(8,128)S(1)} %get-tuple-element.39), channel_id=1, source_target_pairs={{16,0},{9,1},{18,2},{11,3},{20,4},{13,5},{22,6},{15,7},{24,8},{1,9... | collective-permute-start | bytes 393224 | tf_op jit(solution)/shard_map/ppermute | solution.py:483
  216.8 5.0 %collective-permute-start.47 = (f32[64,512]{1,0:T(8,128)S(1)}, f32[64,512]{1,0:T(8,128)S(1)}, u32[]{:S(2)}, u32[]{:S(2)}) collective-permute-start(f32[64,512]{1,0:T(8,128)S(1)} %get-tuple-element.41), channel_id=1, source_target_pairs={{16,0},{9,1},{18,2},{11,3},{20,4},{13,5},{22,6},{15,7},{24,8},{1,9... | collective-permute-start | bytes 393224 | tf_op jit(solution)/shard_map/ppermute | solution.py:483
  224.3 6.9 %collective-permute-start.51 = (s16[144,512]{1,0:T(8,128)(2,1)}, s16[144,512]{1,0:T(8,128)(2,1)S(1)}, u32[]{:S(2)}, u32[]{:S(2)}) collective-permute-start(s16[144,512]{1,0:T(8,128)(2,1)} %get-tuple-element.25), channel_id=1, source_target_pairs={{2,0},{3,1},{4,2},{5,3},{6,4},{7,5},{0,6},{1,7},{10,8},{11,9},{12,... | collective-permute-start | bytes 442376 | tf_op jit(solution)/shard_map/ppermute | solution.py:632
  224.3 11.3 %collective-permute-start.52 = (s16[144,512]{1,0:T(8,128)(2,1)}, s16[144,512]{1,0:T(8,128)(2,1)S(1)}, u32[]{:S(2)}, u32[]{:S(2)}) collective-permute-start(s16[144,512]{1,0:T(8,128)(2,1)} %get-tuple-element.25), channel_id=1, source_target_pairs={{4,0},{5,1},{6,2},{7,3},{0,4},{1,5},{2,6},{3,7},{12,8},{13,9},{14,... | collective-permute-start | bytes 442376 | tf_op jit(solution)/shard_map/ppermute | solution.py:632
  224.3 11.3 %collective-permute-start.53 = (s16[144,512]{1,0:T(8,128)(2,1)}, s16[144,512]{1,0:T(8,128)(2,1)S(1)}, u32[]{:S(2)}, u32[]{:S(2)}) collective-permute-start(s16[144,512]{1,0:T(8,128)(2,1)} %get-tuple-element.25), channel_id=1, source_target_pairs={{6,0},{7,1},{0,2},{1,3},{2,4},{3,5},{4,6},{5,7},{14,8},{15,9},{8,1... | collective-permute-start | bytes 442376 | tf_op jit(solution)/shard_map/ppermute | solution.py:632
  238.3 6.6 %collective-permute-start.54 = (f32[2,64,512]{2,1,0:T(8,128)}, f32[2,64,512]{2,1,0:T(8,128)S(1)}, u32[]{:S(2)}, u32[]{:S(2)}) collective-permute-start(f32[2,64,512]{2,1,0:T(8,128)} %line_sums.1), channel_id=1, source_target_pairs={{16,0},{9,1},{18,2},{11,3},{20,4},{13,5},{22,6},{15,7},{24,8},{1,9... | collective-permute-start | bytes 786440 | tf_op jit(solution)/shard_map/ppermute | solution.py:635
  246.0 10.2 %collective-permute-start.55 = (f32[2,128,512]{2,1,0:T(8,128)S(1)}, f32[2,128,512]{2,1,0:T(8,128)}, u32[]{:S(2)}, u32[]{:S(2)}) collective-permute-start(f32[2,128,512]{2,1,0:T(8,128)S(1)} %maximum_select_fusion.1), channel_id=1, source_target_pairs={{8,0},{17,1},{10,2},{19,3},{12,4},{21,5},{14,6},{23,7},{0,8},{25,9... | collective-permute-start | bytes 1572872 | tf_op jit(solution)/shard_map/ppermute | solution.py:635
  246.3 16.4 %collective-permute-start.43 = (s16[528,512]{1,0:T(8,128)(2,1)}, s16[528,512]{1,0:T(8,128)(2,1)S(1)}, u32[]{:S(2)}, u32[]{:S(2)}) collective-permute-start(s16[528,512]{1,0:T(8,128)(2,1)} %get-tuple-element.18), channel_id=1, source_target_pairs={{0,2},{1,3},{6,4},{7,5},{8,10},{9,11},{14,12},{15,13},{16,18},{17,... | collective-permute-start | bytes 1622024 | tf_op jit(solution)/shard_map/ppermute | solution.py:621
  249.8 41.0 %collective-permute-start.41 = (s16[528,512]{1,0:T(8,128)(2,1)}, s16[528,512]{1,0:T(8,128)(2,1)S(1)}, u32[]{:S(2)}, u32[]{:S(2)}) collective-permute-start(s16[528,512]{1,0:T(8,128)(2,1)} %get-tuple-element.18), channel_id=1, source_target_pairs={{2,4},{3,5},{4,2},{5,3},{10,12},{11,13},{12,10},{13,11},{18,20},{1... | collective-permute-start | bytes 1622024 | tf_op jit(solution)/shard_map/ppermute | solution.py:622
  250.5 40.4 %collective-permute-start.42 = (s16[528,512]{1,0:T(8,128)(2,1)}, s16[528,512]{1,0:T(8,128)(2,1)S(1)}, u32[]{:S(2)}, u32[]{:S(2)}) collective-permute-start(s16[528,512]{1,0:T(8,128)(2,1)} %get-tuple-element.19), channel_id=1, source_target_pairs={{2,0},{3,1},{0,2},{1,3},{6,4},{7,5},{4,6},{5,7},{10,8},{11,9},{8,1... | collective-permute-start | bytes 1622024 | tf_op jit(solution)/shard_map/ppermute | solution.py:622
  253.5 30.3 %collective-permute-start.14 = (s16[528,512]{1,0:T(8,128)(2,1)}, s16[528,512]{1,0:T(8,128)(2,1)}, u32[]{:S(2)}, u32[]{:S(2)}) collective-permute-start(s16[528,512]{1,0:T(8,128)(2,1)} %get-tuple-element.15), channel_id=1, source_target_pairs={{0,2},{1,3},{6,4},{7,5},{8,10},{9,11},{14,12},{15,13},{16,18},{17,... | collective-permute-start | bytes 1622024 | tf_op jit(solution)/shard_map/ppermute | solution.py:621
  257.6 81.2 %collective-permute-start.56 = (f32[2,256,512]{2,1,0:T(8,128)S(1)}, f32[2,256,512]{2,1,0:T(8,128)}, u32[]{:S(2)}, u32[]{:S(2)}) collective-permute-start(f32[2,256,512]{2,1,0:T(8,128)S(1)} %maximum_select_fusion.piece), channel_id=1, source_target_pairs={{1,0},{0,1},{3,2},{2,3},{5,4},{4,5},{7,6},{6,7},{9,8},{8,9},{11,10... | collective-permute-start | bytes 3145736 | tf_op jit(solution)/shard_map/ppermute | solution.py:640
  262.7 53.8 %collective-permute-start.12 = (s16[528,512]{1,0:T(8,128)(2,1)}, s16[528,512]{1,0:T(8,128)(2,1)S(1)}, u32[]{:S(2)}, u32[]{:S(2)}) collective-permute-start(s16[528,512]{1,0:T(8,128)(2,1)} %get-tuple-element.15), channel_id=1, source_target_pairs={{2,4},{3,5},{4,2},{5,3},{10,12},{11,13},{12,10},{13,11},{18,20},{1... | collective-permute-start | bytes 1622024 | tf_op jit(solution)/shard_map/ppermute | solution.py:622
  283.8 30.0 %collective-permute-start.44 = (s16[528,512]{1,0:T(8,128)(2,1)}, s16[528,512]{1,0:T(8,128)(2,1)}, u32[]{:S(2)}, u32[]{:S(2)}) collective-permute-start(s16[528,512]{1,0:T(8,128)(2,1)} %join_far.3), channel_id=1, source_target_pairs={{4,0},{5,1},{6,2},{7,3},{0,4},{1,5},{2,6},{3,7},{12,8},{13,9},{14,... | collective-permute-start | bytes 1622024 | tf_op jit(solution)/shard_map/ppermute | solution.py:624
  290.8 25.8 %collective-permute-start.13 = (s16[528,512]{1,0:T(8,128)(2,1)}, s16[528,512]{1,0:T(8,128)(2,1)S(1)}, u32[]{:S(2)}, u32[]{:S(2)}) collective-permute-start(s16[528,512]{1,0:T(8,128)(2,1)} %get-tuple-element.16), channel_id=1, source_target_pairs={{2,0},{3,1},{0,2},{1,3},{6,4},{7,5},{4,6},{5,7},{10,8},{11,9},{8,1... | collective-permute-start | bytes 1622024 | tf_op jit(solution)/shard_map/ppermute | solution.py:622
  290.9 42.8 %collective-permute-start.15 = (s16[528,512]{1,0:T(8,128)(2,1)}, s16[528,512]{1,0:T(8,128)(2,1)}, u32[]{:S(2)}, u32[]{:S(2)}) collective-permute-start(s16[528,512]{1,0:T(8,128)(2,1)} %join_far.2), channel_id=1, source_target_pairs={{4,0},{5,1},{6,2},{7,3},{0,4},{1,5},{2,6},{3,7},{12,8},{13,9},{14,... | collective-permute-start | bytes 1622024 | tf_op jit(solution)/shard_map/ppermute | solution.py:624
  (33 other events, 414.0 us)
